TPU v7x, 128 devices: a whole 4x4x4 slice. The times are simulated.
128 devices in a mesh: grp: 4 (over x), seq: 32 (over y, z, core).
Axes of the slice: x: 4, y: 4, z: 4, core: 2. Of those that a mesh axis runs over, the one named last changes fastest.
Arguments:
- grad_output: bfloat16 [4096, 8192], P('seq', 'grp'), may hold values from -6 to 6
- hidden: bfloat16 [4096, 28672], P('seq', 'grp'), may hold values from -6 to 6
- down_weight: bfloat16 [28672, 8192], P('seq', 'grp'), may hold values from -0.0625 to 0.0625
- adapter_down: bfloat16 [64, 64, 28672], P(None, None, ('grp', 'seq')), may hold values from -0.03125 to 0.03125
- adapter_up: bfloat16 [64, 64, 8192], P(None, None, ('grp', 'seq')), may hold values from -0.0625 to 0.0625
- job_tenant: int32 [32, 4], replicated, may hold values from 0 to 63, all different within a row
- job_count: int32 [32, 4], replicated, may hold values from 1 to 64, 128 in all within a row
Outputs:
- grad_hidden: bfloat16 [4096, 28672], P('seq', 'grp')
- grad_adapter_down: float32 [64, 64, 28672], P(None, None, ('grp', 'seq'))
- grad_adapter_up: float32 [64, 64, 8192], P(None, None, ('grp', 'seq'))
Inputs may be any that keep to these rules, and one draw needn't show every extreme that they name: `job_tenant`: each row names 4 different tenants; every tenant is named by some row. `job_count`: each row sums to 128, and its largest entry is exactly 64.
All inputs are finite; a program needn't handle non-finite values.
Results may differ from a plain program's by a relative error of at most 0.015.
Values may be sent and summed in bfloat16 or wider, within the bound.
A program may use at most 128 MiB of HBM per device.

v0:
```python
import jax
import jax.numpy as jnp
from jax import lax
from jax.sharding import PartitionSpec as P

ADAPTER_SCALE = 2.0


def shards(grad_output, hidden, down_weight, adapter_down, adapter_up, job_tenant, job_count):
    shard_index = lax.axis_index(SEQ)
    shard_count = lax.axis_size(SEQ)
    group_count = lax.axis_size("grp")
    tok_rows = grad_output.shape[0]
    job_slots = job_tenant.shape[1]
    ranks = adapter_down.shape[1]
    down_slab = adapter_down.shape[2]
    up_slab = adapter_up.shape[2]
    tenant_total = adapter_down.shape[0]
    contract_last = (((1,), (1,)), ((), ()))
    contract_rows = (((0,), (0,)), ((), ()))
    tenant_table = (
        job_tenant[:, :, None] == lax.broadcasted_iota(jnp.int32, (1, 1, tenant_total), 2)
    ).astype(jnp.float32)
    totals = jnp.sum(job_count.astype(jnp.float32)[:, :, None] * tenant_table, axis=(0, 1))
    weights = ADAPTER_SCALE / totals
    table_here = lax.dynamic_index_in_dim(tenant_table, shard_index, 0, keepdims=False)
    job_weights = jnp.sum(table_here * weights[None, :], axis=1)
    counts_here = lax.dynamic_index_in_dim(job_count, shard_index, 0, keepdims=False)
    run_ends = jnp.cumsum(counts_here)
    run_starts = run_ends - counts_here
    positions = lax.broadcasted_iota(jnp.int32, (tok_rows, job_slots), 0)
    member = ((positions >= run_starts[None, :]) & (positions < run_ends[None, :])).astype(
        jnp.float32
    )
    hidden_cols = lax.all_to_all(
        hidden.reshape(tok_rows, shard_count, down_slab), SEQ, split_axis=1, concat_axis=0, tiled=True
    ).reshape(shard_count, tok_rows, down_slab)
    output_cols = lax.all_to_all(
        grad_output.reshape(tok_rows, shard_count, up_slab), SEQ, split_axis=1, concat_axis=0, tiled=True
    ).reshape(shard_count, tok_rows, up_slab)
    chosen = job_tenant.T
    fetched_down, fetched_up = (
        lax.all_to_all(adapter_down[chosen], SEQ, split_axis=1, concat_axis=3, tiled=True),
        lax.all_to_all(adapter_up[chosen], SEQ, split_axis=1, concat_axis=3, tiled=True),
    )
    down_stack = fetched_down.reshape(job_slots * ranks, shard_count * down_slab)
    up_stack = fetched_up.reshape(job_slots * ranks, shard_count * up_slab)

    def select_jobs(projected):
        return jnp.sum(projected.reshape(tok_rows, job_slots, ranks) * member[:, :, None], axis=1)

    grad_proj = lax.dot_general(
        grad_output, up_stack, contract_last, preferred_element_type=jnp.float32
    )
    act_proj = lax.dot_general(
        hidden, down_stack, contract_last, preferred_element_type=jnp.float32
    )
    rank_part = jnp.concatenate([select_jobs(grad_proj), select_jobs(act_proj)], axis=1).astype(
        jnp.bfloat16
    )
    weight_pair = lax.all_gather(down_weight, "core", axis=0, tiled=True)
    tokens_same_core = lax.all_gather(grad_output, "chip", axis=0, tiled=True)
    tokens_same_core, weight_pair, rank_part = lax.optimization_barrier(
        (tokens_same_core, weight_pair, rank_part)
    )
    partial_value = lax.dot_general(
        tokens_same_core, weight_pair, contract_last, preferred_element_type=jnp.float32
    )
    quarter = lax.psum_scatter(
        partial_value.astype(jnp.bfloat16), "grp", scatter_dimension=0, tiled=True
    )
    quarter = quarter.reshape(group_count, tok_rows, quarter.shape[1])
    chip_count = lax.axis_size("chip")
    row_of_chip = chip_count // group_count
    chip = lax.axis_index("chip")
    group = lax.axis_index("grp")
    core = lax.axis_index("core")
    lane = chip % row_of_chip
    arrived = []
    for step in range(group_count):
        piece = lax.dynamic_index_in_dim(quarter, (lane + step) % group_count, 0, keepdims=False)
        pairs = []
        for g in range(group_count):
            for c in range(chip_count):
                for k in range(2):
                    z = c % row_of_chip
                    dest_chip = g * row_of_chip + (z + step) % group_count
                    dest_group = c // row_of_chip
                    pairs.append(((g * chip_count + c) * 2 + k, (dest_group * chip_count + dest_chip) * 2 + k))
        arrived.append(lax.ppermute(piece, ("grp", "chip", "core"), pairs))
    arrived = jnp.stack(arrived)
    order = (lane - jnp.arange(group_count)) % group_count
    base_grad = jnp.take(arrived, order, axis=0).transpose(1, 0, 2).reshape(tok_rows, -1)
    rank_sum = lax.psum(rank_part.astype(jnp.float32), "grp")
    grad_rank = rank_sum[:, :ranks].astype(jnp.bfloat16)
    act_rank = rank_sum[:, ranks:].astype(jnp.bfloat16)
    grad_spread = (
        (member[:, :, None] * lax.optimization_barrier(grad_rank).astype(jnp.float32)[:, None, :])
        .reshape(tok_rows, job_slots * ranks)
        .astype(jnp.bfloat16)
    )
    adapter_term = (
        jnp.dot(grad_spread, down_stack, preferred_element_type=jnp.float32) * ADAPTER_SCALE
    )
    grad_hidden = (base_grad.astype(jnp.float32) + adapter_term).astype(jnp.bfloat16)

    all_positions = lax.broadcasted_iota(jnp.int32, (shard_count, tok_rows, job_slots), 1)
    all_ends = jnp.cumsum(job_count, axis=1)
    all_starts = all_ends - job_count
    member_all = (
        (all_positions >= all_starts[:, None, :]) & (all_positions < all_ends[:, None, :])
    ).astype(jnp.float32)
    weight_all = jnp.sum(tenant_table * weights[None, None, :], axis=2)
    rank_all = lax.all_gather(
        jnp.concatenate([grad_rank, act_rank], axis=1), SEQ, axis=0, tiled=True
    ).astype(jnp.float32).reshape(shard_count, tok_rows, 1, 2 * ranks)
    tenant_map = (
        tenant_table.reshape(shard_count * job_slots, tenant_total).astype(jnp.bfloat16)
    )

    def adapter_grad(rank_rows, columns):
        spread = (member_all[:, :, :, None] * rank_rows).astype(jnp.bfloat16)
        per_job = jnp.einsum(
            "stjr,stc->sjrc", spread, columns, preferred_element_type=jnp.float32
        )
        per_job = (per_job * weight_all[:, :, None, None]).astype(jnp.bfloat16)
        slab = per_job.shape[-1]
        return lax.dot_general(
            tenant_map,
            per_job.reshape(shard_count * job_slots, ranks * slab),
            contract_rows,
            preferred_element_type=jnp.float32,
        ).reshape(tenant_total, ranks, slab)

    grad_adapter_down = adapter_grad(rank_all[..., :ranks], hidden_cols)
    grad_adapter_up = adapter_grad(rank_all[..., ranks:], output_cols)
    return (grad_hidden, grad_adapter_down, grad_adapter_up)


SEQ = ("chip", "core")


def solution(mesh):
    chips = mesh.devices.reshape(mesh.shape["grp"], mesh.shape["seq"] // 2, 2)
    mesh = jax.sharding.Mesh(chips, ("grp", "chip", "core"))
    placed = (
        P(SEQ, "grp"),
        P(SEQ, "grp"),
        P(SEQ, "grp"),
        P(None, None, ("grp", "chip", "core")),
        P(None, None, ("grp", "chip", "core")),
        P(),
        P(),
    )
    return jax.shard_map(
        shards,
        mesh=mesh,
        in_specs=placed,
        out_specs=(P(SEQ, "grp"), P(None, None, ("grp", "chip", "core")), P(None, None, ("grp", "chip", "core"))),
        check_vma=False,
    )
```

profile of v0, /device:TPU:9, one launch (start us, length us, event | category | flops | bytes accessed | tf_op | source)
XLA Modules:
  0.0 398.0 jit_solution(628295968550063302)
XLA Ops:
  14.1 4.6 %reshape.235 = bf16[32,2,8192]{2,1,0:T(2,128)(2,1)} reshape(bf16[32,4,64,64]{3,2,1,0:T(8,128)(2,1)} %bitcast.114) | data formatting | bytes 2097152
  18.7 8.9 %all-to-all-start = ((bf16[32,2,8192]{2,1,0:T(2,128)(2,1)}), bf16[32,2,8192]{2,1,0:T(2,128)(2,1)S(1)}, u32[]{:S(2)}, u32[]{:S(2)}) async-start(bf16[32,2,8192]{2,1,0:T(2,128)(2,1)} %reshape.235), calls=%async_computation | async-start | bytes 2097152 | tf_op jit(solution)/shard_map/all_to_all | solution.py:44
  30.4 4.8 %copy.81 = bf16[4,32,64,224]{3,2,0,1:T(8,128)(2,1)} copy(bf16[4,32,64,224]{3,2,1,0:T(8,128)(2,1)} %bitcast.110) | data formatting | bytes 7340032 | tf_op jit(solution)/shard_map/gather | solution.py:43
  35.3 7.5 %all-to-all-done = bf16[32,2,8192]{2,1,0:T(2,128)(2,1)S(1)} async-done(((bf16[32,2,8192]{2,1,0:T(2,128)(2,1)}), bf16[32,2,8192]{2,1,0:T(2,128)(2,1)S(1)}, u32[]{:S(2)}, u32[]{:S(2)}) %all-to-all-start) | async-done | bytes 1048608 | tf_op jit(solution)/shard_map/all_to_all | solution.py:44
  42.8 6.4 %all-to-all-start.1 = ((bf16[4,32,64,224]{3,2,0,1:T(8,128)(2,1)}), bf16[4,32,64,224]{3,2,0,1:T(8,128)(2,1)}, u32[]{:S(2)}, u32[]{:S(2)}) async-start(bf16[4,32,64,224]{3,2,0,1:T(8,128)(2,1)} %copy.81), calls=%async_computation.1 | async-start | bytes 8388608 | tf_op jit(solution)/shard_map/all_to_all | solution.py:43
  56.7 50.0 %all-to-all-done.1 = bf16[4,32,64,224]{3,2,0,1:T(8,128)(2,1)} async-done(((bf16[4,32,64,224]{3,2,0,1:T(8,128)(2,1)}), bf16[4,32,64,224]{3,2,0,1:T(8,128)(2,1)}, u32[]{:S(2)}, u32[]{:S(2)}) %all-to-all-start.1) | async-done | bytes 3670048 | tf_op jit(solution)/shard_map/all_to_all | solution.py:43
  106.6 6.6 %copy.82 = bf16[4,1,64,32,224]{4,3,2,0,1:T(8,128)(2,1)} copy(bf16[4,1,64,32,224]{4,2,0,3,1:T(8,128)(2,1)} %bitcast.12) | data formatting | bytes 7340032 | tf_op jit(solution)/shard_map/all_to_all | solution.py:43
  113.2 9.0 %reshape.190 = bf16[256,7168]{1,0:T(8,128)(2,1)} reshape(bf16[4,1,64,32,224]{4,3,2,0,1:T(8,128)(2,1)} %copy.82) | data formatting | bytes 7340032 | tf_op jit(solution)/shard_map/reshape | solution.py:46
  125.4 23.4 %all-gather.4.cloned.1.call-done = bf16[2048,2048]{1,0:T(8,128)(2,1)} async-done(((bf16[128,2048]{1,0:T(8,128)(2,1)}), bf16[2048,2048]{1,0:T(8,128)(2,1)}) %all-gather.4.cloned.1.call-update) | async-done | bytes 8388624 | tf_op jit(solution)/shard_map/all_gather | solution.py:62
  148.8 14.2 %psum.7 = bf16[128,128]{0,1:T(8,128)(2,1)} all-reduce(bf16[128,128]{0,1:T(8,128)(2,1)S(1)} %pad_maximum_fusion.1), channel_id=1, replica_groups=mesh['grp'=4,'chip'=16,'core'=2] {'grp'}, use_global_device_ids=true, to_apply=%region_4.5 | all-reduce | flops 16384 | bytes 65536 | tf_op jit(solution)/shard_map/psum | solution.py:94
  163.1 21.3 %convolution_convert_fusion = bf16[2048,1792]{1,0:T(8,128)(2,1)} fusion(bf16[2048,2048]{1,0:T(8,128)(2,1)} %all-gather.4.cloned.1.call-done, bf16[1792,2048]{1,0:T(8,128)(2,1)} %all-gather.6.cloned.1.call-done), kind=kOutput, calls=%fused_computation.7 | convolution fusion | flops 15036055552 | bytes 23068672 | tf_op jit(solution)/shard_map/dot_general | solution.py:66
  186.7 10.0 %all-to-all-start.2 = ((bf16[128,32,224]{0,2,1:T(8,128)(2,1)}), bf16[128,32,224]{0,2,1:T(8,128)(2,1)}, u32[]{:S(2)}, u32[]{:S(2)}) async-start(bf16[128,32,224]{0,2,1:T(8,128)(2,1)} %bitcast.30), calls=%async_computation.3 | async-start | bytes 3670016 | tf_op jit(solution)/shard_map/all_to_all | solution.py:35
  198.9 18.3 %all-gather.8.cloned.1.call-done = bf16[4096,128]{0,1:T(8,128)(2,1)} async-done(((bf16[128,128]{0,1:T(8,128)(2,1)}), bf16[4096,128]{0,1:T(8,128)(2,1)}) %all-gather.8.cloned.1.call-update) | async-done | bytes 1048592 | tf_op jit(solution)/shard_map/all_gather | solution.py:114
  223.6 11.6 %all-to-all-start.3 = ((bf16[128,32,64]{0,2,1:T(8,128)(2,1)}), bf16[128,32,64]{0,2,1:T(8,128)(2,1)}, u32[]{:S(2)}, u32[]{:S(2)}) async-start(bf16[128,32,64]{0,2,1:T(8,128)(2,1)} %bitcast.39), calls=%async_computation.4 | async-start | bytes 1048576 | tf_op jit(solution)/shard_map/all_to_all | solution.py:38
  235.2 4.8 %multiply_convert_fusion = bf16[32,4,64,224]{3,2,1,0:T(8,128)(2,1)} fusion(f32[32,4]{1,0:T(8,128)S(1)} %copy.90, f32[32,128,64]{1,2,0:T(8,128)S(1)} %copy.88, f32[32,128,4]{1,2,0:T(4,128)S(1)} %fusion.9, bf16[128,32,224]{0,2,1:T(8,128)(2,1)} %all-to-all-done.2), kind=kOutput, calls=%fused_computation.6 | convolution fusion | flops 475529216 | bytes 6619648 | tf_op jit(solution)/shard_map/stjr,stc->sjrc/dot_general | solution.py:123
  240.0 8.6 %reshape.197 = bf16[128,14336]{1,0:T(8,128)(2,1)} reshape(bf16[32,4,64,224]{3,2,1,0:T(8,128)(2,1)} %multiply_convert_fusion) | data formatting | bytes 7340032 | tf_op jit(solution)/shard_map/reshape | solution.py:130
  248.6 6.2 %copy.91 = bf16[14336,128]{1,0:T(8,128)(2,1)} copy(bf16[14336,128]{0,1:T(8,128)(2,1)} %bitcast.113) | data formatting | bytes 7340032 | tf_op jit(solution)/shard_map/dot_general | solution.py:128
  255.4 6.5 %fusion.13 = f32[64,64,224]{2,0,1:T(8,128)} fusion(bf16[64,224,128]{2,1,0:T(8,128)(2,1)} %bitcast.112, s32[128]{0:T(128)S(1)} %eq.30), kind=kOutput, calls=%fused_computation.40 | convolution fusion | flops 234905600 | bytes 7340544 | tf_op jit(solution)/shard_map/dot_general | solution.py:128
  261.9 33.3 %reduce-scatter.2.cloned.1.call-done = bf16[512,1792]{1,0:T(8,128)(2,1)} async-done(((bf16[2048,1792]{1,0:T(8,128)(2,1)}), bf16[512,1792]{1,0:T(8,128)(2,1)}) %reduce-scatter.2.cloned.1.call-update) | async-done | bytes 1835024 | tf_op jit(solution)/shard_map/reduce_scatter | solution.py:69
  299.7 3.4 collective-permute-start.1
  311.7 6.6 %copy.96 = f32[64,64,224]{2,1,0:T(8,128)} copy(f32[64,64,224]{2,0,1:T(8,128)} %fusion.13) | data formatting | bytes 7340032
  326.0 23.7 %collective-permute-done.1 = bf16[128,1792]{1,0:T(8,128)(2,1)} collective-permute-done((bf16[128,1792]{1,0:T(8,128)(2,1)}, bf16[128,1792]{1,0:T(8,128)(2,1)}, u32[]{:S(2)}, u32[]{:S(2)}) %collective-permute-start.1) | collective-permute-done | bytes 458784 | tf_op jit(solution)/shard_map/ppermute | solution.py:90
  349.7 24.2 %collective-permute-done.2 = bf16[128,1792]{1,0:T(8,128)(2,1)} collective-permute-done((bf16[128,1792]{1,0:T(8,128)(2,1)}, bf16[128,1792]{1,0:T(8,128)(2,1)}, u32[]{:S(2)}, u32[]{:S(2)}) %collective-permute-start.2) | collective-permute-done | bytes 458784 | tf_op jit(solution)/shard_map/ppermute | solution.py:90
  373.9 8.2 %collective-permute-done.3 = bf16[128,1792]{1,0:T(8,128)(2,1)} collective-permute-done((bf16[128,1792]{1,0:T(8,128)(2,1)}, bf16[128,1792]{1,0:T(8,128)(2,1)}, u32[]{:S(2)}, u32[]{:S(2)}) %collective-permute-start.3) | collective-permute-done | bytes 458784 | tf_op jit(solution)/shard_map/ppermute | solution.py:90
  (88 shorter events, 61.8 us)
Async XLA Ops:
  7.2 20.4 %copy-start = (bf16[64,64,224]{2,1,0:T(8,128)(2,1)S(1)}, bf16[64,64,224]{2,1,0:T(8,128)(2,1)}, u32[]{:S(2)}) copy-start(bf16[64,64,224]{2,1,0:T(8,128)(2,1)} %param.10) | copy-start | bytes 5505028
  7.2 1.5 copy-start.8
  7.2 1.6 copy-start.6
  7.2 118.2 %all-gather.6.cloned.1.call-start = ((), (), s32[]{:S(2)}) async-start(), calls=%async_computation.6 | async-start | bytes 11010048 | tf_op jit(solution)/shard_map/all_gather | solution.py:61
  7.9 140.9 %all-gather.4.cloned.1.call-start = ((), (), s32[]{:S(2)}) async-start(), calls=%async_computation.5 | async-start | bytes 8912896 | tf_op jit(solution)/shard_map/all_gather | solution.py:62
  18.7 24.1 %all-to-all-start = ((bf16[32,2,8192]{2,1,0:T(2,128)(2,1)}), bf16[32,2,8192]{2,1,0:T(2,128)(2,1)S(1)}, u32[]{:S(2)}, u32[]{:S(2)}) async-start(bf16[32,2,8192]{2,1,0:T(2,128)(2,1)} %reshape.235), calls=%async_computation | async-start | bytes 2097152 | tf_op jit(solution)/shard_map/all_to_all | solution.py:44
  35.3 14.0 %copy-start.9 = (s32[32,4]{0,1:T(4,128)S(1)}, s32[32,4]{0,1:T(4,128)}, u32[]{:S(2)}) copy-start(s32[32,4]{0,1:T(4,128)} %param.13) | copy-start | bytes 1540
  42.8 63.8 %all-to-all-start.1 = ((bf16[4,32,64,224]{3,2,0,1:T(8,128)(2,1)}), bf16[4,32,64,224]{3,2,0,1:T(8,128)(2,1)}, u32[]{:S(2)}, u32[]{:S(2)}) async-start(bf16[4,32,64,224]{3,2,0,1:T(8,128)(2,1)} %copy.81), calls=%async_computation.1 | async-start | bytes 8388608 | tf_op jit(solution)/shard_map/all_to_all | solution.py:43
  49.2 168.0 %all-gather.8.cloned.1.call-start = ((), (), s32[]{:S(2)}) async-start(), calls=%async_computation.8 | async-start | bytes 1081344 | tf_op jit(solution)/shard_map/all_gather | solution.py:114
  51.2 3.8 copy-start.5
  113.2 9.0 %copy-start.4 = (bf16[128,7168]{1,0:T(8,128)(2,1)S(1)}, bf16[128,7168]{1,0:T(8,128)(2,1)}, u32[]{:S(2)}) copy-start(bf16[128,7168]{1,0:T(8,128)(2,1)} %param.8) | copy-start | bytes 5505028
  163.0 132.1 %reduce-scatter.2.cloned.1.call-start = ((), (), s32[]{:S(2)}) async-start(), calls=%async_computation.7 | async-start | bytes 9175040 | tf_op jit(solution)/shard_map/reduce_scatter | solution.py:69
  184.4 14.4 %copy-start.7 = (bf16[128,128]{0,1:T(8,128)(2,1)S(1)}, bf16[128,128]{0,1:T(8,128)(2,1)}, u32[]{:S(2)}) copy-start(bf16[128,128]{0,1:T(8,128)(2,1)} %psum.7) | copy-start | bytes 98308
  186.7 36.9 %all-to-all-start.2 = ((bf16[128,32,224]{0,2,1:T(8,128)(2,1)}), bf16[128,32,224]{0,2,1:T(8,128)(2,1)}, u32[]{:S(2)}, u32[]{:S(2)}) async-start(bf16[128,32,224]{0,2,1:T(8,128)(2,1)} %bitcast.30), calls=%async_computation.3 | async-start | bytes 3670016 | tf_op jit(solution)/shard_map/all_to_all | solution.py:35
  223.6 85.1 %all-to-all-start.3 = ((bf16[128,32,64]{0,2,1:T(8,128)(2,1)}), bf16[128,32,64]{0,2,1:T(8,128)(2,1)}, u32[]{:S(2)}, u32[]{:S(2)}) async-start(bf16[128,32,64]{0,2,1:T(8,128)(2,1)} %bitcast.39), calls=%async_computation.4 | async-start | bytes 1048576 | tf_op jit(solution)/shard_map/all_to_all | solution.py:38
  248.6 6.2 %copy-start.3 = (f32[32,128,64]{2,1,0:T(8,128)S(1)}, f32[32,128,64]{2,1,0:T(8,128)}, u32[]{:S(2)}) copy-start(f32[32,128,64]{2,1,0:T(8,128)} %get-tuple-element.26) | copy-start | bytes 3145732
  297.8 28.2 %collective-permute-start = (bf16[128,1792]{1,0:T(8,128)(2,1)}, bf16[128,1792]{1,0:T(8,128)(2,1)}, u32[]{:S(2)}, u32[]{:S(2)}) collective-permute-start(bf16[128,1792]{1,0:T(8,128)(2,1)} %get-tuple-element.28), channel_id=1, source_target_pairs={{0,0},{1,1},{2,2},{3,3},{4,4},{5,5},{6,6},{7,7},{8,32},{9,33},{10,... | collective-permute-start | bytes 1376264 | tf_op jit(solution)/shard_map/ppermute | solution.py:90
  299.7 50.0 %collective-permute-start.1 = (bf16[128,1792]{1,0:T(8,128)(2,1)}, bf16[128,1792]{1,0:T(8,128)(2,1)}, u32[]{:S(2)}, u32[]{:S(2)}) collective-permute-start(bf16[128,1792]{1,0:T(8,128)(2,1)} %get-tuple-element.31), channel_id=1, source_target_pairs={{0,2},{1,3},{2,4},{3,5},{4,6},{5,7},{6,0},{7,1},{8,34},{9,35},{10,... | collective-permute-start | bytes 1376264 | tf_op jit(solution)/shard_map/ppermute | solution.py:90
  303.1 70.8 %collective-permute-start.2 = (bf16[128,1792]{1,0:T(8,128)(2,1)}, bf16[128,1792]{1,0:T(8,128)(2,1)}, u32[]{:S(2)}, u32[]{:S(2)}) collective-permute-start(bf16[128,1792]{1,0:T(8,128)(2,1)} %get-tuple-element.30), channel_id=1, source_target_pairs={{0,4},{1,5},{2,6},{3,7},{4,0},{5,1},{6,2},{7,3},{8,36},{9,37},{10,... | collective-permute-start | bytes 1376264 | tf_op jit(solution)/shard_map/ppermute | solution.py:90
  305.5 76.6 %collective-permute-start.3 = (bf16[128,1792]{1,0:T(8,128)(2,1)}, bf16[128,1792]{1,0:T(8,128)(2,1)}, u32[]{:S(2)}, u32[]{:S(2)}) collective-permute-start(bf16[128,1792]{1,0:T(8,128)(2,1)} %get-tuple-element.29), channel_id=1, source_target_pairs={{0,6},{1,7},{2,0},{3,1},{4,2},{5,3},{6,4},{7,5},{8,38},{9,39},{10,... | collective-permute-start | bytes 1376264 | tf_op jit(solution)/shard_map/ppermute | solution.py:90
  387.5 2.0 copy-start.2
  387.9 3.6 copy-start.1
Sparse Core Ops, SparseCore 0:
  9.7 23.8 all-gather.5
  35.7 113.0 all-gather.3
  163.1 53.9 all-gather.7
  219.4 75.6 reduce-scatter.1
where the time goes:
time: 403 us; the launch traced here: 398 us
  waiting for transfers between devices  190 us (47%)
  local copies, waits for them, and re-layouts  84.1 us (21%)
  starting transfers between devices  47.8 us (12%)
  matrix products  43.5 us (11%)
  blocking collectives  14.2 us (4%)
  between operations  14.2 us (4%)
  other arithmetic  4.29 us (1%)
    ppermute x4, waiting for transfers between devices, shards(): arrived.append(lax.ppermute(piece, ('grp', 'chip', 'core'), pairs))  56.1 us
    all_to_all x1, waiting for transfers between devices, shards(): lax.all_to_all(adapter_down[chosen], SEQ, split_axis=1, concat_axis=3, ti...  50 us
    reduce_scatter x1, waiting for transfers between devices, shards(): lax.psum_scatter(partial_value.astype(jnp.bfloat16), 'grp', scatter_dimen...  33.3 us
    all_gather x1, waiting for transfers between devices, shards(): tokens_same_core = lax.all_gather(grad_output, 'chip', axis=0, tiled=True)  23.4 us
    dot_general x1, matrix products, shards(): lax.dot_general(tokens_same_core, weight_pair, contract_last, preferred_e...  21.3 us
    unnamed x28, local copies, waits for them, and re-layouts  20.3 us
    all_gather x1, waiting for transfers between devices, shards(): lax.all_gather(jnp.concatenate([grad_rank, act_rank], axis=1), SEQ, axis=...  18.3 us
    psum x1, blocking collectives, shards(): rank_sum = lax.psum(rank_part.astype(jnp.float32), 'grp')  14.2 us
  transfers between devices with their start and end apart: 12, of which 8 were waited for; matrix products, arithmetic and copies ran while one was open for 31% of the time, Pallas kernels for 0%

commit v1 on v0

--- a/solution.py
+++ b/solution.py
@@ -60,8 +60,9 @@
     )
     weight_pair = lax.all_gather(down_weight, "core", axis=0, tiled=True)
     tokens_same_core = lax.all_gather(grad_output, "chip", axis=0, tiled=True)
-    tokens_same_core, weight_pair, rank_part = lax.optimization_barrier(
-        (tokens_same_core, weight_pair, rank_part)
+    rank_sum = lax.psum(rank_part.astype(jnp.float32), "grp")
+    tokens_same_core, weight_pair, rank_sum = lax.optimization_barrier(
+        (tokens_same_core, weight_pair, rank_sum)
     )
     partial_value = lax.dot_general(
         tokens_same_core, weight_pair, contract_last, preferred_element_type=jnp.float32
@@ -70,6 +71,9 @@
         partial_value.astype(jnp.bfloat16), "grp", scatter_dimension=0, tiled=True
     )
     quarter = quarter.reshape(group_count, tok_rows, quarter.shape[1])
+    quarter, rank_sum, hidden_cols, output_cols = lax.optimization_barrier(
+        (quarter, rank_sum, hidden_cols, output_cols)
+    )
     chip_count = lax.axis_size("chip")
     row_of_chip = chip_count // group_count
     chip = lax.axis_index("chip")
@@ -91,7 +95,6 @@
     arrived = jnp.stack(arrived)
     order = (lane - jnp.arange(group_count)) % group_count
     base_grad = jnp.take(arrived, order, axis=0).transpose(1, 0, 2).reshape(tok_rows, -1)
-    rank_sum = lax.psum(rank_part.astype(jnp.float32), "grp")
     grad_rank = rank_sum[:, :ranks].astype(jnp.bfloat16)
     act_rank = rank_sum[:, ranks:].astype(jnp.bfloat16)
     grad_spread = (

time: 403 us -> 413 us (1.025)
  waiting for transfers between devices: 190 us -> 212 us
  starting transfers between devices: 47.8 us -> 37.4 us
  matrix products: 43.5 us -> 39.1 us
    all_to_all x1, waiting for transfers between devices: 0.01 us -> 22.8 us  [shards(): lax.all_to_all(hidden.reshape(tok_rows, shard_count, down_slab), SEQ, spl...]
    all_gather x1, waiting for transfers between devices: 23.4 us -> 7.62 us  [shards(): tokens_same_core = lax.all_gather(grad_output, 'chip', axis=0, tiled=True)]
    ppermute x4, waiting for transfers between devices: 56.1 us -> 71.8 us  [shards(): arrived.append(lax.ppermute(piece, ('grp', 'chip', 'core'), pairs))]
    all_to_all x1, waiting for transfers between devices: 0.01 us -> 8.04 us  [shards(): lax.all_to_all(grad_output.reshape(tok_rows, shard_count, up_slab), SEQ,...]
    reduce_scatter x1, waiting for transfers between devices: 33.3 us -> 26.3 us  [shards(): lax.psum_scatter(partial_value.astype(jnp.bfloat16), 'grp', scatter_dimen...]
    all_to_all x1, starting transfers between devices: 11.6 us -> 6.2 us  [shards(): lax.all_to_all(grad_output.reshape(tok_rows, shard_count, up_slab), SEQ,...]
    all_to_all x1, starting transfers between devices: 10 us -> 5.04 us  [shards(): lax.all_to_all(hidden.reshape(tok_rows, shard_count, down_slab), SEQ, spl...]
    unnamed x28 -> x38, local copies, waits for them, and re-layouts: 20.3 us -> 18.1 us
  transfers between devices with their start and end apart: 12 -> 12, of which waited for: 8 -> 11; matrix products, arithmetic and copies ran while one was open for 31% -> 15% of each run, Pallas kernels for 0% -> 0%
where the time goes in v1:
time: 413 us; the launch traced here: 410 us
  waiting for transfers between devices  212 us (51%)
  local copies, waits for them, and re-layouts  85.1 us (21%)
  matrix products  39.1 us (9%)
  starting transfers between devices  37.4 us (9%)
  blocking collectives  15.8 us (4%)
  between operations  14.2 us (3%)
  other arithmetic  6.14 us (1%)
    ppermute x4, waiting for transfers between devices, shards(): arrived.append(lax.ppermute(piece, ('grp', 'chip', 'core'), pairs))  71.8 us
    all_to_all x1, waiting for transfers between devices, shards(): lax.all_to_all(adapter_down[chosen], SEQ, split_axis=1, concat_axis=3, ti...  50 us
    reduce_scatter x1, waiting for transfers between devices, shards(): lax.psum_scatter(partial_value.astype(jnp.bfloat16), 'grp', scatter_dimen...  26.3 us
    all_to_all x1, waiting for transfers between devices, shards(): lax.all_to_all(hidden.reshape(tok_rows, shard_count, down_slab), SEQ, spl...  22.8 us
    dot_general x1, matrix products, shards(): lax.dot_general(tokens_same_core, weight_pair, contract_last, preferred_e...  21.3 us
    unnamed x38, local copies, waits for them, and re-layouts  18.1 us
    all_gather x1, waiting for transfers between devices, shards(): lax.all_gather(jnp.concatenate([grad_rank, act_rank], axis=1), SEQ, axis=...  16.4 us
    psum x1, blocking collectives, shards(): rank_sum = lax.psum(rank_part.astype(jnp.float32), 'grp')  15.8 us
  transfers between devices with their start and end apart: 12, of which 11 were waited for; matrix products, arithmetic and copies ran while one was open for 15% of the time, Pallas kernels for 0%

profile of v1, /device:TPU:9, one launch (start us, length us, event | category | flops | bytes accessed | tf_op | source)
XLA Modules:
  0.0 409.7 jit_solution(15039355121244740926)
XLA Ops:
  14.1 4.6 %reshape.235 = bf16[32,2,8192]{2,1,0:T(2,128)(2,1)} reshape(bf16[32,4,64,64]{3,2,1,0:T(8,128)(2,1)} %bitcast.112) | data formatting | bytes 2097152
  18.7 8.9 %all-to-all-start = ((bf16[32,2,8192]{2,1,0:T(2,128)(2,1)}), bf16[32,2,8192]{2,1,0:T(2,128)(2,1)S(1)}, u32[]{:S(2)}, u32[]{:S(2)}) async-start(bf16[32,2,8192]{2,1,0:T(2,128)(2,1)} %reshape.235), calls=%async_computation | async-start | bytes 2097152 | tf_op jit(solution)/shard_map/all_to_all | solution.py:44
  30.4 4.8 %copy.81 = bf16[4,32,64,224]{3,2,0,1:T(8,128)(2,1)} copy(bf16[4,32,64,224]{3,2,1,0:T(8,128)(2,1)} %bitcast.108) | data formatting | bytes 7340032 | tf_op jit(solution)/shard_map/gather | solution.py:43
  35.2 7.6 %all-to-all-done = bf16[32,2,8192]{2,1,0:T(2,128)(2,1)S(1)} async-done(((bf16[32,2,8192]{2,1,0:T(2,128)(2,1)}), bf16[32,2,8192]{2,1,0:T(2,128)(2,1)S(1)}, u32[]{:S(2)}, u32[]{:S(2)}) %all-to-all-start) | async-done | bytes 1048608 | tf_op jit(solution)/shard_map/all_to_all | solution.py:44
  42.8 6.4 %all-to-all-start.1 = ((bf16[4,32,64,224]{3,2,0,1:T(8,128)(2,1)}), bf16[4,32,64,224]{3,2,0,1:T(8,128)(2,1)}, u32[]{:S(2)}, u32[]{:S(2)}) async-start(bf16[4,32,64,224]{3,2,0,1:T(8,128)(2,1)} %copy.81), calls=%async_computation.1 | async-start | bytes 8388608 | tf_op jit(solution)/shard_map/all_to_all | solution.py:43
  56.7 50.0 %all-to-all-done.1 = bf16[4,32,64,224]{3,2,0,1:T(8,128)(2,1)} async-done(((bf16[4,32,64,224]{3,2,0,1:T(8,128)(2,1)}), bf16[4,32,64,224]{3,2,0,1:T(8,128)(2,1)}, u32[]{:S(2)}, u32[]{:S(2)}) %all-to-all-start.1) | async-done | bytes 3670048 | tf_op jit(solution)/shard_map/all_to_all | solution.py:43
  106.6 6.6 %copy.82 = bf16[4,1,64,32,224]{4,3,2,0,1:T(8,128)(2,1)} copy(bf16[4,1,64,32,224]{4,2,0,3,1:T(8,128)(2,1)} %bitcast.12) | data formatting | bytes 7340032 | tf_op jit(solution)/shard_map/all_to_all | solution.py:43
  113.2 9.0 %reshape.190 = bf16[256,7168]{1,0:T(8,128)(2,1)} reshape(bf16[4,1,64,32,224]{4,3,2,0,1:T(8,128)(2,1)} %copy.82) | data formatting | bytes 7340032 | tf_op jit(solution)/shard_map/reshape | solution.py:46
  125.4 15.8 %psum.7 = bf16[128,128]{0,1:T(8,128)(2,1)} all-reduce(f32[128,128]{0,1:T(8,128)S(1)} %maximum_convert_fusion), channel_id=1, replica_groups=mesh['grp'=4,'chip'=16,'core'=2] {'grp'}, use_global_device_ids=true, to_apply=%region_3.4 | all-reduce | flops 16384 | bytes 98304 | tf_op jit(solution)/shard_map/psum | solution.py:63
  141.2 7.6 %all-gather.4.cloned.1.call-done = bf16[2048,2048]{1,0:T(8,128)(2,1)} async-done(((bf16[128,2048]{1,0:T(8,128)(2,1)}), bf16[2048,2048]{1,0:T(8,128)(2,1)}) %all-gather.4.cloned.1.call-update) | async-done | bytes 8388624 | tf_op jit(solution)/shard_map/all_gather | solution.py:62
  148.8 21.3 %convolution_convert_fusion = bf16[2048,1792]{1,0:T(8,128)(2,1)} fusion(bf16[2048,2048]{1,0:T(8,128)(2,1)} %all-gather.4.cloned.1.call-done, bf16[1792,2048]{1,0:T(8,128)(2,1)} %all-gather.6.cloned.1.call-done), kind=kOutput, calls=%fused_computation.7 | convolution fusion | flops 15036055552 | bytes 23068672 | tf_op jit(solution)/shard_map/dot_general | solution.py:67
  171.1 6.2 %all-to-all-start.3 = ((bf16[128,32,64]{0,2,1:T(8,128)(2,1)}), bf16[128,32,64]{0,2,1:T(8,128)(2,1)S(1)}, u32[]{:S(2)}, u32[]{:S(2)}) async-start(bf16[128,32,64]{0,2,1:T(8,128)(2,1)} %bitcast.20), calls=%async_computation.4 | async-start | bytes 1048576 | tf_op jit(solution)/shard_map/all_to_all | solution.py:38
  179.6 8.0 %all-to-all-done.3 = bf16[128,32,64]{0,2,1:T(8,128)(2,1)S(1)} async-done(((bf16[128,32,64]{0,2,1:T(8,128)(2,1)}), bf16[128,32,64]{0,2,1:T(8,128)(2,1)S(1)}, u32[]{:S(2)}, u32[]{:S(2)}) %all-to-all-start.3) | async-done | bytes 524320 | tf_op jit(solution)/shard_map/all_to_all | solution.py:38
  187.7 5.0 %all-to-all-start.2 = ((bf16[128,32,224]{0,2,1:T(8,128)(2,1)}), bf16[128,32,224]{0,2,1:T(8,128)(2,1)S(1)}, u32[]{:S(2)}, u32[]{:S(2)}) async-start(bf16[128,32,224]{0,2,1:T(8,128)(2,1)} %bitcast.115), calls=%async_computation.3 | async-start | bytes 3670016 | tf_op jit(solution)/shard_map/all_to_all | solution.py:35
  193.2 22.8 %all-to-all-done.2 = bf16[128,32,224]{0,2,1:T(8,128)(2,1)S(1)} async-done(((bf16[128,32,224]{0,2,1:T(8,128)(2,1)}), bf16[128,32,224]{0,2,1:T(8,128)(2,1)S(1)}, u32[]{:S(2)}, u32[]{:S(2)}) %all-to-all-start.2) | async-done | bytes 1835040 | tf_op jit(solution)/shard_map/all_to_all | solution.py:35
  216.1 26.3 %reduce-scatter.2.cloned.1.call-done = bf16[512,1792]{1,0:T(8,128)(2,1)} async-done(((bf16[2048,1792]{1,0:T(8,128)(2,1)}), bf16[512,1792]{1,0:T(8,128)(2,1)}) %reduce-scatter.2.cloned.1.call-update) | async-done | bytes 1835024 | tf_op jit(solution)/shard_map/reduce_scatter | solution.py:70
  257.5 10.6 %collective-permute-done = bf16[128,1792]{1,0:T(8,128)(2,1)} collective-permute-done((bf16[128,1792]{1,0:T(8,128)(2,1)}, bf16[128,1792]{1,0:T(8,128)(2,1)}, u32[]{:S(2)}, u32[]{:S(2)}) %collective-permute-start) | collective-permute-done | bytes 458784 | tf_op jit(solution)/shard_map/ppermute | solution.py:94
  268.1 28.9 %collective-permute-done.1 = bf16[128,1792]{1,0:T(8,128)(2,1)} collective-permute-done((bf16[128,1792]{1,0:T(8,128)(2,1)}, bf16[128,1792]{1,0:T(8,128)(2,1)}, u32[]{:S(2)}, u32[]{:S(2)}) %collective-permute-start.1) | collective-permute-done | bytes 458784 | tf_op jit(solution)/shard_map/ppermute | solution.py:94
  297.0 24.1 %collective-permute-done.2 = bf16[128,1792]{1,0:T(8,128)(2,1)} collective-permute-done((bf16[128,1792]{1,0:T(8,128)(2,1)S(1)}, bf16[128,1792]{1,0:T(8,128)(2,1)}, u32[]{:S(2)}, u32[]{:S(2)}) %collective-permute-start.2) | collective-permute-done | bytes 458784 | tf_op jit(solution)/shard_map/ppermute | solution.py:94
  321.1 8.2 %collective-permute-done.3 = bf16[128,1792]{1,0:T(8,128)(2,1)} collective-permute-done((bf16[128,1792]{1,0:T(8,128)(2,1)S(1)}, bf16[128,1792]{1,0:T(8,128)(2,1)}, u32[]{:S(2)}, u32[]{:S(2)}) %collective-permute-start.3) | collective-permute-done | bytes 458784 | tf_op jit(solution)/shard_map/ppermute | solution.py:94
  341.4 16.4 %all-gather.8.cloned.1.call-done = bf16[4096,128]{0,1:T(8,128)(2,1)} async-done(((bf16[128,128]{0,1:T(8,128)(2,1)}), bf16[4096,128]{0,1:T(8,128)(2,1)}) %all-gather.8.cloned.1.call-update) | async-done | bytes 1048592 | tf_op jit(solution)/shard_map/all_gather | solution.py:117
  379.6 8.5 %reshape.199 = bf16[128,14336]{1,0:T(8,128)(2,1)} reshape(bf16[32,4,64,224]{3,2,1,0:T(8,128)(2,1)} %multiply_convert_fusion) | data formatting | bytes 7340032 | tf_op jit(solution)/shard_map/reshape | solution.py:133
  388.1 6.0 %copy.92 = bf16[14336,128]{1,0:T(8,128)(2,1)} copy(bf16[14336,128]{0,1:T(8,128)(2,1)} %bitcast.111) | data formatting | bytes 7340032 | tf_op jit(solution)/shard_map/dot_general | solution.py:131
  394.2 4.5 %fusion.13 = f32[64,64,224]{2,0,1:T(8,128)S(1)} fusion(bf16[64,224,128]{2,1,0:T(8,128)(2,1)} %bitcast.110, s32[128]{0:T(128)S(1)} %copy-done.14), kind=kOutput, calls=%fused_computation.40 | convolution fusion | flops 234905600 | bytes 7340544 | tf_op jit(solution)/shard_map/dot_general | solution.py:131
  (98 shorter events, 77.3 us)
Async XLA Ops:
  7.2 20.4 %copy-start = (bf16[64,64,224]{2,1,0:T(8,128)(2,1)S(1)}, bf16[64,64,224]{2,1,0:T(8,128)(2,1)}, u32[]{:S(2)}) copy-start(bf16[64,64,224]{2,1,0:T(8,128)(2,1)} %param.10) | copy-start | bytes 5505028
  7.2 134.0 %all-gather.6.cloned.1.call-start = ((), (), s32[]{:S(2)}) async-start(), calls=%async_computation.6 | async-start | bytes 11010048 | tf_op jit(solution)/shard_map/all_gather | solution.py:61
  7.9 140.9 %all-gather.4.cloned.1.call-start = ((), (), s32[]{:S(2)}) async-start(), calls=%async_computation.5 | async-start | bytes 8912896 | tf_op jit(solution)/shard_map/all_gather | solution.py:62
  18.7 24.1 %all-to-all-start = ((bf16[32,2,8192]{2,1,0:T(2,128)(2,1)}), bf16[32,2,8192]{2,1,0:T(2,128)(2,1)S(1)}, u32[]{:S(2)}, u32[]{:S(2)}) async-start(bf16[32,2,8192]{2,1,0:T(2,128)(2,1)} %reshape.235), calls=%async_computation | async-start | bytes 2097152 | tf_op jit(solution)/shard_map/all_to_all | solution.py:44
  35.2 14.0 %copy-start.13 = (s32[32,4]{0,1:T(4,128)S(1)}, s32[32,4]{0,1:T(4,128)}, u32[]{:S(2)}) copy-start(s32[32,4]{0,1:T(4,128)} %param.13) | copy-start | bytes 1540
  42.8 63.8 %all-to-all-start.1 = ((bf16[4,32,64,224]{3,2,0,1:T(8,128)(2,1)}), bf16[4,32,64,224]{3,2,0,1:T(8,128)(2,1)}, u32[]{:S(2)}, u32[]{:S(2)}) async-start(bf16[4,32,64,224]{3,2,0,1:T(8,128)(2,1)} %copy.81), calls=%async_computation.1 | async-start | bytes 8388608 | tf_op jit(solution)/shard_map/all_to_all | solution.py:43
  49.2 193.2 %reduce-scatter.2.cloned.1.call-start = ((), (), s32[]{:S(2)}) async-start(), calls=%async_computation.7 | async-start | bytes 9175040 | tf_op jit(solution)/shard_map/reduce_scatter | solution.py:70
  49.7 75.7 %copy-start.11 = (f32[128,4]{0,1:T(4,128)}, f32[128,4]{0,1:T(4,128)S(1)}, u32[]{:S(2)}) copy-start(f32[128,4]{0,1:T(4,128)S(1)} %fusion.18) | copy-start | bytes 6148
  51.2 3.8 copy-start.6
  113.2 9.0 %copy-start.5 = (bf16[128,7168]{1,0:T(8,128)(2,1)S(1)}, bf16[128,7168]{1,0:T(8,128)(2,1)}, u32[]{:S(2)}) copy-start(bf16[128,7168]{1,0:T(8,128)(2,1)} %param.8) | copy-start | bytes 5505028
  171.1 16.5 %all-to-all-start.3 = ((bf16[128,32,64]{0,2,1:T(8,128)(2,1)}), bf16[128,32,64]{0,2,1:T(8,128)(2,1)S(1)}, u32[]{:S(2)}, u32[]{:S(2)}) async-start(bf16[128,32,64]{0,2,1:T(8,128)(2,1)} %bitcast.20), calls=%async_computation.4 | async-start | bytes 1048576 | tf_op jit(solution)/shard_map/all_to_all | solution.py:38
  187.7 69.8 %copy-start.9 = (bf16[128,128]{0,1:T(8,128)(2,1)S(1)}, bf16[128,128]{0,1:T(8,128)(2,1)}, u32[]{:S(2)}) copy-start(bf16[128,128]{0,1:T(8,128)(2,1)} %psum.7) | copy-start | bytes 98308
  187.7 69.8 %copy-start.12 = (f32[128,4]{0,1:T(4,128)S(1)}, f32[128,4]{0,1:T(4,128)}, u32[]{:S(2)}) copy-start(f32[128,4]{0,1:T(4,128)} %copy-done.11) | copy-start | bytes 6148
  187.7 28.4 %all-to-all-start.2 = ((bf16[128,32,224]{0,2,1:T(8,128)(2,1)}), bf16[128,32,224]{0,2,1:T(8,128)(2,1)S(1)}, u32[]{:S(2)}, u32[]{:S(2)}) async-start(bf16[128,32,224]{0,2,1:T(8,128)(2,1)} %bitcast.115), calls=%async_computation.3 | async-start | bytes 3670016 | tf_op jit(solution)/shard_map/all_to_all | solution.py:35
  192.7 165.1 %all-gather.8.cloned.1.call-start = ((), (), s32[]{:S(2)}) async-start(), calls=%async_computation.8 | async-start | bytes 1081344 | tf_op jit(solution)/shard_map/all_gather | solution.py:117
  216.1 116.1 %copy-start.3 = (bf16[128,32,224]{0,2,1:T(8,128)(2,1)}, bf16[128,32,224]{0,2,1:T(8,128)(2,1)S(1)}, u32[]{:S(2)}) copy-start(bf16[128,32,224]{0,2,1:T(8,128)(2,1)S(1)} %all-to-all-done.2) | copy-start | bytes 5505028
  244.9 23.2 %collective-permute-start = (bf16[128,1792]{1,0:T(8,128)(2,1)}, bf16[128,1792]{1,0:T(8,128)(2,1)}, u32[]{:S(2)}, u32[]{:S(2)}) collective-permute-start(bf16[128,1792]{1,0:T(8,128)(2,1)} %get-tuple-element.36), channel_id=1, source_target_pairs={{0,0},{1,1},{2,2},{3,3},{4,4},{5,5},{6,6},{7,7},{8,32},{9,33},{10,... | collective-permute-start | bytes 1376264 | tf_op jit(solution)/shard_map/ppermute | solution.py:94
  246.8 50.2 %collective-permute-start.1 = (bf16[128,1792]{1,0:T(8,128)(2,1)}, bf16[128,1792]{1,0:T(8,128)(2,1)}, u32[]{:S(2)}, u32[]{:S(2)}) collective-permute-start(bf16[128,1792]{1,0:T(8,128)(2,1)} %get-tuple-element.39), channel_id=1, source_target_pairs={{0,2},{1,3},{2,4},{3,5},{4,6},{5,7},{6,0},{7,1},{8,34},{9,35},{10,... | collective-permute-start | bytes 1376264 | tf_op jit(solution)/shard_map/ppermute | solution.py:94
  250.2 70.8 %collective-permute-start.2 = (bf16[128,1792]{1,0:T(8,128)(2,1)S(1)}, bf16[128,1792]{1,0:T(8,128)(2,1)}, u32[]{:S(2)}, u32[]{:S(2)}) collective-permute-start(bf16[128,1792]{1,0:T(8,128)(2,1)S(1)} %get-tuple-element.38), channel_id=1, source_target_pairs={{0,4},{1,5},{2,6},{3,7},{4,0},{5,1},{6,2},{7,3},{8,36},{9,37},{10,... | collective-permute-start | bytes 1376264 | tf_op jit(solution)/shard_map/ppermute | solution.py:94
  252.5 76.8 %collective-permute-start.3 = (bf16[128,1792]{1,0:T(8,128)(2,1)S(1)}, bf16[128,1792]{1,0:T(8,128)(2,1)}, u32[]{:S(2)}, u32[]{:S(2)}) collective-permute-start(bf16[128,1792]{1,0:T(8,128)(2,1)S(1)} %get-tuple-element.37), channel_id=1, source_target_pairs={{0,6},{1,7},{2,0},{3,1},{4,2},{5,3},{6,4},{7,5},{8,38},{9,39},{10,... | collective-permute-start | bytes 1376264 | tf_op jit(solution)/shard_map/ppermute | solution.py:94
  359.3 4.9 %copy-start.8 = (f32[32,128,4]{1,2,0:T(4,128)S(1)}, f32[32,128,4]{1,2,0:T(4,128)}, u32[]{:S(2)}) copy-start(f32[32,128,4]{1,2,0:T(4,128)} %fusion.9) | copy-start | bytes 196612
  366.3 4.0 copy-start.14
  373.9 2.3 copy-start.4
  394.2 9.0 %copy-start.1 = (bf16[64,64,224]{2,1,0:T(8,128)(2,1)S(1)}, bf16[64,64,224]{2,1,0:T(8,128)(2,1)}, u32[]{:S(2)}) copy-start(bf16[64,64,224]{2,1,0:T(8,128)(2,1)} %param.10) | copy-start | bytes 5505028
  (3 other events, 5.2 us)
Sparse Core Ops, SparseCore 0:
  9.7 23.8 all-gather.5
  35.7 113.0 all-gather.3
  170.3 72.0 reduce-scatter.1
  245.0 112.7 all-gather.7

commit v2 on v1

--- a/solution.py
+++ b/solution.py
@@ -71,8 +71,8 @@
         partial_value.astype(jnp.bfloat16), "grp", scatter_dimension=0, tiled=True
     )
     quarter = quarter.reshape(group_count, tok_rows, quarter.shape[1])
-    quarter, rank_sum, hidden_cols, output_cols = lax.optimization_barrier(
-        (quarter, rank_sum, hidden_cols, output_cols)
+    quarter, hidden_cols, output_cols = lax.optimization_barrier(
+        (quarter, hidden_cols, output_cols)
     )
     chip_count = lax.axis_size("chip")
     row_of_chip = chip_count // group_count
@@ -114,8 +114,13 @@
         (all_positions >= all_starts[:, None, :]) & (all_positions < all_ends[:, None, :])
     ).astype(jnp.float32)
     weight_all = jnp.sum(tenant_table * weights[None, None, :], axis=2)
-    rank_all = lax.all_gather(
-        jnp.concatenate([grad_rank, act_rank], axis=1), SEQ, axis=0, tiled=True
+    rank_rows = jnp.concatenate([grad_rank, act_rank], axis=1)
+    rank_all = lax.all_to_all(
+        jnp.broadcast_to(rank_rows[None], (shard_count,) + rank_rows.shape),
+        SEQ,
+        split_axis=0,
+        concat_axis=0,
+        tiled=True,
     ).astype(jnp.float32).reshape(shard_count, tok_rows, 1, 2 * ranks)
     tenant_map = (
         tenant_table.reshape(shard_count * job_slots, tenant_total).astype(jnp.bfloat16)

time: 413 us -> 359 us (0.87)
  waiting for transfers between devices: 212 us -> 147 us
  blocking collectives: 15.8 us -> 31.5 us
  local copies, waits for them, and re-layouts: 85.1 us -> 76.9 us
    ppermute x4, waiting for transfers between devices: 71.8 us -> 41.6 us  [shards(): arrived.append(lax.ppermute(piece, ('grp', 'chip', 'core'), pairs))]
    reduce_scatter x1, waiting for transfers between devices: 26.3 us -> 4.54 us  [shards(): lax.psum_scatter(partial_value.astype(jnp.bfloat16), 'grp', scatter_dimen...]
    all_to_all x0 -> x1, blocking collectives: none -> 16.4 us  [shards(): lax.all_to_all(grad_output.reshape(tok_rows, shard_count, up_slab), SEQ,...]
    all_gather x1 -> x0, waiting for transfers between devices: 16.4 us -> none  [shards(): lax.all_gather(jnp.concatenate([grad_rank, act_rank], axis=1), SEQ, axis=...]
    mul x3 -> x1, local copies, waits for them, and re-layouts: 7.23 us -> 1.17 us  [adapter_grad(): spread = (member_all[:, :, :, None] * rank_rows).astype(jnp.bfloat16)]
    all_to_all x1, waiting for transfers between devices: 8.04 us -> 12.8 us  [shards(): lax.all_to_all(jnp.broadcast_to(rank_rows[None], (shard_count,) + rank_ro...]
    unnamed x38 -> x26, local copies, waits for them, and re-layouts: 18.1 us -> 17.4 us
  transfers between devices with their start and end apart: 12 -> 11, of which waited for: 11 -> 9; matrix products, arithmetic and copies ran while one was open for 15% -> 23% of each run, Pallas kernels for 0% -> 0%
where the time goes in v2:
time: 359 us; the launch traced here: 354 us
  waiting for transfers between devices  147 us (41%)
  local copies, waits for them, and re-layouts  76.9 us (21%)
  matrix products  41.7 us (12%)
  starting transfers between devices  37.4 us (10%)
  blocking collectives  31.5 us (9%)
  between operations  14.1 us (4%)
  other arithmetic  4.52 us (1%)
    all_to_all x1, waiting for transfers between devices, shards(): lax.all_to_all(adapter_down[chosen], SEQ, split_axis=1, concat_axis=3, ti...  50 us
    ppermute x4, waiting for transfers between devices, shards(): arrived.append(lax.ppermute(piece, ('grp', 'chip', 'core'), pairs))  41.6 us
    dot_general x1, matrix products, shards(): lax.dot_general(tokens_same_core, weight_pair, contract_last, preferred_e...  21.3 us
    all_to_all x1, waiting for transfers between devices, shards(): lax.all_to_all(hidden.reshape(tok_rows, shard_count, down_slab), SEQ, spl...  21 us
    unnamed x26, local copies, waits for them, and re-layouts  17.4 us
    all_to_all x1, blocking collectives, shards(): lax.all_to_all(grad_output.reshape(tok_rows, shard_count, up_slab), SEQ,...  16.4 us
    psum x1, blocking collectives, shards(): rank_sum = lax.psum(rank_part.astype(jnp.float32), 'grp')  15.1 us
    all_to_all x1, waiting for transfers between devices, shards(): lax.all_to_all(jnp.broadcast_to(rank_rows[None], (shard_count,) + rank_ro...  12.8 us
  transfers between devices with their start and end apart: 11, of which 9 were waited for; matrix products, arithmetic and copies ran while one was open for 23% of the time, Pallas kernels for 0%

profile of v2, /device:TPU:9, one launch (start us, length us, event | category | flops | bytes accessed | tf_op | source)
XLA Modules:
  0.0 353.5 jit_solution(15708552846607498993)
XLA Ops:
  14.1 4.6 %reshape.236 = bf16[32,2,8192]{2,1,0:T(2,128)(2,1)} reshape(bf16[32,4,64,64]{3,2,1,0:T(8,128)(2,1)} %bitcast.113) | data formatting | bytes 2097152
  18.7 8.9 %all-to-all-start = ((bf16[32,2,8192]{2,1,0:T(2,128)(2,1)}), bf16[32,2,8192]{2,1,0:T(2,128)(2,1)S(1)}, u32[]{:S(2)}, u32[]{:S(2)}) async-start(bf16[32,2,8192]{2,1,0:T(2,128)(2,1)} %reshape.236), calls=%async_computation | async-start | bytes 2097152 | tf_op jit(solution)/shard_map/all_to_all | solution.py:44
  30.4 4.7 %copy.72 = bf16[4,32,64,224]{3,2,0,1:T(8,128)(2,1)} copy(bf16[4,32,64,224]{3,2,1,0:T(8,128)(2,1)} %bitcast.109) | data formatting | bytes 7340032 | tf_op jit(solution)/shard_map/gather | solution.py:43
  35.2 7.6 %all-to-all-done = bf16[32,2,8192]{2,1,0:T(2,128)(2,1)S(1)} async-done(((bf16[32,2,8192]{2,1,0:T(2,128)(2,1)}), bf16[32,2,8192]{2,1,0:T(2,128)(2,1)S(1)}, u32[]{:S(2)}, u32[]{:S(2)}) %all-to-all-start) | async-done | bytes 1048608 | tf_op jit(solution)/shard_map/all_to_all | solution.py:44
  42.8 6.4 %all-to-all-start.1 = ((bf16[4,32,64,224]{3,2,0,1:T(8,128)(2,1)}), bf16[4,32,64,224]{3,2,0,1:T(8,128)(2,1)}, u32[]{:S(2)}, u32[]{:S(2)}) async-start(bf16[4,32,64,224]{3,2,0,1:T(8,128)(2,1)} %copy.72), calls=%async_computation.1 | async-start | bytes 8388608 | tf_op jit(solution)/shard_map/all_to_all | solution.py:43
  56.7 50.0 %all-to-all-done.1 = bf16[4,32,64,224]{3,2,0,1:T(8,128)(2,1)} async-done(((bf16[4,32,64,224]{3,2,0,1:T(8,128)(2,1)}), bf16[4,32,64,224]{3,2,0,1:T(8,128)(2,1)}, u32[]{:S(2)}, u32[]{:S(2)}) %all-to-all-start.1) | async-done | bytes 3670048 | tf_op jit(solution)/shard_map/all_to_all | solution.py:43
  106.7 6.6 %copy.73 = bf16[4,1,64,32,224]{4,3,2,0,1:T(8,128)(2,1)} copy(bf16[4,1,64,32,224]{4,2,0,3,1:T(8,128)(2,1)} %bitcast.12) | data formatting | bytes 7340032 | tf_op jit(solution)/shard_map/all_to_all | solution.py:43
  113.3 9.0 %reshape.191 = bf16[256,7168]{1,0:T(8,128)(2,1)} reshape(bf16[4,1,64,32,224]{4,3,2,0,1:T(8,128)(2,1)} %copy.73) | data formatting | bytes 7340032 | tf_op jit(solution)/shard_map/reshape | solution.py:46
  125.5 15.1 %psum.7 = bf16[128,128]{0,1:T(8,128)(2,1)S(1)} all-reduce(f32[128,128]{0,1:T(8,128)S(1)} %maximum_convert_fusion), channel_id=1, replica_groups=mesh['grp'=4,'chip'=16,'core'=2] {'grp'}, use_global_device_ids=true, to_apply=%region_3.4 | all-reduce | flops 16384 | bytes 98304 | tf_op jit(solution)/shard_map/psum | solution.py:63
  140.6 8.2 %all-gather.3.cloned.1.call-done = bf16[2048,2048]{1,0:T(8,128)(2,1)} async-done(((bf16[128,2048]{1,0:T(8,128)(2,1)}), bf16[2048,2048]{1,0:T(8,128)(2,1)}) %all-gather.3.cloned.1.call-update) | async-done | bytes 8388624 | tf_op jit(solution)/shard_map/all_gather | solution.py:62
  148.8 21.3 %convolution_convert_fusion = bf16[2048,1792]{1,0:T(8,128)(2,1)} fusion(bf16[2048,2048]{1,0:T(8,128)(2,1)} %all-gather.3.cloned.1.call-done, bf16[1792,2048]{1,0:T(8,128)(2,1)} %all-gather.5.cloned.1.call-done), kind=kOutput, calls=%fused_computation.7 | convolution fusion | flops 15036055552 | bytes 23068672 | tf_op jit(solution)/shard_map/dot_general | solution.py:67
  170.4 16.4 %all_to_all.65 = bf16[128,32,64]{0,2,1:T(8,128)(2,1)} all-to-all(bf16[128,32,64]{0,2,1:T(8,128)(2,1)S(1)} %bitcast.117), channel_id=1, replica_groups=mesh['grp'=4,'chip'=16,'core'=2] {'chip','core'}, dimensions={1} | all-to-all | bytes 1048576 | tf_op jit(solution)/shard_map/all_to_all | solution.py:38
  188.0 4.9 %all-to-all-start.4 = ((bf16[32,128,128]{1,2,0:T(8,128)(2,1)}), bf16[32,128,128]{1,2,0:T(8,128)(2,1)S(1)}, u32[]{:S(2)}, u32[]{:S(2)}) async-start(bf16[32,128,128]{1,2,0:T(8,128)(2,1)} %broadcast_in_dim.17), calls=%async_computation.5 | async-start | bytes 2097152 | tf_op jit(solution)/shard_map/all_to_all | solution.py:118
  195.3 12.8 %all-to-all-done.4 = bf16[32,128,128]{1,2,0:T(8,128)(2,1)S(1)} async-done(((bf16[32,128,128]{1,2,0:T(8,128)(2,1)}), bf16[32,128,128]{1,2,0:T(8,128)(2,1)S(1)}, u32[]{:S(2)}, u32[]{:S(2)}) %all-to-all-start.4) | async-done | bytes 1048608 | tf_op jit(solution)/shard_map/all_to_all | solution.py:118
  208.1 6.2 %all-to-all-start.2 = ((bf16[128,32,224]{0,2,1:T(8,128)(2,1)}), bf16[128,32,224]{0,2,1:T(8,128)(2,1)}, u32[]{:S(2)}, u32[]{:S(2)}) async-start(bf16[128,32,224]{0,2,1:T(8,128)(2,1)} %bitcast.16), calls=%async_computation.3 | async-start | bytes 3670016 | tf_op jit(solution)/shard_map/all_to_all | solution.py:35
  216.8 21.0 %all-to-all-done.2 = bf16[128,32,224]{0,2,1:T(8,128)(2,1)} async-done(((bf16[128,32,224]{0,2,1:T(8,128)(2,1)}), bf16[128,32,224]{0,2,1:T(8,128)(2,1)}, u32[]{:S(2)}, u32[]{:S(2)}) %all-to-all-start.2) | async-done | bytes 1835040 | tf_op jit(solution)/shard_map/all_to_all | solution.py:35
  237.9 4.5 %reduce-scatter.2.cloned.1.call-done = bf16[512,1792]{1,0:T(8,128)(2,1)} async-done(((bf16[2048,1792]{1,0:T(8,128)(2,1)}), bf16[512,1792]{1,0:T(8,128)(2,1)}) %reduce-scatter.2.cloned.1.call-update) | async-done | bytes 1835024 | tf_op jit(solution)/shard_map/reduce_scatter | solution.py:70
  264.1 4.8 %multiply_convert_fusion = bf16[32,4,64,224]{3,2,1,0:T(8,128)(2,1)} fusion(f32[32,4]{1,0:T(8,128)S(1)} %copy.80, f32[32,128,64]{1,2,0:T(8,128)S(1)} %get-tuple-element.33, f32[32,128,4]{1,2,0:T(4,128)S(1)} %fusion.9, bf16[32,128,224]{1,2,0:T(8,128)(2,1)} %bitcast.19), kind=kOutput, calls=%fused_computation.6 | convolution fusion | flops 475529216 | bytes 6619648 | tf_op jit(solution)/shard_map/stjr,stc->sjrc/dot_general | solution.py:131
  272.5 8.5 %reshape.200 = bf16[128,14336]{1,0:T(8,128)(2,1)} reshape(bf16[32,4,64,224]{3,2,1,0:T(8,128)(2,1)} %multiply_convert_fusion) | data formatting | bytes 7340032 | tf_op jit(solution)/shard_map/reshape | solution.py:138
  281.1 6.0 %copy.81 = bf16[14336,128]{1,0:T(8,128)(2,1)} copy(bf16[14336,128]{0,1:T(8,128)(2,1)} %bitcast.112) | data formatting | bytes 7340032 | tf_op jit(solution)/shard_map/dot_general | solution.py:136
  291.5 4.5 %copy.84 = f32[64,64,224]{2,1,0:T(8,128)} copy(f32[64,64,224]{2,0,1:T(8,128)S(1)} %fusion.13) | data formatting | bytes 7340032
  296.0 9.1 %collective-permute-done.1 = bf16[128,1792]{1,0:T(8,128)(2,1)} collective-permute-done((bf16[128,1792]{1,0:T(8,128)(2,1)}, bf16[128,1792]{1,0:T(8,128)(2,1)}, u32[]{:S(2)}, u32[]{:S(2)}) %collective-permute-start.1) | collective-permute-done | bytes 458784 | tf_op jit(solution)/shard_map/ppermute | solution.py:94
  305.1 24.3 %collective-permute-done.2 = bf16[128,1792]{1,0:T(8,128)(2,1)} collective-permute-done((bf16[128,1792]{1,0:T(8,128)(2,1)}, bf16[128,1792]{1,0:T(8,128)(2,1)}, u32[]{:S(2)}, u32[]{:S(2)}) %collective-permute-start.2) | collective-permute-done | bytes 458784 | tf_op jit(solution)/shard_map/ppermute | solution.py:94
  329.3 8.2 %collective-permute-done.3 = bf16[128,1792]{1,0:T(8,128)(2,1)} collective-permute-done((bf16[128,1792]{1,0:T(8,128)(2,1)}, bf16[128,1792]{1,0:T(8,128)(2,1)}, u32[]{:S(2)}, u32[]{:S(2)}) %collective-permute-start.3) | collective-permute-done | bytes 458784 | tf_op jit(solution)/shard_map/ppermute | solution.py:94
  (83 shorter events, 65.5 us)
Async XLA Ops:
  7.2 20.4 %copy-start = (bf16[64,64,224]{2,1,0:T(8,128)(2,1)S(1)}, bf16[64,64,224]{2,1,0:T(8,128)(2,1)}, u32[]{:S(2)}) copy-start(bf16[64,64,224]{2,1,0:T(8,128)(2,1)} %param.10) | copy-start | bytes 5505028
  7.2 1.5 copy-start.7
  7.2 1.6 copy-start.6
  7.2 133.4 %all-gather.5.cloned.1.call-start = ((), (), s32[]{:S(2)}) async-start(), calls=%async_computation.7 | async-start | bytes 11010048 | tf_op jit(solution)/shard_map/all_gather | solution.py:61
  7.9 140.9 %all-gather.3.cloned.1.call-start = ((), (), s32[]{:S(2)}) async-start(), calls=%async_computation.6 | async-start | bytes 8912896 | tf_op jit(solution)/shard_map/all_gather | solution.py:62
  18.7 24.1 %all-to-all-start = ((bf16[32,2,8192]{2,1,0:T(2,128)(2,1)}), bf16[32,2,8192]{2,1,0:T(2,128)(2,1)S(1)}, u32[]{:S(2)}, u32[]{:S(2)}) async-start(bf16[32,2,8192]{2,1,0:T(2,128)(2,1)} %reshape.236), calls=%async_computation | async-start | bytes 2097152 | tf_op jit(solution)/shard_map/all_to_all | solution.py:44
  35.2 14.0 %copy-start.8 = (s32[32,4]{0,1:T(4,128)S(1)}, s32[32,4]{0,1:T(4,128)}, u32[]{:S(2)}) copy-start(s32[32,4]{0,1:T(4,128)} %param.13) | copy-start | bytes 1540
  42.8 63.9 %all-to-all-start.1 = ((bf16[4,32,64,224]{3,2,0,1:T(8,128)(2,1)}), bf16[4,32,64,224]{3,2,0,1:T(8,128)(2,1)}, u32[]{:S(2)}, u32[]{:S(2)}) async-start(bf16[4,32,64,224]{3,2,0,1:T(8,128)(2,1)} %copy.72), calls=%async_computation.1 | async-start | bytes 8388608 | tf_op jit(solution)/shard_map/all_to_all | solution.py:43
  49.2 193.2 %reduce-scatter.2.cloned.1.call-start = ((), (), s32[]{:S(2)}) async-start(), calls=%async_computation.8 | async-start | bytes 9175040 | tf_op jit(solution)/shard_map/reduce_scatter | solution.py:70
  51.2 3.8 %copy-start.4 = (bf16[128,2048]{1,0:T(8,128)(2,1)S(1)}, bf16[128,2048]{1,0:T(8,128)(2,1)}, u32[]{:S(2)}) copy-start(bf16[128,2048]{1,0:T(8,128)(2,1)} %param.7) | copy-start | bytes 1572868
  113.3 9.0 %copy-start.3 = (bf16[128,7168]{1,0:T(8,128)(2,1)S(1)}, bf16[128,7168]{1,0:T(8,128)(2,1)}, u32[]{:S(2)}) copy-start(bf16[128,7168]{1,0:T(8,128)(2,1)} %param.8) | copy-start | bytes 5505028
  188.0 20.1 %all-to-all-start.4 = ((bf16[32,128,128]{1,2,0:T(8,128)(2,1)}), bf16[32,128,128]{1,2,0:T(8,128)(2,1)S(1)}, u32[]{:S(2)}, u32[]{:S(2)}) async-start(bf16[32,128,128]{1,2,0:T(8,128)(2,1)} %broadcast_in_dim.17), calls=%async_computation.5 | async-start | bytes 2097152 | tf_op jit(solution)/shard_map/all_to_all | solution.py:118
  208.1 29.7 %all-to-all-start.2 = ((bf16[128,32,224]{0,2,1:T(8,128)(2,1)}), bf16[128,32,224]{0,2,1:T(8,128)(2,1)}, u32[]{:S(2)}, u32[]{:S(2)}) async-start(bf16[128,32,224]{0,2,1:T(8,128)(2,1)} %bitcast.16), calls=%async_computation.3 | async-start | bytes 3670016 | tf_op jit(solution)/shard_map/all_to_all | solution.py:35
  253.1 15.7 %copy-start.5 = (bf16[4096,128]{1,0:T(8,128)(2,1)S(1)}, bf16[4096,128]{1,0:T(8,128)(2,1)}, u32[]{:S(2)}) copy-start(bf16[4096,128]{1,0:T(8,128)(2,1)} %copy.83) | copy-start | bytes 3145732
  253.1 42.8 %collective-permute-start = (bf16[128,1792]{1,0:T(8,128)(2,1)}, bf16[128,1792]{1,0:T(8,128)(2,1)}, u32[]{:S(2)}, u32[]{:S(2)}) collective-permute-start(bf16[128,1792]{1,0:T(8,128)(2,1)} %get-tuple-element.34), channel_id=1, source_target_pairs={{0,0},{1,1},{2,2},{3,3},{4,4},{5,5},{6,6},{7,7},{8,32},{9,33},{10,... | collective-permute-start | bytes 1376264 | tf_op jit(solution)/shard_map/ppermute | solution.py:94
  255.2 49.9 %collective-permute-start.1 = (bf16[128,1792]{1,0:T(8,128)(2,1)}, bf16[128,1792]{1,0:T(8,128)(2,1)}, u32[]{:S(2)}, u32[]{:S(2)}) collective-permute-start(bf16[128,1792]{1,0:T(8,128)(2,1)} %get-tuple-element.37), channel_id=1, source_target_pairs={{0,2},{1,3},{2,4},{3,5},{4,6},{5,7},{6,0},{7,1},{8,34},{9,35},{10,... | collective-permute-start | bytes 1376264 | tf_op jit(solution)/shard_map/ppermute | solution.py:94
  258.6 70.7 %collective-permute-start.2 = (bf16[128,1792]{1,0:T(8,128)(2,1)}, bf16[128,1792]{1,0:T(8,128)(2,1)}, u32[]{:S(2)}, u32[]{:S(2)}) collective-permute-start(bf16[128,1792]{1,0:T(8,128)(2,1)} %get-tuple-element.36), channel_id=1, source_target_pairs={{0,4},{1,5},{2,6},{3,7},{4,0},{5,1},{6,2},{7,3},{8,36},{9,37},{10,... | collective-permute-start | bytes 1376264 | tf_op jit(solution)/shard_map/ppermute | solution.py:94
  260.9 76.7 %collective-permute-start.3 = (bf16[128,1792]{1,0:T(8,128)(2,1)}, bf16[128,1792]{1,0:T(8,128)(2,1)}, u32[]{:S(2)}, u32[]{:S(2)}) collective-permute-start(bf16[128,1792]{1,0:T(8,128)(2,1)} %get-tuple-element.35), channel_id=1, source_target_pairs={{0,6},{1,7},{2,0},{3,1},{4,2},{5,3},{6,4},{7,5},{8,38},{9,39},{10,... | collective-permute-start | bytes 1376264 | tf_op jit(solution)/shard_map/ppermute | solution.py:94
  343.0 2.0 copy-start.2
  343.4 3.6 %copy-start.1 = (bf16[64,64,224]{2,1,0:T(8,128)(2,1)S(1)}, bf16[64,64,224]{2,1,0:T(8,128)(2,1)}, u32[]{:S(2)}) copy-start(bf16[64,64,224]{2,1,0:T(8,128)(2,1)} %param.10) | copy-start | bytes 5505028
Sparse Core Ops, SparseCore 0:
  9.7 23.8 all-gather.4
  35.7 113.0 all-gather.2
  170.2 72.1 reduce-scatter.1

commit v3 on v2

--- a/solution.py
+++ b/solution.py
@@ -39,9 +39,13 @@
         grad_output.reshape(tok_rows, shard_count, up_slab), SEQ, split_axis=1, concat_axis=0, tiled=True
     ).reshape(shard_count, tok_rows, up_slab)
     chosen = job_tenant.T
+    tokens_same_core = lax.all_gather(grad_output, "chip", axis=0, tiled=True)
+    down_picked, up_picked, tokens_same_core = lax.optimization_barrier(
+        (adapter_down[chosen], adapter_up[chosen], tokens_same_core)
+    )
     fetched_down, fetched_up = (
-        lax.all_to_all(adapter_down[chosen], SEQ, split_axis=1, concat_axis=3, tiled=True),
-        lax.all_to_all(adapter_up[chosen], SEQ, split_axis=1, concat_axis=3, tiled=True),
+        lax.all_to_all(down_picked, SEQ, split_axis=1, concat_axis=3, tiled=True),
+        lax.all_to_all(up_picked, SEQ, split_axis=1, concat_axis=3, tiled=True),
     )
     down_stack = fetched_down.reshape(job_slots * ranks, shard_count * down_slab)
     up_stack = fetched_up.reshape(job_slots * ranks, shard_count * up_slab)
@@ -58,12 +62,16 @@
     rank_part = jnp.concatenate([select_jobs(grad_proj), select_jobs(act_proj)], axis=1).astype(
         jnp.bfloat16
     )
-    weight_pair = lax.all_gather(down_weight, "core", axis=0, tiled=True)
-    tokens_same_core = lax.all_gather(grad_output, "chip", axis=0, tiled=True)
+    partner_weight = lax.ppermute(down_weight, "core", [(0, 1), (1, 0)])
+    on_first_core = lax.axis_index("core") == 0
+    weight_pair = jnp.concatenate(
+        [
+            jnp.where(on_first_core, down_weight, partner_weight),
+            jnp.where(on_first_core, partner_weight, down_weight),
+        ],
+        axis=0,
+    )
     rank_sum = lax.psum(rank_part.astype(jnp.float32), "grp")
-    tokens_same_core, weight_pair, rank_sum = lax.optimization_barrier(
-        (tokens_same_core, weight_pair, rank_sum)
-    )
     partial_value = lax.dot_general(
         tokens_same_core, weight_pair, contract_last, preferred_element_type=jnp.float32
     )

time: 359 us -> 395 us (1.10)
  waiting for transfers between devices: 147 us -> 182 us
  blocking collectives: 31.5 us -> 13.7 us
  starting transfers between devices: 37.4 us -> 50.6 us
  other arithmetic: 4.52 us -> 11.8 us
    all_gather x1, waiting for transfers between devices: 8.24 us -> 61.7 us  [shards(): tokens_same_core = lax.all_gather(grad_output, 'chip', axis=0, tiled=True)]
    all_to_all x1 -> x0, blocking collectives: 16.4 us -> none  [shards(): lax.all_to_all(grad_output.reshape(tok_rows, shard_count, up_slab), SEQ,...]
    all_to_all x2 -> x3, waiting for transfers between devices: 57.6 us -> 49 us  [the longest x1 38.6 us: shards(): lax.all_to_all(down_picked, SEQ, split_axis=1, concat_axis=3, tiled=True)]
    select_n x1 -> x2, other arithmetic: 0.01 us -> 7.29 us  [the longest x1 6.6 us: shards(): jnp.where(on_first_core, down_weight, partner_weight)]
    all_to_all x2 -> x3, starting transfers between devices: 15.2 us -> 22.5 us  [the longest x1 9.92 us: shards(): lax.all_to_all(grad_output.reshape(tok_rows, shard_count, up_slab), SEQ,...]
    ppermute x4, waiting for transfers between devices: 41.6 us -> 34.8 us  [shards(): arrived.append(lax.ppermute(piece, ('grp', 'chip', 'core'), pairs))]
    optimization_barrier x0 -> x2, local copies, waits for them, and re-layouts: none -> 6.3 us  [shards(): lax.optimization_barrier((adapter_down[chosen], adapter_up[chosen], token...]
    all_to_all x1, starting transfers between devices: 4.91 us -> 11.1 us  [shards(): lax.all_to_all(jnp.broadcast_to(rank_rows[None], (shard_count,) + rank_ro...]
  transfers between devices with their start and end apart: 11 -> 12, of which waited for: 9 -> 9; matrix products, arithmetic and copies ran while one was open for 23% -> 25% of each run, Pallas kernels for 0% -> 0%
where the time goes in v3:
time: 395 us; the launch traced here: 391 us
  waiting for transfers between devices  182 us (46%)
  local copies, waits for them, and re-layouts  78.3 us (20%)
  starting transfers between devices  50.6 us (13%)
  matrix products  40.5 us (10%)
  between operations  14.5 us (4%)
  blocking collectives  13.7 us (3%)
  other arithmetic  11.8 us (3%)
    all_gather x1, waiting for transfers between devices, shards(): tokens_same_core = lax.all_gather(grad_output, 'chip', axis=0, tiled=True)  61.7 us
    all_to_all x1, waiting for transfers between devices, shards(): lax.all_to_all(down_picked, SEQ, split_axis=1, concat_axis=3, tiled=True)  38.6 us
    ppermute x4, waiting for transfers between devices, shards(): arrived.append(lax.ppermute(piece, ('grp', 'chip', 'core'), pairs))  34.8 us
    unnamed x34, local copies, waits for them, and re-layouts  21.5 us
    dot_general x1, matrix products, shards(): lax.dot_general(tokens_same_core, weight_pair, contract_last, preferred_e...  21.3 us
    all_to_all x1, waiting for transfers between devices, shards(): lax.all_to_all(hidden.reshape(tok_rows, shard_count, down_slab), SEQ, spl...  21 us
    psum x1, blocking collectives, shards(): rank_sum = lax.psum(rank_part.astype(jnp.float32), 'grp')  13.7 us
    all_to_all x1, waiting for transfers between devices, shards(): lax.all_to_all(jnp.broadcast_to(rank_rows[None], (shard_count,) + rank_ro...  12.8 us
  transfers between devices with their start and end apart: 12, of which 9 were waited for; matrix products, arithmetic and copies ran while one was open for 25% of the time, Pallas kernels for 0%

profile of v3, /device:TPU:9, one launch (start us, length us, event | category | flops | bytes accessed | tf_op | source)
XLA Modules:
  0.0 391.1 jit_solution(7845690695208656709)
XLA Ops:
  15.1 6.6 %broadcast_select_fusion.1 = (bf16[896,2048]{1,0:T(8,128)(2,1)}, bf16[896,2048]{1,0:T(8,128)(2,1)}) fusion(bf16[896,2048]{1,0:T(8,128)(2,1)} %param.9, bf16[896,2048]{1,0:T(8,128)(2,1)} %collective-permute-done, pred[]{:T(512)S(6)} %eq.33), kind=kLoop, calls=%fused_computation.16 | loop fusion | flops 3670016 | bytes 14680065 | tf_op jit(solution)/shard_map/jit(_where)/select_n | solution.py:69
  21.7 61.7 %all-gather.2.cloned.1.call-done = bf16[2048,2048]{1,0:T(8,128)(2,1)} async-done(((bf16[128,2048]{1,0:T(8,128)(2,1)}), bf16[2048,2048]{1,0:T(8,128)(2,1)}) %all-gather.2.cloned.1.call-update) | async-done | bytes 8388624 | tf_op jit(solution)/shard_map/all_gather | solution.py:42
  83.4 21.3 %convolution_convert_fusion = bf16[2048,1792]{1,0:T(8,128)(2,1)} fusion(bf16[2048,2048]{1,0:T(8,128)(2,1)} %all-gather.2.cloned.1.call-done, bf16[896,2048]{1,0:T(8,128)(2,1)} %get-tuple-element.33, bf16[896,2048]{1,0:T(8,128)(2,1)} %get-tuple-element.32), kind=kOutput, calls=%fused_computation.7 | convolution fusion | flops 15050735616 | bytes 23068672 | tf_op jit(solution)/shard_map/dot_general | solution.py:75
  106.2 4.6 %reshape.236 = bf16[32,2,8192]{2,1,0:T(2,128)(2,1)} reshape(bf16[32,4,64,64]{3,2,1,0:T(8,128)(2,1)} %bitcast.113) | data formatting | bytes 2097152
  110.9 6.2 %all-to-all-start.2 = ((bf16[32,2,8192]{2,1,0:T(2,128)(2,1)}), bf16[32,2,8192]{2,1,0:T(2,128)(2,1)S(1)}, u32[]{:S(2)}, u32[]{:S(2)}) async-start(bf16[32,2,8192]{2,1,0:T(2,128)(2,1)} %reshape.236), calls=%async_computation.3 | async-start | bytes 2097152 | tf_op jit(solution)/shard_map/all_to_all | solution.py:48
  117.1 4.7 %copy.75 = bf16[4,32,64,224]{3,2,0,1:T(8,128)(2,1)} copy(bf16[4,32,64,224]{3,2,1,0:T(8,128)(2,1)} %bitcast.108) | data formatting | bytes 7340032 | tf_op jit(solution)/shard_map/optimization_barrier | solution.py:43
  121.8 10.4 %all-to-all-done.2 = bf16[32,2,8192]{2,1,0:T(2,128)(2,1)S(1)} async-done(((bf16[32,2,8192]{2,1,0:T(2,128)(2,1)}), bf16[32,2,8192]{2,1,0:T(2,128)(2,1)S(1)}, u32[]{:S(2)}, u32[]{:S(2)}) %all-to-all-start.2) | async-done | bytes 1048608 | tf_op jit(solution)/shard_map/all_to_all | solution.py:48
  133.2 6.4 %all-to-all-start.3 = ((bf16[4,32,64,224]{3,2,0,1:T(8,128)(2,1)}), bf16[4,32,64,224]{3,2,0,1:T(8,128)(2,1)}, u32[]{:S(2)}, u32[]{:S(2)}) async-start(bf16[4,32,64,224]{3,2,0,1:T(8,128)(2,1)} %copy.75), calls=%async_computation.4 | async-start | bytes 8388608 | tf_op jit(solution)/shard_map/all_to_all | solution.py:47
  150.5 38.6 %all-to-all-done.3 = bf16[4,32,64,224]{3,2,0,1:T(8,128)(2,1)} async-done(((bf16[4,32,64,224]{3,2,0,1:T(8,128)(2,1)}), bf16[4,32,64,224]{3,2,0,1:T(8,128)(2,1)}, u32[]{:S(2)}, u32[]{:S(2)}) %all-to-all-start.3) | async-done | bytes 3670048 | tf_op jit(solution)/shard_map/all_to_all | solution.py:47
  189.0 9.9 %all-to-all-start.1 = ((bf16[128,32,64]{0,2,1:T(8,128)(2,1)}), bf16[128,32,64]{0,2,1:T(8,128)(2,1)S(1)}, u32[]{:S(2)}, u32[]{:S(2)}) async-start(bf16[128,32,64]{0,2,1:T(8,128)(2,1)} %bitcast.8), calls=%async_computation.2 | async-start | bytes 1048576 | tf_op jit(solution)/shard_map/all_to_all | solution.py:38
  199.0 6.6 %copy.76 = bf16[4,1,64,32,224]{4,3,2,0,1:T(8,128)(2,1)} copy(bf16[4,1,64,32,224]{4,2,0,3,1:T(8,128)(2,1)} %bitcast.31) | data formatting | bytes 7340032 | tf_op jit(solution)/shard_map/all_to_all | solution.py:47
  205.6 8.9 %reshape.196 = bf16[256,7168]{1,0:T(8,128)(2,1)} reshape(bf16[4,1,64,32,224]{4,3,2,0,1:T(8,128)(2,1)} %copy.76) | data formatting | bytes 7340032 | tf_op jit(solution)/shard_map/reshape | solution.py:50
  217.7 13.7 %psum.7 = bf16[128,128]{0,1:T(8,128)(2,1)S(1)} all-reduce(f32[128,128]{0,1:T(8,128)S(1)} %maximum_convert_fusion), channel_id=1, replica_groups=mesh['grp'=4,'chip'=16,'core'=2] {'grp'}, use_global_device_ids=true, to_apply=%region_4.5 | all-reduce | flops 16384 | bytes 98304 | tf_op jit(solution)/shard_map/psum | solution.py:74
  232.7 11.1 %all-to-all-start.4 = ((bf16[32,128,128]{1,2,0:T(8,128)(2,1)}), bf16[32,128,128]{1,2,0:T(8,128)(2,1)S(1)}, u32[]{:S(2)}, u32[]{:S(2)}) async-start(bf16[32,128,128]{1,2,0:T(8,128)(2,1)} %broadcast_in_dim.17), calls=%async_computation.5 | async-start | bytes 2097152 | tf_op jit(solution)/shard_map/all_to_all | solution.py:126
  246.2 12.8 %all-to-all-done.4 = bf16[32,128,128]{1,2,0:T(8,128)(2,1)S(1)} async-done(((bf16[32,128,128]{1,2,0:T(8,128)(2,1)}), bf16[32,128,128]{1,2,0:T(8,128)(2,1)S(1)}, u32[]{:S(2)}, u32[]{:S(2)}) %all-to-all-start.4) | async-done | bytes 1048608 | tf_op jit(solution)/shard_map/all_to_all | solution.py:126
  259.0 6.2 %all-to-all-start = ((bf16[128,32,224]{0,2,1:T(8,128)(2,1)}), bf16[128,32,224]{0,2,1:T(8,128)(2,1)}, u32[]{:S(2)}, u32[]{:S(2)}) async-start(bf16[128,32,224]{0,2,1:T(8,128)(2,1)} %bitcast.4), calls=%async_computation.1 | async-start | bytes 3670016 | tf_op jit(solution)/shard_map/all_to_all | solution.py:35
  267.7 21.0 %all-to-all-done = bf16[128,32,224]{0,2,1:T(8,128)(2,1)} async-done(((bf16[128,32,224]{0,2,1:T(8,128)(2,1)}), bf16[128,32,224]{0,2,1:T(8,128)(2,1)}, u32[]{:S(2)}, u32[]{:S(2)}) %all-to-all-start) | async-done | bytes 1835040 | tf_op jit(solution)/shard_map/all_to_all | solution.py:35
  308.0 4.9 %multiply_convert_fusion = bf16[32,4,64,224]{3,2,1,0:T(8,128)(2,1)} fusion(f32[32,4]{1,0:T(8,128)S(1)} %copy.80, f32[32,128,64]{1,2,0:T(8,128)S(1)} %get-tuple-element.35, f32[32,128,4]{1,2,0:T(4,128)S(1)} %fusion.12, bf16[32,128,224]{1,2,0:T(8,128)(2,1)} %bitcast.7), kind=kOutput, calls=%fused_computation.6 | convolution fusion | flops 475529216 | bytes 6619648 | tf_op jit(solution)/shard_map/stjr,stc->sjrc/dot_general | solution.py:139
  316.6 8.5 %reshape.200 = bf16[128,14336]{1,0:T(8,128)(2,1)} reshape(bf16[32,4,64,224]{3,2,1,0:T(8,128)(2,1)} %multiply_convert_fusion) | data formatting | bytes 7340032 | tf_op jit(solution)/shard_map/reshape | solution.py:146
  325.1 6.0 %copy.81 = bf16[14336,128]{1,0:T(8,128)(2,1)} copy(bf16[14336,128]{0,1:T(8,128)(2,1)} %bitcast.111) | data formatting | bytes 7340032 | tf_op jit(solution)/shard_map/dot_general | solution.py:144
  331.2 4.4 %fusion.16 = f32[64,64,224]{2,0,1:T(8,128)S(1)} fusion(bf16[64,224,128]{2,1,0:T(8,128)(2,1)} %bitcast.110, s32[128]{0:T(128)S(1)} %eq.34), kind=kOutput, calls=%fused_computation.46 | convolution fusion | flops 234905600 | bytes 7340544 | tf_op jit(solution)/shard_map/dot_general | solution.py:144
  335.6 4.4 %copy.84 = f32[64,64,224]{2,1,0:T(8,128)} copy(f32[64,64,224]{2,0,1:T(8,128)S(1)} %fusion.16) | data formatting | bytes 7340032
  344.1 22.1 %collective-permute-done.3 = bf16[128,1792]{1,0:T(8,128)(2,1)} collective-permute-done((bf16[128,1792]{1,0:T(8,128)(2,1)}, bf16[128,1792]{1,0:T(8,128)(2,1)}, u32[]{:S(2)}, u32[]{:S(2)}) %collective-permute-start.3) | collective-permute-done | bytes 458784 | tf_op jit(solution)/shard_map/ppermute | solution.py:102
  366.1 8.7 %collective-permute-done.4 = bf16[128,1792]{1,0:T(8,128)(2,1)} collective-permute-done((bf16[128,1792]{1,0:T(8,128)(2,1)}, bf16[128,1792]{1,0:T(8,128)(2,1)}, u32[]{:S(2)}, u32[]{:S(2)}) %collective-permute-start.4) | collective-permute-done | bytes 458784 | tf_op jit(solution)/shard_map/ppermute | solution.py:102
  (92 shorter events, 66.7 us)
Async XLA Ops:
  7.2 2.3 copy-start
  7.2 76.2 %all-gather.2.cloned.1.call-start = ((), (), s32[]{:S(2)}) async-start(), calls=%async_computation.6 | async-start | bytes 8912896 | tf_op jit(solution)/shard_map/all_gather | solution.py:42
  7.9 280.8 %reduce-scatter.2.cloned.1.call-start = ((), (), s32[]{:S(2)}) async-start(), calls=%async_computation.7 | async-start | bytes 9175040 | tf_op jit(solution)/shard_map/reduce_scatter | solution.py:78
  8.0 7.1 %collective-permute-start = (bf16[896,2048]{1,0:T(8,128)(2,1)}, bf16[896,2048]{1,0:T(8,128)(2,1)}, u32[]{:S(2)}, u32[]{:S(2)}) collective-permute-start(bf16[896,2048]{1,0:T(8,128)(2,1)} %param.9), channel_id=1, source_target_pairs={{0,1},{1,0},{2,3},{3,2},{4,5},{5,4},{6,7},{7,6},{8,9},{9,8},{10,11... | collective-permute-start | bytes 11010056 | tf_op jit(solution)/shard_map/ppermute | solution.py:65
  9.5 2.8 copy-start.7
  110.9 21.4 %all-to-all-start.2 = ((bf16[32,2,8192]{2,1,0:T(2,128)(2,1)}), bf16[32,2,8192]{2,1,0:T(2,128)(2,1)S(1)}, u32[]{:S(2)}, u32[]{:S(2)}) async-start(bf16[32,2,8192]{2,1,0:T(2,128)(2,1)} %reshape.236), calls=%async_computation.3 | async-start | bytes 2097152 | tf_op jit(solution)/shard_map/all_to_all | solution.py:48
  121.8 17.8 %copy-start.4 = (bf16[128,2048]{1,0:T(8,128)(2,1)S(1)}, bf16[128,2048]{1,0:T(8,128)(2,1)}, u32[]{:S(2)}) copy-start(bf16[128,2048]{1,0:T(8,128)(2,1)} %param.7) | copy-start | bytes 1572868
  121.8 18.8 %copy-start.12 = (s32[32,4]{0,1:T(4,128)S(1)}, s32[32,4]{0,1:T(4,128)}, u32[]{:S(2)}) copy-start(s32[32,4]{0,1:T(4,128)} %param.13) | copy-start | bytes 1540
  133.2 55.8 %all-to-all-start.3 = ((bf16[4,32,64,224]{3,2,0,1:T(8,128)(2,1)}), bf16[4,32,64,224]{3,2,0,1:T(8,128)(2,1)}, u32[]{:S(2)}, u32[]{:S(2)}) async-start(bf16[4,32,64,224]{3,2,0,1:T(8,128)(2,1)} %copy.75), calls=%async_computation.4 | async-start | bytes 8388608 | tf_op jit(solution)/shard_map/all_to_all | solution.py:47
  189.0 42.4 %all-to-all-start.1 = ((bf16[128,32,64]{0,2,1:T(8,128)(2,1)}), bf16[128,32,64]{0,2,1:T(8,128)(2,1)S(1)}, u32[]{:S(2)}, u32[]{:S(2)}) async-start(bf16[128,32,64]{0,2,1:T(8,128)(2,1)} %bitcast.8), calls=%async_computation.2 | async-start | bytes 1048576 | tf_op jit(solution)/shard_map/all_to_all | solution.py:38
  205.6 8.9 %copy-start.3 = (bf16[128,7168]{1,0:T(8,128)(2,1)S(1)}, bf16[128,7168]{1,0:T(8,128)(2,1)}, u32[]{:S(2)}) copy-start(bf16[128,7168]{1,0:T(8,128)(2,1)} %param.8) | copy-start | bytes 5505028
  231.4 1.2 copy-start.9
  232.7 26.3 %all-to-all-start.4 = ((bf16[32,128,128]{1,2,0:T(8,128)(2,1)}), bf16[32,128,128]{1,2,0:T(8,128)(2,1)S(1)}, u32[]{:S(2)}, u32[]{:S(2)}) async-start(bf16[32,128,128]{1,2,0:T(8,128)(2,1)} %broadcast_in_dim.17), calls=%async_computation.5 | async-start | bytes 2097152 | tf_op jit(solution)/shard_map/all_to_all | solution.py:126
  243.8 21.4 %copy-start.11 = (s32[32,4]{0,1:T(4,128)S(1)}, s32[32,4]{0,1:T(4,128)}, u32[]{:S(2)}) copy-start(s32[32,4]{0,1:T(4,128)} %param.12) | copy-start | bytes 1540
  259.0 29.7 %all-to-all-start = ((bf16[128,32,224]{0,2,1:T(8,128)(2,1)}), bf16[128,32,224]{0,2,1:T(8,128)(2,1)}, u32[]{:S(2)}, u32[]{:S(2)}) async-start(bf16[128,32,224]{0,2,1:T(8,128)(2,1)} %bitcast.4), calls=%async_computation.1 | async-start | bytes 3670016 | tf_op jit(solution)/shard_map/all_to_all | solution.py:35
  267.7 33.7 %copy-start.8 = (f32[32,128,64]{1,2,0:T(8,128)S(1)}, f32[32,128,64]{1,2,0:T(8,128)}, u32[]{:S(2)}) copy-start(f32[32,128,64]{1,2,0:T(8,128)} %get-tuple-element.34) | copy-start | bytes 3145732
  267.7 33.7 %copy-start.10 = (bf16[128,32,64]{0,2,1:T(8,128)(2,1)S(1)}, bf16[128,32,64]{0,2,1:T(8,128)(2,1)}, u32[]{:S(2)}) copy-start(bf16[128,32,64]{0,2,1:T(8,128)(2,1)} %copy-done.9) | copy-start | bytes 1572868
  291.4 48.6 %collective-permute-start.1 = (bf16[128,1792]{1,0:T(8,128)(2,1)}, bf16[128,1792]{1,0:T(8,128)(2,1)}, u32[]{:S(2)}, u32[]{:S(2)}) collective-permute-start(bf16[128,1792]{1,0:T(8,128)(2,1)} %get-tuple-element.36), channel_id=1, source_target_pairs={{0,0},{1,1},{2,2},{3,3},{4,4},{5,5},{6,6},{7,7},{8,32},{9,33},{10,... | collective-permute-start | bytes 1376264 | tf_op jit(solution)/shard_map/ppermute | solution.py:102
  293.7 50.3 %collective-permute-start.2 = (bf16[128,1792]{1,0:T(8,128)(2,1)}, bf16[128,1792]{1,0:T(8,128)(2,1)}, u32[]{:S(2)}, u32[]{:S(2)}) collective-permute-start(bf16[128,1792]{1,0:T(8,128)(2,1)} %get-tuple-element.39), channel_id=1, source_target_pairs={{0,2},{1,3},{2,4},{3,5},{4,6},{5,7},{6,0},{7,1},{8,34},{9,35},{10,... | collective-permute-start | bytes 1376264 | tf_op jit(solution)/shard_map/ppermute | solution.py:102
  296.1 70.0 %collective-permute-start.3 = (bf16[128,1792]{1,0:T(8,128)(2,1)}, bf16[128,1792]{1,0:T(8,128)(2,1)}, u32[]{:S(2)}, u32[]{:S(2)}) collective-permute-start(bf16[128,1792]{1,0:T(8,128)(2,1)} %get-tuple-element.38), channel_id=1, source_target_pairs={{0,4},{1,5},{2,6},{3,7},{4,0},{5,1},{6,2},{7,3},{8,36},{9,37},{10,... | collective-permute-start | bytes 1376264 | tf_op jit(solution)/shard_map/ppermute | solution.py:102
  298.4 76.4 %collective-permute-start.4 = (bf16[128,1792]{1,0:T(8,128)(2,1)}, bf16[128,1792]{1,0:T(8,128)(2,1)}, u32[]{:S(2)}, u32[]{:S(2)}) collective-permute-start(bf16[128,1792]{1,0:T(8,128)(2,1)} %get-tuple-element.37), channel_id=1, source_target_pairs={{0,6},{1,7},{2,0},{3,1},{4,2},{5,3},{6,4},{7,5},{8,38},{9,39},{10,... | collective-permute-start | bytes 1376264 | tf_op jit(solution)/shard_map/ppermute | solution.py:102
  308.0 4.9 %copy-start.6 = (bf16[4096,128]{1,0:T(8,128)(2,1)S(1)}, bf16[4096,128]{1,0:T(8,128)(2,1)}, u32[]{:S(2)}) copy-start(bf16[4096,128]{1,0:T(8,128)(2,1)} %copy.83) | copy-start | bytes 3145732
  380.2 2.0 copy-start.2
  380.6 3.6 copy-start.1
  (1 other events, 1.0 us)
Sparse Core Ops, SparseCore 0:
  10.2 73.1 all-gather.1
  104.8 72.1 reduce-scatter.1

commit v4 on v2

--- a/solution.py
+++ b/solution.py
@@ -32,20 +32,43 @@
     member = ((positions >= run_starts[None, :]) & (positions < run_ends[None, :])).astype(
         jnp.float32
     )
+    chosen = job_tenant.T
+    tokens_same_core = lax.all_gather(grad_output, "chip", axis=0, tiled=True)
+    down_picked, up_picked, hidden_moved, output_moved, tokens_same_core = lax.optimization_barrier(
+        (adapter_down[chosen], adapter_up[chosen], hidden, grad_output, tokens_same_core)
+    )
     hidden_cols = lax.all_to_all(
-        hidden.reshape(tok_rows, shard_count, down_slab), SEQ, split_axis=1, concat_axis=0, tiled=True
+        hidden_moved.reshape(tok_rows, shard_count, down_slab), SEQ, split_axis=1, concat_axis=0, tiled=True
     ).reshape(shard_count, tok_rows, down_slab)
     output_cols = lax.all_to_all(
-        grad_output.reshape(tok_rows, shard_count, up_slab), SEQ, split_axis=1, concat_axis=0, tiled=True
+        output_moved.reshape(tok_rows, shard_count, up_slab), SEQ, split_axis=1, concat_axis=0, tiled=True
     ).reshape(shard_count, tok_rows, up_slab)
-    chosen = job_tenant.T
     fetched_down, fetched_up = (
-        lax.all_to_all(adapter_down[chosen], SEQ, split_axis=1, concat_axis=3, tiled=True),
-        lax.all_to_all(adapter_up[chosen], SEQ, split_axis=1, concat_axis=3, tiled=True),
+        lax.all_to_all(down_picked, SEQ, split_axis=1, concat_axis=3, tiled=True),
+        lax.all_to_all(up_picked, SEQ, split_axis=1, concat_axis=3, tiled=True),
     )
     down_stack = fetched_down.reshape(job_slots * ranks, shard_count * down_slab)
     up_stack = fetched_up.reshape(job_slots * ranks, shard_count * up_slab)
 
+    partner_weight = lax.ppermute(down_weight, "core", [(0, 1), (1, 0)])
+    on_first_core = lax.axis_index("core") == 0
+    weight_pair = jnp.concatenate(
+        [
+            jnp.where(on_first_core, down_weight, partner_weight),
+            jnp.where(on_first_core, partner_weight, down_weight),
+        ],
+        axis=0,
+    )
+    partial_value = lax.dot_general(
+        tokens_same_core, weight_pair, contract_last, preferred_element_type=jnp.float32
+    )
+    quarter = lax.psum_scatter(
+        partial_value.astype(jnp.bfloat16), "grp", scatter_dimension=0, tiled=True
+    )
+    quarter = quarter.reshape(group_count, tok_rows, quarter.shape[1])
+    down_stack, up_stack, hidden_cols, output_cols, quarter = lax.optimization_barrier(
+        (down_stack, up_stack, hidden_cols, output_cols, quarter)
+    )
     def select_jobs(projected):
         return jnp.sum(projected.reshape(tok_rows, job_slots, ranks) * member[:, :, None], axis=1)
 
@@ -58,22 +81,7 @@
     rank_part = jnp.concatenate([select_jobs(grad_proj), select_jobs(act_proj)], axis=1).astype(
         jnp.bfloat16
     )
-    weight_pair = lax.all_gather(down_weight, "core", axis=0, tiled=True)
-    tokens_same_core = lax.all_gather(grad_output, "chip", axis=0, tiled=True)
     rank_sum = lax.psum(rank_part.astype(jnp.float32), "grp")
-    tokens_same_core, weight_pair, rank_sum = lax.optimization_barrier(
-        (tokens_same_core, weight_pair, rank_sum)
-    )
-    partial_value = lax.dot_general(
-        tokens_same_core, weight_pair, contract_last, preferred_element_type=jnp.float32
-    )
-    quarter = lax.psum_scatter(
-        partial_value.astype(jnp.bfloat16), "grp", scatter_dimension=0, tiled=True
-    )
-    quarter = quarter.reshape(group_count, tok_rows, quarter.shape[1])
-    quarter, hidden_cols, output_cols = lax.optimization_barrier(
-        (quarter, hidden_cols, output_cols)
-    )
     chip_count = lax.axis_size("chip")
     row_of_chip = chip_count // group_count
     chip = lax.axis_index("chip")

time: 359 us -> 412 us (1.15)
  blocking collectives: 31.5 us -> 80.2 us
  waiting for transfers between devices: 147 us -> 130 us
  starting transfers between devices: 37.4 us -> 51.9 us
  other arithmetic: 4.52 us -> 11.8 us
    psum x1, blocking collectives: 15.1 us -> 80.2 us  [shards(): rank_sum = lax.psum(rank_part.astype(jnp.float32), 'grp')]
    all_gather x1, waiting for transfers between devices: 8.24 us -> 61.7 us  [shards(): tokens_same_core = lax.all_gather(grad_output, 'chip', axis=0, tiled=True)]
    ppermute x4, waiting for transfers between devices: 41.6 us -> 0.01 us  [shards(): arrived.append(lax.ppermute(piece, ('grp', 'chip', 'core'), pairs))]
    all_to_all x3 -> x4, waiting for transfers between devices: 78.7 us -> 61 us  [the longest x1 46.6 us: shards(): lax.all_to_all(down_picked, SEQ, split_axis=1, concat_axis=3, tiled=True)]
    all_to_all x1 -> x0, blocking collectives: 16.4 us -> none  [shards(): lax.all_to_all(grad_output.reshape(tok_rows, shard_count, up_slab), SEQ,...]
    optimization_barrier x0 -> x4, local copies, waits for them, and re-layouts: none -> 9.66 us  [shards(): lax.optimization_barrier((adapter_down[chosen], adapter_up[chosen], hidde...]
    all_to_all x1, waiting for transfers between devices: 12.8 us -> 4.97 us  [shards(): lax.all_to_all(jnp.broadcast_to(rank_rows[None], (shard_count,) + rank_ro...]
    all_to_all x1, starting transfers between devices: 4.91 us -> 12.7 us  [shards(): lax.all_to_all(jnp.broadcast_to(rank_rows[None], (shard_count,) + rank_ro...]
  transfers between devices with their start and end apart: 11 -> 12, of which waited for: 9 -> 6; matrix products, arithmetic and copies ran while one was open for 23% -> 15% of each run, Pallas kernels for 0% -> 0%
where the time goes in v4:
time: 412 us; the launch traced here: 408 us
  waiting for transfers between devices  130 us (32%)
  blocking collectives  80.2 us (19%)
  local copies, waits for them, and re-layouts  77.1 us (19%)
  starting transfers between devices  51.9 us (13%)
  matrix products  41.9 us (10%)
  between operations  14.4 us (3%)
  other arithmetic  11.8 us (3%)
    psum x1, blocking collectives, shards(): rank_sum = lax.psum(rank_part.astype(jnp.float32), 'grp')  80.2 us
    all_gather x1, waiting for transfers between devices, shards(): tokens_same_core = lax.all_gather(grad_output, 'chip', axis=0, tiled=True)  61.7 us
    all_to_all x1, waiting for transfers between devices, shards(): lax.all_to_all(down_picked, SEQ, split_axis=1, concat_axis=3, tiled=True)  46.6 us
    dot_general x1, matrix products, shards(): lax.dot_general(tokens_same_core, weight_pair, contract_last, preferred_e...  21.3 us
    unnamed x32, local copies, waits for them, and re-layouts  19.8 us
    all_to_all x1, starting transfers between devices, shards(): lax.all_to_all(jnp.broadcast_to(rank_rows[None], (shard_count,) + rank_ro...  12.7 us
    reshape x2, local copies, waits for them, and re-layouts, adapter_grad(): per_job.reshape(shard_count * job_slots, ranks * slab)  11.9 us
    ppermute x4, starting transfers between devices, shards(): arrived.append(lax.ppermute(piece, ('grp', 'chip', 'core'), pairs))  10.6 us
  transfers between devices with their start and end apart: 12, of which 6 were waited for; matrix products, arithmetic and copies ran while one was open for 15% of the time, Pallas kernels for 0%

profile of v4, /device:TPU:9, one launch (start us, length us, event | category | flops | bytes accessed | tf_op | source)
XLA Modules:
  0.0 407.5 jit_solution(1276728895273993235)
XLA Ops:
  15.1 6.6 %broadcast_select_fusion.1 = (bf16[896,2048]{1,0:T(8,128)(2,1)}, bf16[896,2048]{1,0:T(8,128)(2,1)}) fusion(bf16[896,2048]{1,0:T(8,128)(2,1)} %param.9, bf16[896,2048]{1,0:T(8,128)(2,1)} %collective-permute-done, pred[]{:T(512)S(6)} %eq.33), kind=kLoop, calls=%fused_computation.16 | loop fusion | flops 3670016 | bytes 14680065 | tf_op jit(solution)/shard_map/jit(_where)/select_n | solution.py:57
  21.7 61.7 %all-gather.2.cloned.1.call-done = bf16[2048,2048]{1,0:T(8,128)(2,1)} async-done(((bf16[128,2048]{1,0:T(8,128)(2,1)}), bf16[2048,2048]{1,0:T(8,128)(2,1)}) %all-gather.2.cloned.1.call-update) | async-done | bytes 8388624 | tf_op jit(solution)/shard_map/all_gather | solution.py:36
  83.4 21.3 %convolution_convert_fusion = bf16[2048,1792]{1,0:T(8,128)(2,1)} fusion(bf16[2048,2048]{1,0:T(8,128)(2,1)} %all-gather.2.cloned.1.call-done, bf16[896,2048]{1,0:T(8,128)(2,1)} %get-tuple-element.41, bf16[896,2048]{1,0:T(8,128)(2,1)} %get-tuple-element.40), kind=kOutput, calls=%fused_computation.7 | convolution fusion | flops 15050735616 | bytes 23068672 | tf_op jit(solution)/shard_map/dot_general | solution.py:62
  106.7 6.2 %all-to-all-start.3 = ((bf16[128,32,64]{0,2,1:T(8,128)(2,1)}), bf16[128,32,64]{0,2,1:T(8,128)(2,1)S(1)}, u32[]{:S(2)}, u32[]{:S(2)}) async-start(bf16[128,32,64]{0,2,1:T(8,128)(2,1)} %bitcast.11), calls=%async_computation.3 | async-start | bytes 1048576 | tf_op jit(solution)/shard_map/all_to_all | solution.py:43
  114.5 4.8 %reshape.228 = bf16[32,2,8192]{2,1,0:T(2,128)(2,1)} reshape(bf16[32,4,64,64]{3,2,1,0:T(8,128)(2,1)} %bitcast.113) | data formatting | bytes 2097152
  119.3 3.9 all-to-all-done.3
  123.2 5.4 %all-to-all-start.1 = ((bf16[32,2,8192]{2,1,0:T(2,128)(2,1)}), bf16[32,2,8192]{2,1,0:T(2,128)(2,1)}, u32[]{:S(2)}, u32[]{:S(2)}) async-start(bf16[32,2,8192]{2,1,0:T(2,128)(2,1)} %reshape.228), calls=%async_computation.1 | async-start | bytes 2097152 | tf_op jit(solution)/shard_map/all_to_all | solution.py:48
  128.6 4.7 %copy.69 = bf16[4,32,64,224]{3,2,0,1:T(8,128)(2,1)} copy(bf16[4,32,64,224]{3,2,1,0:T(8,128)(2,1)} %bitcast.108) | data formatting | bytes 7340032 | tf_op jit(solution)/shard_map/optimization_barrier | solution.py:37
  133.3 10.5 %all-to-all-done.1 = bf16[32,2,8192]{2,1,0:T(2,128)(2,1)} async-done(((bf16[32,2,8192]{2,1,0:T(2,128)(2,1)}), bf16[32,2,8192]{2,1,0:T(2,128)(2,1)}, u32[]{:S(2)}, u32[]{:S(2)}) %all-to-all-start.1) | async-done | bytes 1048608 | tf_op jit(solution)/shard_map/all_to_all | solution.py:48
  143.9 6.3 %all-to-all-start = ((bf16[4,32,64,224]{3,2,0,1:T(8,128)(2,1)}), bf16[4,32,64,224]{3,2,0,1:T(8,128)(2,1)}, u32[]{:S(2)}, u32[]{:S(2)}) async-start(bf16[4,32,64,224]{3,2,0,1:T(8,128)(2,1)} %copy.69), calls=%async_computation | async-start | bytes 8388608 | tf_op jit(solution)/shard_map/all_to_all | solution.py:47
  153.2 46.6 %all-to-all-done = bf16[4,32,64,224]{3,2,0,1:T(8,128)(2,1)} async-done(((bf16[4,32,64,224]{3,2,0,1:T(8,128)(2,1)}), bf16[4,32,64,224]{3,2,0,1:T(8,128)(2,1)}, u32[]{:S(2)}, u32[]{:S(2)}) %all-to-all-start) | async-done | bytes 3670048 | tf_op jit(solution)/shard_map/all_to_all | solution.py:47
  199.8 9.8 %all-to-all-start.2 = ((bf16[128,32,224]{0,2,1:T(8,128)(2,1)}), bf16[128,32,224]{0,2,1:T(8,128)(2,1)}, u32[]{:S(2)}, u32[]{:S(2)}) async-start(bf16[128,32,224]{0,2,1:T(8,128)(2,1)} %bitcast.7), calls=%async_computation.2 | async-start | bytes 3670016 | tf_op jit(solution)/shard_map/all_to_all | solution.py:40
  210.5 3.8 reshape.229
  218.2 6.6 %copy.70 = bf16[4,1,64,32,224]{4,3,2,0,1:T(8,128)(2,1)} copy(bf16[4,1,64,32,224]{4,2,0,3,1:T(8,128)(2,1)} %bitcast.4) | data formatting | bytes 7340032 | tf_op jit(solution)/shard_map/all_to_all | solution.py:47
  224.8 8.9 %reshape.179 = bf16[256,7168]{1,0:T(8,128)(2,1)} reshape(bf16[4,1,64,32,224]{4,3,2,0,1:T(8,128)(2,1)} %copy.70) | data formatting | bytes 7340032 | tf_op jit(solution)/shard_map/reshape | solution.py:50
  239.7 4.3 %collective-permute-start.1 = (bf16[128,1792]{1,0:T(8,128)(2,1)}, bf16[128,1792]{1,0:T(8,128)(2,1)S(1)}, u32[]{:S(2)}, u32[]{:S(2)}) collective-permute-start(bf16[128,1792]{1,0:T(8,128)(2,1)} %get-tuple-element.44), channel_id=1, source_target_pairs={{0,0},{1,1},{2,2},{3,3},{4,4},{5,5},{6,6},{7,7},{8,32},{9,33},{10,... | collective-permute-start | bytes 1376264 | tf_op jit(solution)/shard_map/ppermute | solution.py:102
  250.3 80.2 %psum.7 = bf16[128,128]{0,1:T(8,128)(2,1)S(1)} all-reduce(f32[128,128]{0,1:T(8,128)S(1)} %maximum_convert_fusion), channel_id=1, replica_groups=mesh['grp'=4,'chip'=16,'core'=2] {'grp'}, use_global_device_ids=true, to_apply=%region_4.5 | all-reduce | flops 16384 | bytes 98304 | tf_op jit(solution)/shard_map/psum | solution.py:84
  331.8 12.7 %all-to-all-start.4 = ((bf16[32,128,128]{1,2,0:T(8,128)(2,1)}), bf16[32,128,128]{1,2,0:T(8,128)(2,1)S(1)}, u32[]{:S(2)}, u32[]{:S(2)}) async-start(bf16[32,128,128]{1,2,0:T(8,128)(2,1)} %broadcast_in_dim.17), calls=%async_computation.5 | async-start | bytes 2097152 | tf_op jit(solution)/shard_map/all_to_all | solution.py:126
  354.7 5.0 %all-to-all-done.4 = bf16[32,128,128]{1,2,0:T(8,128)(2,1)S(1)} async-done(((bf16[32,128,128]{1,2,0:T(8,128)(2,1)}), bf16[32,128,128]{1,2,0:T(8,128)(2,1)S(1)}, u32[]{:S(2)}, u32[]{:S(2)}) %all-to-all-start.4) | async-done | bytes 1048608 | tf_op jit(solution)/shard_map/all_to_all | solution.py:126
  372.3 4.8 %multiply_convert_fusion = bf16[32,4,64,224]{3,2,1,0:T(8,128)(2,1)} fusion(f32[32,4]{1,0:T(8,128)S(1)} %copy.80, f32[32,128,64]{1,2,0:T(8,128)S(1)} %get-tuple-element.43, f32[32,128,4]{1,2,0:T(4,128)S(1)} %fusion.12, bf16[32,128,224]{1,2,0:T(8,128)(2,1)} %bitcast.10), kind=kOutput, calls=%fused_computation.6 | convolution fusion | flops 475529216 | bytes 6619648 | tf_op jit(solution)/shard_map/stjr,stc->sjrc/dot_general | solution.py:139
  377.1 8.5 %reshape.192 = bf16[128,14336]{1,0:T(8,128)(2,1)} reshape(bf16[32,4,64,224]{3,2,1,0:T(8,128)(2,1)} %multiply_convert_fusion) | data formatting | bytes 7340032 | tf_op jit(solution)/shard_map/reshape | solution.py:146
  385.6 6.0 %copy.81 = bf16[14336,128]{1,0:T(8,128)(2,1)} copy(bf16[14336,128]{0,1:T(8,128)(2,1)} %bitcast.111) | data formatting | bytes 7340032 | tf_op jit(solution)/shard_map/dot_general | solution.py:144
  391.7 4.5 %fusion.16 = f32[64,64,224]{2,0,1:T(8,128)S(1)} fusion(bf16[64,224,128]{2,1,0:T(8,128)(2,1)} %bitcast.110, s32[128]{0:T(128)S(1)} %eq.34), kind=kOutput, calls=%fused_computation.46 | convolution fusion | flops 234905600 | bytes 7340544 | tf_op jit(solution)/shard_map/dot_general | solution.py:144
  396.2 4.5 %copy.84 = f32[64,64,224]{2,1,0:T(8,128)} copy(f32[64,64,224]{2,0,1:T(8,128)S(1)} %fusion.16) | data formatting | bytes 7340032
  (92 shorter events, 55.3 us)
Async XLA Ops:
  7.2 2.3 copy-start
  7.2 76.2 %all-gather.2.cloned.1.call-start = ((), (), s32[]{:S(2)}) async-start(), calls=%async_computation.6 | async-start | bytes 8912896 | tf_op jit(solution)/shard_map/all_gather | solution.py:36
  7.9 225.9 %reduce-scatter.2.cloned.1.call-start = ((), (), s32[]{:S(2)}) async-start(), calls=%async_computation.7 | async-start | bytes 9175040 | tf_op jit(solution)/shard_map/reduce_scatter | solution.py:65
  8.0 7.1 %collective-permute-start = (bf16[896,2048]{1,0:T(8,128)(2,1)}, bf16[896,2048]{1,0:T(8,128)(2,1)}, u32[]{:S(2)}, u32[]{:S(2)}) collective-permute-start(bf16[896,2048]{1,0:T(8,128)(2,1)} %param.9), channel_id=1, source_target_pairs={{0,1},{1,0},{2,3},{3,2},{4,5},{5,4},{6,7},{7,6},{8,9},{9,8},{10,11... | collective-permute-start | bytes 11010056 | tf_op jit(solution)/shard_map/ppermute | solution.py:53
  9.5 2.8 copy-start.6
  104.6 1.0 copy-start.5
  106.7 16.5 %all-to-all-start.3 = ((bf16[128,32,64]{0,2,1:T(8,128)(2,1)}), bf16[128,32,64]{0,2,1:T(8,128)(2,1)S(1)}, u32[]{:S(2)}, u32[]{:S(2)}) async-start(bf16[128,32,64]{0,2,1:T(8,128)(2,1)} %bitcast.11), calls=%async_computation.3 | async-start | bytes 1048576 | tf_op jit(solution)/shard_map/all_to_all | solution.py:43
  123.2 10.1 %copy-start.8 = (bf16[128,32,64]{0,2,1:T(8,128)(2,1)}, bf16[128,32,64]{0,2,1:T(8,128)(2,1)S(1)}, u32[]{:S(2)}) copy-start(bf16[128,32,64]{0,2,1:T(8,128)(2,1)S(1)} %all-to-all-done.3) | copy-start | bytes 1572868
  123.2 20.7 %all-to-all-start.1 = ((bf16[32,2,8192]{2,1,0:T(2,128)(2,1)}), bf16[32,2,8192]{2,1,0:T(2,128)(2,1)}, u32[]{:S(2)}, u32[]{:S(2)}) async-start(bf16[32,2,8192]{2,1,0:T(2,128)(2,1)} %reshape.228), calls=%async_computation.1 | async-start | bytes 2097152 | tf_op jit(solution)/shard_map/all_to_all | solution.py:48
  133.3 16.9 %copy-start.11 = (s32[32,4]{0,1:T(4,128)S(1)}, s32[32,4]{0,1:T(4,128)}, u32[]{:S(2)}) copy-start(s32[32,4]{0,1:T(4,128)} %param.12) | copy-start | bytes 1540
  133.3 17.0 %copy-start.12 = (s32[32,4]{0,1:T(4,128)S(1)}, s32[32,4]{0,1:T(4,128)}, u32[]{:S(2)}) copy-start(s32[32,4]{0,1:T(4,128)} %param.13) | copy-start | bytes 1540
  133.3 17.6 %copy-start.3 = (bf16[128,7168]{1,0:T(8,128)(2,1)S(1)}, bf16[128,7168]{1,0:T(8,128)(2,1)}, u32[]{:S(2)}) copy-start(bf16[128,7168]{1,0:T(8,128)(2,1)} %param.8) | copy-start | bytes 5505028
  143.9 55.9 %all-to-all-start = ((bf16[4,32,64,224]{3,2,0,1:T(8,128)(2,1)}), bf16[4,32,64,224]{3,2,0,1:T(8,128)(2,1)}, u32[]{:S(2)}, u32[]{:S(2)}) async-start(bf16[4,32,64,224]{3,2,0,1:T(8,128)(2,1)} %copy.69), calls=%async_computation | async-start | bytes 8388608 | tf_op jit(solution)/shard_map/all_to_all | solution.py:47
  199.8 34.0 %all-to-all-start.2 = ((bf16[128,32,224]{0,2,1:T(8,128)(2,1)}), bf16[128,32,224]{0,2,1:T(8,128)(2,1)}, u32[]{:S(2)}, u32[]{:S(2)}) async-start(bf16[128,32,224]{0,2,1:T(8,128)(2,1)} %bitcast.7), calls=%async_computation.2 | async-start | bytes 3670016 | tf_op jit(solution)/shard_map/all_to_all | solution.py:40
  224.8 9.0 %copy-start.4 = (bf16[128,7168]{1,0:T(8,128)(2,1)S(1)}, bf16[128,7168]{1,0:T(8,128)(2,1)}, u32[]{:S(2)}) copy-start(bf16[128,7168]{1,0:T(8,128)(2,1)} %param.8) | copy-start | bytes 5505028
  233.8 5.0 %copy-start.7 = (bf16[512,1792]{1,0:T(8,128)(2,1)S(1)}, bf16[512,1792]{1,0:T(8,128)(2,1)}, u32[]{:S(2)}) copy-start(bf16[512,1792]{1,0:T(8,128)(2,1)} %reduce-scatter.2.cloned.1.call-done) | copy-start | bytes 5505028
  239.7 104.9 %collective-permute-start.1 = (bf16[128,1792]{1,0:T(8,128)(2,1)}, bf16[128,1792]{1,0:T(8,128)(2,1)S(1)}, u32[]{:S(2)}, u32[]{:S(2)}) collective-permute-start(bf16[128,1792]{1,0:T(8,128)(2,1)} %get-tuple-element.44), channel_id=1, source_target_pairs={{0,0},{1,1},{2,2},{3,3},{4,4},{5,5},{6,6},{7,7},{8,32},{9,33},{10,... | collective-permute-start | bytes 1376264 | tf_op jit(solution)/shard_map/ppermute | solution.py:102
  244.0 100.6 %collective-permute-start.2 = (bf16[128,1792]{1,0:T(8,128)(2,1)S(1)}, bf16[128,1792]{1,0:T(8,128)(2,1)}, u32[]{:S(2)}, u32[]{:S(2)}) collective-permute-start(bf16[128,1792]{1,0:T(8,128)(2,1)S(1)} %get-tuple-element.47), channel_id=1, source_target_pairs={{0,2},{1,3},{2,4},{3,5},{4,6},{5,7},{6,0},{7,1},{8,34},{9,35},{10,... | collective-permute-start | bytes 1376264 | tf_op jit(solution)/shard_map/ppermute | solution.py:102
  244.9 99.7 %collective-permute-start.3 = (bf16[128,1792]{1,0:T(8,128)(2,1)S(1)}, bf16[128,1792]{1,0:T(8,128)(2,1)}, u32[]{:S(2)}, u32[]{:S(2)}) collective-permute-start(bf16[128,1792]{1,0:T(8,128)(2,1)S(1)} %get-tuple-element.46), channel_id=1, source_target_pairs={{0,4},{1,5},{2,6},{3,7},{4,0},{5,1},{6,2},{7,3},{8,36},{9,37},{10,... | collective-permute-start | bytes 1376264 | tf_op jit(solution)/shard_map/ppermute | solution.py:102
  248.2 96.4 %collective-permute-start.4 = (bf16[128,1792]{1,0:T(8,128)(2,1)S(1)}, bf16[128,1792]{1,0:T(8,128)(2,1)}, u32[]{:S(2)}, u32[]{:S(2)}) collective-permute-start(bf16[128,1792]{1,0:T(8,128)(2,1)S(1)} %get-tuple-element.45), channel_id=1, source_target_pairs={{0,6},{1,7},{2,0},{3,1},{4,2},{5,3},{6,4},{7,5},{8,38},{9,39},{10,... | collective-permute-start | bytes 1376264 | tf_op jit(solution)/shard_map/ppermute | solution.py:102
  331.8 27.9 %all-to-all-start.4 = ((bf16[32,128,128]{1,2,0:T(8,128)(2,1)}), bf16[32,128,128]{1,2,0:T(8,128)(2,1)S(1)}, u32[]{:S(2)}, u32[]{:S(2)}) async-start(bf16[32,128,128]{1,2,0:T(8,128)(2,1)} %broadcast_in_dim.17), calls=%async_computation.5 | async-start | bytes 2097152 | tf_op jit(solution)/shard_map/all_to_all | solution.py:126
  350.7 2.0 copy-start.2
  359.7 1.0 copy-start.9
  391.7 9.0 %copy-start.1 = (bf16[64,64,224]{2,1,0:T(8,128)(2,1)S(1)}, bf16[64,64,224]{2,1,0:T(8,128)(2,1)}, u32[]{:S(2)}) copy-start(bf16[64,64,224]{2,1,0:T(8,128)(2,1)} %param.10) | copy-start | bytes 5505028
  (1 other events, 0.8 us)
Sparse Core Ops, SparseCore 0:
  10.2 73.1 all-gather.1
  104.8 72.1 reduce-scatter.1

commit v5 on v2

--- a/solution.py
+++ b/solution.py
@@ -58,7 +58,15 @@
     rank_part = jnp.concatenate([select_jobs(grad_proj), select_jobs(act_proj)], axis=1).astype(
         jnp.bfloat16
     )
-    weight_pair = lax.all_gather(down_weight, "core", axis=0, tiled=True)
+    partner_weight = lax.ppermute(down_weight, "core", [(0, 1), (1, 0)])
+    on_first_core = lax.axis_index("core") == 0
+    weight_pair = jnp.concatenate(
+        [
+            jnp.where(on_first_core, down_weight, partner_weight),
+            jnp.where(on_first_core, partner_weight, down_weight),
+        ],
+        axis=0,
+    )
     tokens_same_core = lax.all_gather(grad_output, "chip", axis=0, tiled=True)
     rank_sum = lax.psum(rank_part.astype(jnp.float32), "grp")
     tokens_same_core, weight_pair, rank_sum = lax.optimization_barrier(

time: 359 us -> 396 us (1.10)
  waiting for transfers between devices: 147 us -> 164 us
  other arithmetic: 4.52 us -> 19.4 us
    all_to_all x1, waiting for transfers between devices: 50 us -> 73.2 us  [shards(): lax.all_to_all(adapter_down[chosen], SEQ, split_axis=1, concat_axis=3, ti...]
    all_gather x1, waiting for transfers between devices: 8.24 us -> 0.01 us  [shards(): tokens_same_core = lax.all_gather(grad_output, 'chip', axis=0, tiled=True)]
    concatenate x0 -> x1, other arithmetic: none -> 7.53 us  [shards(): jnp.concatenate([jnp.where(on_first_core, down_weight, partner_weight), j...]
    select_n x0 -> x1, other arithmetic: none -> 6.67 us  [shards(): jnp.where(on_first_core, down_weight, partner_weight)]
    all_to_all x1, blocking collectives: 16.4 us -> 21.4 us  [shards(): lax.all_to_all(grad_output.reshape(tok_rows, shard_count, up_slab), SEQ,...]
    all_to_all x1, waiting for transfers between devices: 7.59 us -> 11.7 us  [shards(): lax.all_to_all(adapter_up[chosen], SEQ, split_axis=1, concat_axis=3, tile...]
    unnamed x26 -> x24, local copies, waits for them, and re-layouts: 17.4 us -> 17.4 us
  transfers between devices with their start and end apart: 11 -> 11, of which waited for: 9 -> 8; matrix products, arithmetic and copies ran while one was open for 23% -> 25% of each run, Pallas kernels for 0% -> 0%
where the time goes in v5:
time: 396 us; the launch traced here: 390 us
  waiting for transfers between devices  164 us (41%)
  local copies, waits for them, and re-layouts  78.1 us (20%)
  matrix products  41.7 us (11%)
  starting transfers between devices  37.6 us (9%)
  blocking collectives  35.2 us (9%)
  other arithmetic  19.4 us (5%)
  between operations  14.4 us (4%)
    all_to_all x1, waiting for transfers between devices, shards(): lax.all_to_all(adapter_down[chosen], SEQ, split_axis=1, concat_axis=3, ti...  73.2 us
    ppermute x4, waiting for transfers between devices, shards(): arrived.append(lax.ppermute(piece, ('grp', 'chip', 'core'), pairs))  41.6 us
    all_to_all x1, blocking collectives, shards(): lax.all_to_all(grad_output.reshape(tok_rows, shard_count, up_slab), SEQ,...  21.4 us
    dot_general x1, matrix products, shards(): lax.dot_general(tokens_same_core, weight_pair, contract_last, preferred_e...  21.2 us
    all_to_all x1, waiting for transfers between devices, shards(): lax.all_to_all(hidden.reshape(tok_rows, shard_count, down_slab), SEQ, spl...  21 us
    unnamed x24, local copies, waits for them, and re-layouts  17.4 us
    psum x1, blocking collectives, shards(): rank_sum = lax.psum(rank_part.astype(jnp.float32), 'grp')  13.8 us
    all_to_all x1, waiting for transfers between devices, shards(): lax.all_to_all(jnp.broadcast_to(rank_rows[None], (shard_count,) + rank_ro...  12.8 us
  transfers between devices with their start and end apart: 11, of which 8 were waited for; matrix products, arithmetic and copies ran while one was open for 25% of the time, Pallas kernels for 0%

profile of v5, /device:TPU:9, one launch (start us, length us, event | category | flops | bytes accessed | tf_op | source)
XLA Modules:
  0.0 390.5 jit_solution(6411313271361791088)
XLA Ops:
  15.2 4.6 %reshape.236 = bf16[32,2,8192]{2,1,0:T(2,128)(2,1)} reshape(bf16[32,4,64,64]{3,2,1,0:T(8,128)(2,1)} %bitcast.113) | data formatting | bytes 2097152
  19.9 8.9 %all-to-all-start = ((bf16[32,2,8192]{2,1,0:T(2,128)(2,1)}), bf16[32,2,8192]{2,1,0:T(2,128)(2,1)S(1)}, u32[]{:S(2)}, u32[]{:S(2)}) async-start(bf16[32,2,8192]{2,1,0:T(2,128)(2,1)} %reshape.236), calls=%async_computation | async-start | bytes 2097152 | tf_op jit(solution)/shard_map/all_to_all | solution.py:44
  31.6 4.7 %copy.72 = bf16[4,32,64,224]{3,2,0,1:T(8,128)(2,1)} copy(bf16[4,32,64,224]{3,2,1,0:T(8,128)(2,1)} %bitcast.109) | data formatting | bytes 7340032 | tf_op jit(solution)/shard_map/gather | solution.py:43
  36.3 11.7 %all-to-all-done = bf16[32,2,8192]{2,1,0:T(2,128)(2,1)S(1)} async-done(((bf16[32,2,8192]{2,1,0:T(2,128)(2,1)}), bf16[32,2,8192]{2,1,0:T(2,128)(2,1)S(1)}, u32[]{:S(2)}, u32[]{:S(2)}) %all-to-all-start) | async-done | bytes 1048608 | tf_op jit(solution)/shard_map/all_to_all | solution.py:44
  48.0 6.2 %all-to-all-start.1 = ((bf16[4,32,64,224]{3,2,0,1:T(8,128)(2,1)}), bf16[4,32,64,224]{3,2,0,1:T(8,128)(2,1)}, u32[]{:S(2)}, u32[]{:S(2)}) async-start(bf16[4,32,64,224]{3,2,0,1:T(8,128)(2,1)} %copy.72), calls=%async_computation.1 | async-start | bytes 8388608 | tf_op jit(solution)/shard_map/all_to_all | solution.py:43
  62.1 73.2 %all-to-all-done.1 = bf16[4,32,64,224]{3,2,0,1:T(8,128)(2,1)} async-done(((bf16[4,32,64,224]{3,2,0,1:T(8,128)(2,1)}), bf16[4,32,64,224]{3,2,0,1:T(8,128)(2,1)}, u32[]{:S(2)}, u32[]{:S(2)}) %all-to-all-start.1) | async-done | bytes 3670048 | tf_op jit(solution)/shard_map/all_to_all | solution.py:43
  135.3 6.6 %copy.73 = bf16[4,1,64,32,224]{4,3,2,0,1:T(8,128)(2,1)} copy(bf16[4,1,64,32,224]{4,2,0,3,1:T(8,128)(2,1)} %bitcast.12) | data formatting | bytes 7340032 | tf_op jit(solution)/shard_map/all_to_all | solution.py:43
  142.0 8.9 %reshape.191 = bf16[256,7168]{1,0:T(8,128)(2,1)} reshape(bf16[4,1,64,32,224]{4,3,2,0,1:T(8,128)(2,1)} %copy.73) | data formatting | bytes 7340032 | tf_op jit(solution)/shard_map/reshape | solution.py:46
  154.1 13.8 %psum.7 = bf16[128,128]{0,1:T(8,128)(2,1)S(1)} all-reduce(f32[128,128]{0,1:T(8,128)S(1)} %maximum_convert_fusion), channel_id=1, replica_groups=mesh['grp'=4,'chip'=16,'core'=2] {'grp'}, use_global_device_ids=true, to_apply=%region_3.4 | all-reduce | flops 16384 | bytes 98304 | tf_op jit(solution)/shard_map/psum | solution.py:71
  167.9 6.7 %broadcast_select_fusion.1 = (bf16[896,2048]{1,0:T(8,128)(2,1)}, bf16[896,2048]{1,0:T(8,128)(2,1)}) fusion(bf16[896,2048]{1,0:T(8,128)(2,1)} %param.9, bf16[896,2048]{1,0:T(8,128)(2,1)} %collective-permute-done, pred[]{:T(512)S(6)} %eq.33), kind=kLoop, calls=%fused_computation.14 | loop fusion | flops 3670016 | bytes 14680065 | tf_op jit(solution)/shard_map/jit(_where)/select_n | solution.py:65
  174.6 7.5 %pad_maximum_fusion = bf16[1792,2048]{1,0:T(8,128)(2,1)} fusion(bf16[896,2048]{1,0:T(8,128)(2,1)} %get-tuple-element.33, bf16[896,2048]{1,0:T(8,128)(2,1)} %get-tuple-element.32), kind=kLoop, calls=%fused_computation.8 | loop fusion | flops 14680064 | bytes 14680064 | tf_op jit(solution)/shard_map/concatenate | solution.py:63
  182.1 21.2 %convolution_convert_fusion = bf16[2048,1792]{1,0:T(8,128)(2,1)} fusion(bf16[2048,2048]{1,0:T(8,128)(2,1)} %all-gather.2.cloned.1.call-done, bf16[1792,2048]{1,0:T(8,128)(2,1)} %pad_maximum_fusion), kind=kOutput, calls=%fused_computation.7 | convolution fusion | flops 15036055552 | bytes 23068672 | tf_op jit(solution)/shard_map/dot_general | solution.py:75
  203.7 21.4 %all_to_all.65 = bf16[128,32,64]{0,2,1:T(8,128)(2,1)} all-to-all(bf16[128,32,64]{0,2,1:T(8,128)(2,1)S(1)} %bitcast.117), channel_id=1, replica_groups=mesh['grp'=4,'chip'=16,'core'=2] {'chip','core'}, dimensions={1} | all-to-all | bytes 1048576 | tf_op jit(solution)/shard_map/all_to_all | solution.py:38
  226.3 4.9 %all-to-all-start.4 = ((bf16[32,128,128]{1,2,0:T(8,128)(2,1)}), bf16[32,128,128]{1,2,0:T(8,128)(2,1)S(1)}, u32[]{:S(2)}, u32[]{:S(2)}) async-start(bf16[32,128,128]{1,2,0:T(8,128)(2,1)} %broadcast_in_dim.17), calls=%async_computation.5 | async-start | bytes 2097152 | tf_op jit(solution)/shard_map/all_to_all | solution.py:126
  233.6 12.8 %all-to-all-done.4 = bf16[32,128,128]{1,2,0:T(8,128)(2,1)S(1)} async-done(((bf16[32,128,128]{1,2,0:T(8,128)(2,1)}), bf16[32,128,128]{1,2,0:T(8,128)(2,1)S(1)}, u32[]{:S(2)}, u32[]{:S(2)}) %all-to-all-start.4) | async-done | bytes 1048608 | tf_op jit(solution)/shard_map/all_to_all | solution.py:126
  246.4 6.2 %all-to-all-start.2 = ((bf16[128,32,224]{0,2,1:T(8,128)(2,1)}), bf16[128,32,224]{0,2,1:T(8,128)(2,1)}, u32[]{:S(2)}, u32[]{:S(2)}) async-start(bf16[128,32,224]{0,2,1:T(8,128)(2,1)} %bitcast.16), calls=%async_computation.3 | async-start | bytes 3670016 | tf_op jit(solution)/shard_map/all_to_all | solution.py:35
  255.1 21.0 %all-to-all-done.2 = bf16[128,32,224]{0,2,1:T(8,128)(2,1)} async-done(((bf16[128,32,224]{0,2,1:T(8,128)(2,1)}), bf16[128,32,224]{0,2,1:T(8,128)(2,1)}, u32[]{:S(2)}, u32[]{:S(2)}) %all-to-all-start.2) | async-done | bytes 1835040 | tf_op jit(solution)/shard_map/all_to_all | solution.py:35
  300.7 4.8 %multiply_convert_fusion = bf16[32,4,64,224]{3,2,1,0:T(8,128)(2,1)} fusion(f32[32,4]{1,0:T(8,128)S(1)} %copy.80, f32[32,128,64]{1,2,0:T(8,128)S(1)} %get-tuple-element.35, f32[32,128,4]{1,2,0:T(4,128)S(1)} %fusion.9, bf16[32,128,224]{1,2,0:T(8,128)(2,1)} %bitcast.19), kind=kOutput, calls=%fused_computation.6 | convolution fusion | flops 475529216 | bytes 6619648 | tf_op jit(solution)/shard_map/stjr,stc->sjrc/dot_general | solution.py:139
  309.2 8.5 %reshape.200 = bf16[128,14336]{1,0:T(8,128)(2,1)} reshape(bf16[32,4,64,224]{3,2,1,0:T(8,128)(2,1)} %multiply_convert_fusion) | data formatting | bytes 7340032 | tf_op jit(solution)/shard_map/reshape | solution.py:146
  317.7 6.0 %copy.81 = bf16[14336,128]{1,0:T(8,128)(2,1)} copy(bf16[14336,128]{0,1:T(8,128)(2,1)} %bitcast.112) | data formatting | bytes 7340032 | tf_op jit(solution)/shard_map/dot_general | solution.py:144
  328.2 4.4 %copy.84 = f32[64,64,224]{2,1,0:T(8,128)} copy(f32[64,64,224]{2,0,1:T(8,128)S(1)} %fusion.13) | data formatting | bytes 7340032
  332.6 9.2 %collective-permute-done.2 = bf16[128,1792]{1,0:T(8,128)(2,1)} collective-permute-done((bf16[128,1792]{1,0:T(8,128)(2,1)}, bf16[128,1792]{1,0:T(8,128)(2,1)}, u32[]{:S(2)}, u32[]{:S(2)}) %collective-permute-start.2) | collective-permute-done | bytes 458784 | tf_op jit(solution)/shard_map/ppermute | solution.py:102
  341.8 24.2 %collective-permute-done.3 = bf16[128,1792]{1,0:T(8,128)(2,1)} collective-permute-done((bf16[128,1792]{1,0:T(8,128)(2,1)}, bf16[128,1792]{1,0:T(8,128)(2,1)}, u32[]{:S(2)}, u32[]{:S(2)}) %collective-permute-start.3) | collective-permute-done | bytes 458784 | tf_op jit(solution)/shard_map/ppermute | solution.py:102
  366.0 8.3 %collective-permute-done.4 = bf16[128,1792]{1,0:T(8,128)(2,1)} collective-permute-done((bf16[128,1792]{1,0:T(8,128)(2,1)}, bf16[128,1792]{1,0:T(8,128)(2,1)}, u32[]{:S(2)}, u32[]{:S(2)}) %collective-permute-start.4) | collective-permute-done | bytes 458784 | tf_op jit(solution)/shard_map/ppermute | solution.py:102
  (82 shorter events, 70.1 us)
Async XLA Ops:
  7.2 21.6 %copy-start = (bf16[64,64,224]{2,1,0:T(8,128)(2,1)S(1)}, bf16[64,64,224]{2,1,0:T(8,128)(2,1)}, u32[]{:S(2)}) copy-start(bf16[64,64,224]{2,1,0:T(8,128)(2,1)} %param.10) | copy-start | bytes 5505028
  7.2 175.0 %all-gather.2.cloned.1.call-start = ((), (), s32[]{:S(2)}) async-start(), calls=%async_computation.6 | async-start | bytes 8912896 | tf_op jit(solution)/shard_map/all_gather | solution.py:70
  19.9 28.2 %all-to-all-start = ((bf16[32,2,8192]{2,1,0:T(2,128)(2,1)}), bf16[32,2,8192]{2,1,0:T(2,128)(2,1)S(1)}, u32[]{:S(2)}, u32[]{:S(2)}) async-start(bf16[32,2,8192]{2,1,0:T(2,128)(2,1)} %reshape.236), calls=%async_computation | async-start | bytes 2097152 | tf_op jit(solution)/shard_map/all_to_all | solution.py:44
  36.3 18.4 %copy-start.7 = (s32[32,4]{0,1:T(4,128)S(1)}, s32[32,4]{0,1:T(4,128)}, u32[]{:S(2)}) copy-start(s32[32,4]{0,1:T(4,128)} %param.13) | copy-start | bytes 1540
  48.0 87.3 %all-to-all-start.1 = ((bf16[4,32,64,224]{3,2,0,1:T(8,128)(2,1)}), bf16[4,32,64,224]{3,2,0,1:T(8,128)(2,1)}, u32[]{:S(2)}, u32[]{:S(2)}) async-start(bf16[4,32,64,224]{3,2,0,1:T(8,128)(2,1)} %copy.72), calls=%async_computation.1 | async-start | bytes 8388608 | tf_op jit(solution)/shard_map/all_to_all | solution.py:43
  54.2 224.9 %reduce-scatter.2.cloned.1.call-start = ((), (), s32[]{:S(2)}) async-start(), calls=%async_computation.7 | async-start | bytes 9175040 | tf_op jit(solution)/shard_map/reduce_scatter | solution.py:78
  54.3 113.7 %collective-permute-start = (bf16[896,2048]{1,0:T(8,128)(2,1)}, bf16[896,2048]{1,0:T(8,128)(2,1)}, u32[]{:S(2)}, u32[]{:S(2)}) collective-permute-start(bf16[896,2048]{1,0:T(8,128)(2,1)} %param.9), channel_id=1, source_target_pairs={{0,1},{1,0},{2,3},{3,2},{4,5},{5,4},{6,7},{7,6},{8,9},{9,8},{10,11... | collective-permute-start | bytes 11010056 | tf_op jit(solution)/shard_map/ppermute | solution.py:61
  56.7 3.8 copy-start.4
  141.9 9.0 %copy-start.3 = (bf16[128,7168]{1,0:T(8,128)(2,1)S(1)}, bf16[128,7168]{1,0:T(8,128)(2,1)}, u32[]{:S(2)}) copy-start(bf16[128,7168]{1,0:T(8,128)(2,1)} %param.8) | copy-start | bytes 5505028
  226.3 20.1 %all-to-all-start.4 = ((bf16[32,128,128]{1,2,0:T(8,128)(2,1)}), bf16[32,128,128]{1,2,0:T(8,128)(2,1)S(1)}, u32[]{:S(2)}, u32[]{:S(2)}) async-start(bf16[32,128,128]{1,2,0:T(8,128)(2,1)} %broadcast_in_dim.17), calls=%async_computation.5 | async-start | bytes 2097152 | tf_op jit(solution)/shard_map/all_to_all | solution.py:126
  231.2 21.4 %copy-start.6 = (s32[32,4]{0,1:T(4,128)S(1)}, s32[32,4]{0,1:T(4,128)}, u32[]{:S(2)}) copy-start(s32[32,4]{0,1:T(4,128)} %param.12) | copy-start | bytes 1540
  246.4 29.7 %all-to-all-start.2 = ((bf16[128,32,224]{0,2,1:T(8,128)(2,1)}), bf16[128,32,224]{0,2,1:T(8,128)(2,1)}, u32[]{:S(2)}, u32[]{:S(2)}) async-start(bf16[128,32,224]{0,2,1:T(8,128)(2,1)} %bitcast.16), calls=%async_computation.3 | async-start | bytes 3670016 | tf_op jit(solution)/shard_map/all_to_all | solution.py:35
  289.8 15.7 %copy-start.5 = (bf16[4096,128]{1,0:T(8,128)(2,1)S(1)}, bf16[4096,128]{1,0:T(8,128)(2,1)}, u32[]{:S(2)}) copy-start(bf16[4096,128]{1,0:T(8,128)(2,1)} %copy.83) | copy-start | bytes 3145732
  289.8 42.8 %collective-permute-start.1 = (bf16[128,1792]{1,0:T(8,128)(2,1)}, bf16[128,1792]{1,0:T(8,128)(2,1)}, u32[]{:S(2)}, u32[]{:S(2)}) collective-permute-start(bf16[128,1792]{1,0:T(8,128)(2,1)} %get-tuple-element.36), channel_id=1, source_target_pairs={{0,0},{1,1},{2,2},{3,3},{4,4},{5,5},{6,6},{7,7},{8,32},{9,33},{10,... | collective-permute-start | bytes 1376264 | tf_op jit(solution)/shard_map/ppermute | solution.py:102
  291.9 49.9 %collective-permute-start.2 = (bf16[128,1792]{1,0:T(8,128)(2,1)}, bf16[128,1792]{1,0:T(8,128)(2,1)}, u32[]{:S(2)}, u32[]{:S(2)}) collective-permute-start(bf16[128,1792]{1,0:T(8,128)(2,1)} %get-tuple-element.39), channel_id=1, source_target_pairs={{0,2},{1,3},{2,4},{3,5},{4,6},{5,7},{6,0},{7,1},{8,34},{9,35},{10,... | collective-permute-start | bytes 1376264 | tf_op jit(solution)/shard_map/ppermute | solution.py:102
  295.3 70.7 %collective-permute-start.3 = (bf16[128,1792]{1,0:T(8,128)(2,1)}, bf16[128,1792]{1,0:T(8,128)(2,1)}, u32[]{:S(2)}, u32[]{:S(2)}) collective-permute-start(bf16[128,1792]{1,0:T(8,128)(2,1)} %get-tuple-element.38), channel_id=1, source_target_pairs={{0,4},{1,5},{2,6},{3,7},{4,0},{5,1},{6,2},{7,3},{8,36},{9,37},{10,... | collective-permute-start | bytes 1376264 | tf_op jit(solution)/shard_map/ppermute | solution.py:102
  297.6 76.7 %collective-permute-start.4 = (bf16[128,1792]{1,0:T(8,128)(2,1)}, bf16[128,1792]{1,0:T(8,128)(2,1)}, u32[]{:S(2)}, u32[]{:S(2)}) collective-permute-start(bf16[128,1792]{1,0:T(8,128)(2,1)} %get-tuple-element.37), channel_id=1, source_target_pairs={{0,6},{1,7},{2,0},{3,1},{4,2},{5,3},{6,4},{7,5},{8,38},{9,39},{10,... | collective-permute-start | bytes 1376264 | tf_op jit(solution)/shard_map/ppermute | solution.py:102
  379.6 2.0 copy-start.2
  380.0 3.6 copy-start.1
Sparse Core Ops, SparseCore 0:
  10.2 126.8 all-gather.1
  203.5 75.5 reduce-scatter.1

commit v6 on v2

--- a/solution.py
+++ b/solution.py
@@ -64,12 +64,21 @@
     tokens_same_core, weight_pair, rank_sum = lax.optimization_barrier(
         (tokens_same_core, weight_pair, rank_sum)
     )
-    partial_value = lax.dot_general(
-        tokens_same_core, weight_pair, contract_last, preferred_element_type=jnp.float32
-    )
-    quarter = lax.psum_scatter(
-        partial_value.astype(jnp.bfloat16), "grp", scatter_dimension=0, tiled=True
-    )
+    half_rows = weight_pair.shape[0] // 2
+    halves = []
+    for half in range(2):
+        partial_value = lax.dot_general(
+            tokens_same_core,
+            weight_pair[half * half_rows:(half + 1) * half_rows],
+            contract_last,
+            preferred_element_type=jnp.float32,
+        )
+        halves.append(
+            lax.psum_scatter(
+                partial_value.astype(jnp.bfloat16), "grp", scatter_dimension=0, tiled=True
+            )
+        )
+    quarter = jnp.concatenate(halves, axis=1)
     quarter = quarter.reshape(group_count, tok_rows, quarter.shape[1])
     quarter, hidden_cols, output_cols = lax.optimization_barrier(
         (quarter, hidden_cols, output_cols)

time: 359 us -> 365 us (1.017)
  matrix products: 41.7 us -> 47.4 us
    reduce_scatter x1 -> x2, waiting for transfers between devices: 4.54 us -> 25.7 us  [shards(): lax.psum_scatter(partial_value.astype(jnp.bfloat16), 'grp', scatter_dimen...]
    all_to_all x1, waiting for transfers between devices: 21 us -> 0.01 us  [shards(): lax.all_to_all(hidden.reshape(tok_rows, shard_count, down_slab), SEQ, spl...]
    dot_general x1 -> x2, matrix products: 21.3 us -> 27.3 us  [shards(): lax.dot_general(tokens_same_core, weight_pair[half * half_rows:(half + 1)...]
    unnamed x26 -> x38, local copies, waits for them, and re-layouts: 17.4 us -> 17.4 us
  transfers between devices with their start and end apart: 11 -> 12, of which waited for: 9 -> 8; matrix products, arithmetic and copies ran while one was open for 23% -> 27% of each run, Pallas kernels for 0% -> 0%
where the time goes in v6:
time: 365 us; the launch traced here: 361 us
  waiting for transfers between devices  147 us (40%)
  local copies, waits for them, and re-layouts  76 us (21%)
  matrix products  47.4 us (13%)
  starting transfers between devices  37.5 us (10%)
  blocking collectives  31.6 us (9%)
  between operations  14.1 us (4%)
  other arithmetic  7.12 us (2%)
    all_to_all x1, waiting for transfers between devices, shards(): lax.all_to_all(adapter_down[chosen], SEQ, split_axis=1, concat_axis=3, ti...  50 us
    ppermute x4, waiting for transfers between devices, shards(): arrived.append(lax.ppermute(piece, ('grp', 'chip', 'core'), pairs))  41.6 us
    dot_general x2, matrix products, shards(): lax.dot_general(tokens_same_core, weight_pair[half * half_rows:(half + 1)...  27.3 us
    reduce_scatter x2, waiting for transfers between devices, shards(): lax.psum_scatter(partial_value.astype(jnp.bfloat16), 'grp', scatter_dimen...  25.7 us
    unnamed x38, local copies, waits for them, and re-layouts  17.4 us
    all_to_all x1, blocking collectives, shards(): lax.all_to_all(grad_output.reshape(tok_rows, shard_count, up_slab), SEQ,...  16.4 us
    psum x1, blocking collectives, shards(): rank_sum = lax.psum(rank_part.astype(jnp.float32), 'grp')  15.1 us
    all_to_all x1, waiting for transfers between devices, shards(): lax.all_to_all(jnp.broadcast_to(rank_rows[None], (shard_count,) + rank_ro...  12.4 us
  transfers between devices with their start and end apart: 12, of which 8 were waited for; matrix products, arithmetic and copies ran while one was open for 27% of the time, Pallas kernels for 0%

profile of v6, /device:TPU:9, one launch (start us, length us, event | category | flops | bytes accessed | tf_op | source)
XLA Modules:
  0.0 360.6 jit_solution(4864098441025533891)
XLA Ops:
  14.1 4.6 %reshape.236 = bf16[32,2,8192]{2,1,0:T(2,128)(2,1)} reshape(bf16[32,4,64,64]{3,2,1,0:T(8,128)(2,1)} %bitcast.113) | data formatting | bytes 2097152
  18.7 8.9 %all-to-all-start = ((bf16[32,2,8192]{2,1,0:T(2,128)(2,1)}), bf16[32,2,8192]{2,1,0:T(2,128)(2,1)S(1)}, u32[]{:S(2)}, u32[]{:S(2)}) async-start(bf16[32,2,8192]{2,1,0:T(2,128)(2,1)} %reshape.236), calls=%async_computation | async-start | bytes 2097152 | tf_op jit(solution)/shard_map/all_to_all | solution.py:44
  30.4 4.8 %copy.72 = bf16[4,32,64,224]{3,2,0,1:T(8,128)(2,1)} copy(bf16[4,32,64,224]{3,2,1,0:T(8,128)(2,1)} %bitcast.109) | data formatting | bytes 7340032 | tf_op jit(solution)/shard_map/gather | solution.py:43
  35.2 7.6 %all-to-all-done = bf16[32,2,8192]{2,1,0:T(2,128)(2,1)S(1)} async-done(((bf16[32,2,8192]{2,1,0:T(2,128)(2,1)}), bf16[32,2,8192]{2,1,0:T(2,128)(2,1)S(1)}, u32[]{:S(2)}, u32[]{:S(2)}) %all-to-all-start) | async-done | bytes 1048608 | tf_op jit(solution)/shard_map/all_to_all | solution.py:44
  42.8 6.4 %all-to-all-start.1 = ((bf16[4,32,64,224]{3,2,0,1:T(8,128)(2,1)}), bf16[4,32,64,224]{3,2,0,1:T(8,128)(2,1)}, u32[]{:S(2)}, u32[]{:S(2)}) async-start(bf16[4,32,64,224]{3,2,0,1:T(8,128)(2,1)} %copy.72), calls=%async_computation.1 | async-start | bytes 8388608 | tf_op jit(solution)/shard_map/all_to_all | solution.py:43
  56.7 50.0 %all-to-all-done.1 = bf16[4,32,64,224]{3,2,0,1:T(8,128)(2,1)} async-done(((bf16[4,32,64,224]{3,2,0,1:T(8,128)(2,1)}), bf16[4,32,64,224]{3,2,0,1:T(8,128)(2,1)}, u32[]{:S(2)}, u32[]{:S(2)}) %all-to-all-start.1) | async-done | bytes 3670048 | tf_op jit(solution)/shard_map/all_to_all | solution.py:43
  106.7 6.6 %copy.73 = bf16[4,1,64,32,224]{4,3,2,0,1:T(8,128)(2,1)} copy(bf16[4,1,64,32,224]{4,2,0,3,1:T(8,128)(2,1)} %bitcast.12) | data formatting | bytes 7340032 | tf_op jit(solution)/shard_map/all_to_all | solution.py:43
  113.3 9.0 %reshape.191 = bf16[256,7168]{1,0:T(8,128)(2,1)} reshape(bf16[4,1,64,32,224]{4,3,2,0,1:T(8,128)(2,1)} %copy.73) | data formatting | bytes 7340032 | tf_op jit(solution)/shard_map/reshape | solution.py:46
  125.5 15.1 %psum.7 = bf16[128,128]{0,1:T(8,128)(2,1)S(1)} all-reduce(f32[128,128]{0,1:T(8,128)S(1)} %maximum_convert_fusion), channel_id=1, replica_groups=mesh['grp'=4,'chip'=16,'core'=2] {'grp'}, use_global_device_ids=true, to_apply=%region_3.4 | all-reduce | flops 16384 | bytes 98304 | tf_op jit(solution)/shard_map/psum | solution.py:63
  140.6 8.1 %all-gather.3.cloned.1.call-done = bf16[2048,2048]{1,0:T(8,128)(2,1)} async-done(((bf16[128,2048]{1,0:T(8,128)(2,1)}), bf16[2048,2048]{1,0:T(8,128)(2,1)}) %all-gather.3.cloned.1.call-update) | async-done | bytes 8388624 | tf_op jit(solution)/shard_map/all_gather | solution.py:62
  148.8 13.7 %fusion.6 = bf16[2048,896]{1,0:T(8,128)(2,1)} fusion(bf16[2048,2048]{1,0:T(8,128)(2,1)} %all-gather.3.cloned.1.call-done, bf16[1792,2048]{1,0:T(8,128)(2,1)} %all-gather.5.cloned.1.call-done), kind=kOutput, calls=%fused_computation.15 | convolution fusion | flops 7518027776 | bytes 15728640 | tf_op jit(solution)/shard_map/dot_general | solution.py:70
  162.5 13.6 %fusion.9 = bf16[2048,896]{1,0:T(8,128)(2,1)} fusion(bf16[2048,2048]{1,0:T(8,128)(2,1)} %all-gather.3.cloned.1.call-done, bf16[1792,2048]{1,0:T(8,128)(2,1)} %all-gather.5.cloned.1.call-done), kind=kOutput, calls=%fused_computation.16 | convolution fusion | flops 7518027776 | bytes 15728640 | tf_op jit(solution)/shard_map/dot_general | solution.py:70
  176.4 16.4 %all_to_all.65 = bf16[128,32,64]{0,2,1:T(8,128)(2,1)} all-to-all(bf16[128,32,64]{0,2,1:T(8,128)(2,1)S(1)} %bitcast.118), channel_id=1, replica_groups=mesh['grp'=4,'chip'=16,'core'=2] {'chip','core'}, dimensions={1} | all-to-all | bytes 1048576 | tf_op jit(solution)/shard_map/all_to_all | solution.py:38
  194.1 4.9 %all-to-all-start.4 = ((bf16[32,128,128]{1,2,0:T(8,128)(2,1)}), bf16[32,128,128]{1,2,0:T(8,128)(2,1)S(1)}, u32[]{:S(2)}, u32[]{:S(2)}) async-start(bf16[32,128,128]{1,2,0:T(8,128)(2,1)} %broadcast_in_dim.17), calls=%async_computation.6 | async-start | bytes 2097152 | tf_op jit(solution)/shard_map/all_to_all | solution.py:127
  201.7 12.4 %all-to-all-done.4 = bf16[32,128,128]{1,2,0:T(8,128)(2,1)S(1)} async-done(((bf16[32,128,128]{1,2,0:T(8,128)(2,1)}), bf16[32,128,128]{1,2,0:T(8,128)(2,1)S(1)}, u32[]{:S(2)}, u32[]{:S(2)}) %all-to-all-start.4) | async-done | bytes 1048608 | tf_op jit(solution)/shard_map/all_to_all | solution.py:127
  214.2 6.2 %all-to-all-start.2 = ((bf16[128,32,224]{0,2,1:T(8,128)(2,1)}), bf16[128,32,224]{0,2,1:T(8,128)(2,1)}, u32[]{:S(2)}, u32[]{:S(2)}) async-start(bf16[128,32,224]{0,2,1:T(8,128)(2,1)} %bitcast.16), calls=%async_computation.4 | async-start | bytes 3670016 | tf_op jit(solution)/shard_map/all_to_all | solution.py:35
  224.2 25.7 %reduce-scatter.5.cloned.1.call-done = bf16[512,896]{1,0:T(8,128)(2,1)} async-done(((bf16[2048,896]{1,0:T(8,128)(2,1)}), bf16[512,896]{1,0:T(8,128)(2,1)}) %reduce-scatter.5.cloned.1.call-update) | async-done | bytes 917520 | tf_op jit(solution)/shard_map/reduce_scatter | solution.py:77
  271.2 4.8 %multiply_convert_fusion = bf16[32,4,64,224]{3,2,1,0:T(8,128)(2,1)} fusion(f32[32,4]{1,0:T(8,128)S(1)} %copy.80, f32[32,128,64]{1,2,0:T(8,128)S(1)} %copy-done.5, f32[32,128,4]{1,2,0:T(4,128)S(1)} %copy-done.9, bf16[32,128,224]{1,2,0:T(8,128)(2,1)} %bitcast.19), kind=kOutput, calls=%fused_computation.6 | convolution fusion | flops 475529216 | bytes 6619648 | tf_op jit(solution)/shard_map/stjr,stc->sjrc/dot_general | solution.py:140
  279.7 8.5 %reshape.200 = bf16[128,14336]{1,0:T(8,128)(2,1)} reshape(bf16[32,4,64,224]{3,2,1,0:T(8,128)(2,1)} %multiply_convert_fusion) | data formatting | bytes 7340032 | tf_op jit(solution)/shard_map/reshape | solution.py:147
  288.2 6.0 %copy.81 = bf16[14336,128]{1,0:T(8,128)(2,1)} copy(bf16[14336,128]{0,1:T(8,128)(2,1)} %bitcast.112) | data formatting | bytes 7340032 | tf_op jit(solution)/shard_map/dot_general | solution.py:145
  298.6 4.4 %copy.84 = f32[64,64,224]{2,1,0:T(8,128)} copy(f32[64,64,224]{2,0,1:T(8,128)S(1)} %fusion.23) | data formatting | bytes 7340032
  303.1 9.2 %collective-permute-done.1 = bf16[128,1792]{1,0:T(8,128)(2,1)} collective-permute-done((bf16[128,1792]{1,0:T(8,128)(2,1)}, bf16[128,1792]{1,0:T(8,128)(2,1)}, u32[]{:S(2)}, u32[]{:S(2)}) %collective-permute-start.1) | collective-permute-done | bytes 458784 | tf_op jit(solution)/shard_map/ppermute | solution.py:103
  312.3 24.2 %collective-permute-done.2 = bf16[128,1792]{1,0:T(8,128)(2,1)} collective-permute-done((bf16[128,1792]{1,0:T(8,128)(2,1)S(1)}, bf16[128,1792]{1,0:T(8,128)(2,1)}, u32[]{:S(2)}, u32[]{:S(2)}) %collective-permute-start.2) | collective-permute-done | bytes 458784 | tf_op jit(solution)/shard_map/ppermute | solution.py:103
  336.5 8.2 %collective-permute-done.3 = bf16[128,1792]{1,0:T(8,128)(2,1)} collective-permute-done((bf16[128,1792]{1,0:T(8,128)(2,1)S(1)}, bf16[128,1792]{1,0:T(8,128)(2,1)}, u32[]{:S(2)}, u32[]{:S(2)}) %collective-permute-start.3) | collective-permute-done | bytes 458784 | tf_op jit(solution)/shard_map/ppermute | solution.py:103
  (100 shorter events, 66.9 us)
Async XLA Ops:
  7.2 20.4 %copy-start = (bf16[64,64,224]{2,1,0:T(8,128)(2,1)S(1)}, bf16[64,64,224]{2,1,0:T(8,128)(2,1)}, u32[]{:S(2)}) copy-start(bf16[64,64,224]{2,1,0:T(8,128)(2,1)} %param.10) | copy-start | bytes 5505028
  7.2 133.4 %all-gather.5.cloned.1.call-start = ((), (), s32[]{:S(2)}) async-start(), calls=%async_computation.8 | async-start | bytes 11010048 | tf_op jit(solution)/shard_map/all_gather | solution.py:61
  7.9 140.8 %all-gather.3.cloned.1.call-start = ((), (), s32[]{:S(2)}) async-start(), calls=%async_computation.7 | async-start | bytes 8912896 | tf_op jit(solution)/shard_map/all_gather | solution.py:62
  18.7 24.1 %all-to-all-start = ((bf16[32,2,8192]{2,1,0:T(2,128)(2,1)}), bf16[32,2,8192]{2,1,0:T(2,128)(2,1)S(1)}, u32[]{:S(2)}, u32[]{:S(2)}) async-start(bf16[32,2,8192]{2,1,0:T(2,128)(2,1)} %reshape.236), calls=%async_computation | async-start | bytes 2097152 | tf_op jit(solution)/shard_map/all_to_all | solution.py:44
  35.2 14.0 %copy-start.11 = (s32[32,4]{0,1:T(4,128)S(1)}, s32[32,4]{0,1:T(4,128)}, u32[]{:S(2)}) copy-start(s32[32,4]{0,1:T(4,128)} %param.13) | copy-start | bytes 1540
  42.8 63.9 %all-to-all-start.1 = ((bf16[4,32,64,224]{3,2,0,1:T(8,128)(2,1)}), bf16[4,32,64,224]{3,2,0,1:T(8,128)(2,1)}, u32[]{:S(2)}, u32[]{:S(2)}) async-start(bf16[4,32,64,224]{3,2,0,1:T(8,128)(2,1)} %copy.72), calls=%async_computation.1 | async-start | bytes 8388608 | tf_op jit(solution)/shard_map/all_to_all | solution.py:43
  49.2 175.0 %reduce-scatter.3.cloned.1.call-start = ((), (), s32[]{:S(2)}) async-start(), calls=%async_computation.9 | async-start | bytes 4587520 | tf_op jit(solution)/shard_map/reduce_scatter | solution.py:77
  51.2 3.8 %copy-start.4 = (bf16[128,2048]{1,0:T(8,128)(2,1)S(1)}, bf16[128,2048]{1,0:T(8,128)(2,1)}, u32[]{:S(2)}) copy-start(bf16[128,2048]{1,0:T(8,128)(2,1)} %param.7) | copy-start | bytes 1572868
  113.3 9.0 %copy-start.3 = (bf16[128,7168]{1,0:T(8,128)(2,1)S(1)}, bf16[128,7168]{1,0:T(8,128)(2,1)}, u32[]{:S(2)}) copy-start(bf16[128,7168]{1,0:T(8,128)(2,1)} %param.8) | copy-start | bytes 5505028
  162.5 87.4 %reduce-scatter.5.cloned.1.call-start = ((), (), s32[]{:S(2)}) async-start(), calls=%async_computation.10 | async-start | bytes 4587520 | tf_op jit(solution)/shard_map/reduce_scatter | solution.py:77
  194.1 20.1 %all-to-all-start.4 = ((bf16[32,128,128]{1,2,0:T(8,128)(2,1)}), bf16[32,128,128]{1,2,0:T(8,128)(2,1)S(1)}, u32[]{:S(2)}, u32[]{:S(2)}) async-start(bf16[32,128,128]{1,2,0:T(8,128)(2,1)} %broadcast_in_dim.17), calls=%async_computation.6 | async-start | bytes 2097152 | tf_op jit(solution)/shard_map/all_to_all | solution.py:127
  214.2 37.3 %all-to-all-start.2 = ((bf16[128,32,224]{0,2,1:T(8,128)(2,1)}), bf16[128,32,224]{0,2,1:T(8,128)(2,1)}, u32[]{:S(2)}, u32[]{:S(2)}) async-start(bf16[128,32,224]{0,2,1:T(8,128)(2,1)} %bitcast.16), calls=%async_computation.4 | async-start | bytes 3670016 | tf_op jit(solution)/shard_map/all_to_all | solution.py:35
  222.7 28.8 %copy-start.8 = (f32[32,128,4]{1,2,0:T(4,128)}, f32[32,128,4]{1,2,0:T(4,128)S(1)}, u32[]{:S(2)}) copy-start(f32[32,128,4]{1,2,0:T(4,128)S(1)} %fusion.19) | copy-start | bytes 196612
  257.9 13.3 %copy-start.9 = (f32[32,128,4]{1,2,0:T(4,128)S(1)}, f32[32,128,4]{1,2,0:T(4,128)}, u32[]{:S(2)}) copy-start(f32[32,128,4]{1,2,0:T(4,128)} %copy-done.8) | copy-start | bytes 196612
  259.2 12.0 %copy-start.5 = (f32[32,128,64]{1,2,0:T(8,128)S(1)}, f32[32,128,64]{1,2,0:T(8,128)}, u32[]{:S(2)}) copy-start(f32[32,128,64]{1,2,0:T(8,128)} %get-tuple-element.33) | copy-start | bytes 3145732
  260.3 15.7 %copy-start.6 = (bf16[4096,128]{1,0:T(8,128)(2,1)S(1)}, bf16[4096,128]{1,0:T(8,128)(2,1)}, u32[]{:S(2)}) copy-start(bf16[4096,128]{1,0:T(8,128)(2,1)} %copy.83) | copy-start | bytes 3145732
  260.3 15.7 %copy-start.12 = (s32[128]{0:T(128)S(1)}, s32[128]{0:T(128)}, u32[]{:S(2)}) copy-start(s32[128]{0:T(128)} %eq.30) | copy-start | bytes 1540
  260.3 42.8 %collective-permute-start = (bf16[128,1792]{1,0:T(8,128)(2,1)}, bf16[128,1792]{1,0:T(8,128)(2,1)S(1)}, u32[]{:S(2)}, u32[]{:S(2)}) collective-permute-start(bf16[128,1792]{1,0:T(8,128)(2,1)} %get-tuple-element.34), channel_id=1, source_target_pairs={{0,0},{1,1},{2,2},{3,3},{4,4},{5,5},{6,6},{7,7},{8,32},{9,33},{10,... | collective-permute-start | bytes 1376264 | tf_op jit(solution)/shard_map/ppermute | solution.py:103
  262.3 50.0 %collective-permute-start.1 = (bf16[128,1792]{1,0:T(8,128)(2,1)}, bf16[128,1792]{1,0:T(8,128)(2,1)}, u32[]{:S(2)}, u32[]{:S(2)}) collective-permute-start(bf16[128,1792]{1,0:T(8,128)(2,1)} %get-tuple-element.37), channel_id=1, source_target_pairs={{0,2},{1,3},{2,4},{3,5},{4,6},{5,7},{6,0},{7,1},{8,34},{9,35},{10,... | collective-permute-start | bytes 1376264 | tf_op jit(solution)/shard_map/ppermute | solution.py:103
  265.7 70.7 %collective-permute-start.2 = (bf16[128,1792]{1,0:T(8,128)(2,1)S(1)}, bf16[128,1792]{1,0:T(8,128)(2,1)}, u32[]{:S(2)}, u32[]{:S(2)}) collective-permute-start(bf16[128,1792]{1,0:T(8,128)(2,1)S(1)} %get-tuple-element.36), channel_id=1, source_target_pairs={{0,4},{1,5},{2,6},{3,7},{4,0},{5,1},{6,2},{7,3},{8,36},{9,37},{10,... | collective-permute-start | bytes 1376264 | tf_op jit(solution)/shard_map/ppermute | solution.py:103
  268.0 76.7 %collective-permute-start.3 = (bf16[128,1792]{1,0:T(8,128)(2,1)S(1)}, bf16[128,1792]{1,0:T(8,128)(2,1)}, u32[]{:S(2)}, u32[]{:S(2)}) collective-permute-start(bf16[128,1792]{1,0:T(8,128)(2,1)S(1)} %get-tuple-element.35), channel_id=1, source_target_pairs={{0,6},{1,7},{2,0},{3,1},{4,2},{5,3},{6,4},{7,5},{8,38},{9,39},{10,... | collective-permute-start | bytes 1376264 | tf_op jit(solution)/shard_map/ppermute | solution.py:103
  288.2 6.0 %copy-start.13 = (s32[128]{0:T(128)S(1)}, s32[128]{0:T(128)}, u32[]{:S(2)}) copy-start(s32[128]{0:T(128)} %eq.30) | copy-start | bytes 1540
  344.7 3.5 copy-start.14
  350.5 3.6 copy-start.1
  (3 other events, 5.2 us)
Sparse Core Ops, SparseCore 0:
  9.7 23.8 all-gather.4
  35.7 113.0 all-gather.2
  162.6 42.1 reduce-scatter.2
  207.6 42.2 reduce-scatter.4

commit v7 on v2

--- a/solution.py
+++ b/solution.py
@@ -39,8 +39,10 @@
         grad_output.reshape(tok_rows, shard_count, up_slab), SEQ, split_axis=1, concat_axis=0, tiled=True
     ).reshape(shard_count, tok_rows, up_slab)
     chosen = job_tenant.T
+    tokens_same_core = lax.all_gather(grad_output, "chip", axis=0, tiled=True)
+    down_picked, tokens_same_core = lax.optimization_barrier((adapter_down[chosen], tokens_same_core))
     fetched_down, fetched_up = (
-        lax.all_to_all(adapter_down[chosen], SEQ, split_axis=1, concat_axis=3, tiled=True),
+        lax.all_to_all(down_picked, SEQ, split_axis=1, concat_axis=3, tiled=True),
         lax.all_to_all(adapter_up[chosen], SEQ, split_axis=1, concat_axis=3, tiled=True),
     )
     down_stack = fetched_down.reshape(job_slots * ranks, shard_count * down_slab)
@@ -59,11 +61,7 @@
         jnp.bfloat16
     )
     weight_pair = lax.all_gather(down_weight, "core", axis=0, tiled=True)
-    tokens_same_core = lax.all_gather(grad_output, "chip", axis=0, tiled=True)
     rank_sum = lax.psum(rank_part.astype(jnp.float32), "grp")
-    tokens_same_core, weight_pair, rank_sum = lax.optimization_barrier(
-        (tokens_same_core, weight_pair, rank_sum)
-    )
     partial_value = lax.dot_general(
         tokens_same_core, weight_pair, contract_last, preferred_element_type=jnp.float32
     )

time: 359 us -> 421 us (1.17)
  waiting for transfers between devices: 147 us -> 215 us
  blocking collectives: 31.5 us -> 13.7 us
  starting transfers between devices: 37.4 us -> 49.7 us
    all_gather x1, waiting for transfers between devices: 8.24 us -> 71.7 us  [shards(): tokens_same_core = lax.all_gather(grad_output, 'chip', axis=0, tiled=True)]
    all_gather x1, waiting for transfers between devices: 0.02 us -> 22.8 us  [shards(): weight_pair = lax.all_gather(down_weight, 'core', axis=0, tiled=True)]
    all_to_all x1 -> x0, blocking collectives: 16.4 us -> none  [shards(): lax.all_to_all(grad_output.reshape(tok_rows, shard_count, up_slab), SEQ,...]
    all_to_all x1 -> x2, waiting for transfers between devices: 50 us -> 38.7 us  [the longest x1 38.7 us: shards(): lax.all_to_all(down_picked, SEQ, split_axis=1, concat_axis=3, tiled=True)]
    all_to_all x1 -> x2, starting transfers between devices: 6.37 us -> 16.3 us  [the longest x1 9.97 us: shards(): lax.all_to_all(grad_output.reshape(tok_rows, shard_count, up_slab), SEQ,...]
    all_to_all x1, starting transfers between devices: 4.91 us -> 11.1 us  [shards(): lax.all_to_all(jnp.broadcast_to(rank_rows[None], (shard_count,) + rank_ro...]
    ppermute x4, waiting for transfers between devices: 41.6 us -> 36.2 us  [shards(): arrived.append(lax.ppermute(piece, ('grp', 'chip', 'core'), pairs))]
    unnamed x26 -> x32, local copies, waits for them, and re-layouts: 17.4 us -> 22.7 us
  transfers between devices with their start and end apart: 11 -> 12, of which waited for: 9 -> 9; matrix products, arithmetic and copies ran while one was open for 23% -> 21% of each run, Pallas kernels for 0% -> 0%
where the time goes in v7:
time: 421 us; the launch traced here: 416 us
  waiting for transfers between devices  215 us (51%)
  local copies, waits for them, and re-layouts  78.8 us (19%)
  starting transfers between devices  49.7 us (12%)
  matrix products  40.5 us (10%)
  between operations  14.2 us (3%)
  blocking collectives  13.7 us (3%)
  other arithmetic  4.52 us (1%)
    all_gather x1, waiting for transfers between devices, shards(): tokens_same_core = lax.all_gather(grad_output, 'chip', axis=0, tiled=True)  71.7 us
    all_to_all x1, waiting for transfers between devices, shards(): lax.all_to_all(down_picked, SEQ, split_axis=1, concat_axis=3, tiled=True)  38.7 us
    ppermute x4, waiting for transfers between devices, shards(): arrived.append(lax.ppermute(piece, ('grp', 'chip', 'core'), pairs))  36.2 us
    all_gather x1, waiting for transfers between devices, shards(): weight_pair = lax.all_gather(down_weight, 'core', axis=0, tiled=True)  22.8 us
    unnamed x32, local copies, waits for them, and re-layouts  22.7 us
    dot_general x1, matrix products, shards(): lax.dot_general(tokens_same_core, weight_pair, contract_last, preferred_e...  21.3 us
    all_to_all x1, waiting for transfers between devices, shards(): lax.all_to_all(hidden.reshape(tok_rows, shard_count, down_slab), SEQ, spl...  21 us
    psum x1, blocking collectives, shards(): rank_sum = lax.psum(rank_part.astype(jnp.float32), 'grp')  13.7 us
  transfers between devices with their start and end apart: 12, of which 9 were waited for; matrix products, arithmetic and copies ran while one was open for 21% of the time, Pallas kernels for 0%

profile of v7, /device:TPU:9, one launch (start us, length us, event | category | flops | bytes accessed | tf_op | source)
XLA Modules:
  0.0 416.3 jit_solution(14952444703818122932)
XLA Ops:
  11.7 71.7 %all-gather.3.cloned.1.call-done = bf16[2048,2048]{1,0:T(8,128)(2,1)} async-done(((bf16[128,2048]{1,0:T(8,128)(2,1)}), bf16[2048,2048]{1,0:T(8,128)(2,1)}) %all-gather.3.cloned.1.call-update) | async-done | bytes 8388624 | tf_op jit(solution)/shard_map/all_gather | solution.py:42
  83.4 22.8 %all-gather.5.cloned.1.call-done = bf16[1792,2048]{1,0:T(8,128)(2,1)} async-done(((bf16[896,2048]{1,0:T(8,128)(2,1)}), bf16[1792,2048]{1,0:T(8,128)(2,1)}) %all-gather.5.cloned.1.call-update) | async-done | bytes 7340048 | tf_op jit(solution)/shard_map/all_gather | solution.py:63
  106.2 21.3 %convolution_convert_fusion = bf16[2048,1792]{1,0:T(8,128)(2,1)} fusion(bf16[2048,2048]{1,0:T(8,128)(2,1)} %all-gather.3.cloned.1.call-done, bf16[1792,2048]{1,0:T(8,128)(2,1)} %all-gather.5.cloned.1.call-done), kind=kOutput, calls=%fused_computation.7 | convolution fusion | flops 15036055552 | bytes 23068672 | tf_op jit(solution)/shard_map/dot_general | solution.py:65
  131.2 4.6 %reshape.236 = bf16[32,2,8192]{2,1,0:T(2,128)(2,1)} reshape(bf16[32,4,64,64]{3,2,1,0:T(8,128)(2,1)} %bitcast.114) | data formatting | bytes 2097152
  135.8 7.4 %all-to-all-start.2 = ((bf16[32,2,8192]{2,1,0:T(2,128)(2,1)}), bf16[32,2,8192]{2,1,0:T(2,128)(2,1)S(1)}, u32[]{:S(2)}, u32[]{:S(2)}) async-start(bf16[32,2,8192]{2,1,0:T(2,128)(2,1)} %reshape.236), calls=%async_computation.3 | async-start | bytes 2097152 | tf_op jit(solution)/shard_map/all_to_all | solution.py:46
  143.2 4.7 %copy.75 = bf16[4,32,64,224]{3,2,0,1:T(8,128)(2,1)} copy(bf16[4,32,64,224]{3,2,1,0:T(8,128)(2,1)} %bitcast.109) | data formatting | bytes 7340032 | tf_op jit(solution)/shard_map/optimization_barrier | solution.py:43
  148.0 10.4 %all-to-all-done.2 = bf16[32,2,8192]{2,1,0:T(2,128)(2,1)S(1)} async-done(((bf16[32,2,8192]{2,1,0:T(2,128)(2,1)}), bf16[32,2,8192]{2,1,0:T(2,128)(2,1)S(1)}, u32[]{:S(2)}, u32[]{:S(2)}) %all-to-all-start.2) | async-done | bytes 1048608 | tf_op jit(solution)/shard_map/all_to_all | solution.py:46
  159.4 6.4 %all-to-all-start.3 = ((bf16[4,32,64,224]{3,2,0,1:T(8,128)(2,1)}), bf16[4,32,64,224]{3,2,0,1:T(8,128)(2,1)}, u32[]{:S(2)}, u32[]{:S(2)}) async-start(bf16[4,32,64,224]{3,2,0,1:T(8,128)(2,1)} %copy.75), calls=%async_computation.4 | async-start | bytes 8388608 | tf_op jit(solution)/shard_map/all_to_all | solution.py:45
  176.6 38.7 %all-to-all-done.3 = bf16[4,32,64,224]{3,2,0,1:T(8,128)(2,1)} async-done(((bf16[4,32,64,224]{3,2,0,1:T(8,128)(2,1)}), bf16[4,32,64,224]{3,2,0,1:T(8,128)(2,1)}, u32[]{:S(2)}, u32[]{:S(2)}) %all-to-all-start.3) | async-done | bytes 3670048 | tf_op jit(solution)/shard_map/all_to_all | solution.py:45
  215.3 10.0 %all-to-all-start.1 = ((bf16[128,32,64]{0,2,1:T(8,128)(2,1)}), bf16[128,32,64]{0,2,1:T(8,128)(2,1)S(1)}, u32[]{:S(2)}, u32[]{:S(2)}) async-start(bf16[128,32,64]{0,2,1:T(8,128)(2,1)} %bitcast.7), calls=%async_computation.2 | async-start | bytes 1048576 | tf_op jit(solution)/shard_map/all_to_all | solution.py:38
  225.3 6.6 %copy.76 = bf16[4,1,64,32,224]{4,3,2,0,1:T(8,128)(2,1)} copy(bf16[4,1,64,32,224]{4,2,0,3,1:T(8,128)(2,1)} %bitcast.31) | data formatting | bytes 7340032 | tf_op jit(solution)/shard_map/all_to_all | solution.py:45
  231.9 8.9 %reshape.196 = bf16[256,7168]{1,0:T(8,128)(2,1)} reshape(bf16[4,1,64,32,224]{4,3,2,0,1:T(8,128)(2,1)} %copy.76) | data formatting | bytes 7340032 | tf_op jit(solution)/shard_map/reshape | solution.py:48
  244.1 13.7 %psum.7 = bf16[128,128]{0,1:T(8,128)(2,1)S(1)} all-reduce(f32[128,128]{0,1:T(8,128)S(1)} %maximum_convert_fusion), channel_id=1, replica_groups=mesh['grp'=4,'chip'=16,'core'=2] {'grp'}, use_global_device_ids=true, to_apply=%region_4.5 | all-reduce | flops 16384 | bytes 98304 | tf_op jit(solution)/shard_map/psum | solution.py:64
  259.0 11.1 %all-to-all-start.4 = ((bf16[32,128,128]{1,2,0:T(8,128)(2,1)}), bf16[32,128,128]{1,2,0:T(8,128)(2,1)S(1)}, u32[]{:S(2)}, u32[]{:S(2)}) async-start(bf16[32,128,128]{1,2,0:T(8,128)(2,1)} %broadcast_in_dim.17), calls=%async_computation.5 | async-start | bytes 2097152 | tf_op jit(solution)/shard_map/all_to_all | solution.py:116
  272.5 12.8 %all-to-all-done.4 = bf16[32,128,128]{1,2,0:T(8,128)(2,1)S(1)} async-done(((bf16[32,128,128]{1,2,0:T(8,128)(2,1)}), bf16[32,128,128]{1,2,0:T(8,128)(2,1)S(1)}, u32[]{:S(2)}, u32[]{:S(2)}) %all-to-all-start.4) | async-done | bytes 1048608 | tf_op jit(solution)/shard_map/all_to_all | solution.py:116
  285.3 6.2 %all-to-all-start = ((bf16[128,32,224]{0,2,1:T(8,128)(2,1)}), bf16[128,32,224]{0,2,1:T(8,128)(2,1)}, u32[]{:S(2)}, u32[]{:S(2)}) async-start(bf16[128,32,224]{0,2,1:T(8,128)(2,1)} %bitcast.3), calls=%async_computation.1 | async-start | bytes 3670016 | tf_op jit(solution)/shard_map/all_to_all | solution.py:35
  294.1 21.0 %all-to-all-done = bf16[128,32,224]{0,2,1:T(8,128)(2,1)} async-done(((bf16[128,32,224]{0,2,1:T(8,128)(2,1)}), bf16[128,32,224]{0,2,1:T(8,128)(2,1)}, u32[]{:S(2)}, u32[]{:S(2)}) %all-to-all-start) | async-done | bytes 1835040 | tf_op jit(solution)/shard_map/all_to_all | solution.py:35
  326.2 4.8 %multiply_convert_fusion = bf16[32,4,64,224]{3,2,1,0:T(8,128)(2,1)} fusion(f32[32,4]{1,0:T(8,128)S(1)} %copy.80, f32[32,128,64]{1,2,0:T(8,128)S(1)} %get-tuple-element.31, f32[32,128,4]{1,2,0:T(4,128)S(1)} %fusion.9, bf16[32,128,224]{1,2,0:T(8,128)(2,1)} %bitcast.6), kind=kOutput, calls=%fused_computation.6 | convolution fusion | flops 475529216 | bytes 6619648 | tf_op jit(solution)/shard_map/stjr,stc->sjrc/dot_general | solution.py:129
  331.0 8.5 %reshape.200 = bf16[128,14336]{1,0:T(8,128)(2,1)} reshape(bf16[32,4,64,224]{3,2,1,0:T(8,128)(2,1)} %multiply_convert_fusion) | data formatting | bytes 7340032 | tf_op jit(solution)/shard_map/reshape | solution.py:136
  339.6 6.0 %copy.81 = bf16[14336,128]{1,0:T(8,128)(2,1)} copy(bf16[14336,128]{0,1:T(8,128)(2,1)} %bitcast.111) | data formatting | bytes 7340032 | tf_op jit(solution)/shard_map/dot_general | solution.py:134
  345.6 4.5 %fusion.13 = f32[64,64,224]{2,0,1:T(8,128)S(1)} fusion(bf16[64,224,128]{2,1,0:T(8,128)(2,1)} %bitcast.112, s32[128]{0:T(128)S(1)} %eq.30), kind=kOutput, calls=%fused_computation.41 | convolution fusion | flops 234905600 | bytes 7340544 | tf_op jit(solution)/shard_map/dot_general | solution.py:134
  352.2 4.4 %copy.84 = f32[64,64,224]{2,1,0:T(8,128)} copy(f32[64,64,224]{2,0,1:T(8,128)S(1)} %fusion.13) | data formatting | bytes 7340032
  367.0 23.6 %collective-permute-done.1 = bf16[128,1792]{1,0:T(8,128)(2,1)} collective-permute-done((bf16[128,1792]{1,0:T(8,128)(2,1)}, bf16[128,1792]{1,0:T(8,128)(2,1)}, u32[]{:S(2)}, u32[]{:S(2)}) %collective-permute-start.1) | collective-permute-done | bytes 458784 | tf_op jit(solution)/shard_map/ppermute | solution.py:92
  390.6 9.8 %collective-permute-done = bf16[128,1792]{1,0:T(8,128)(2,1)} collective-permute-done((bf16[128,1792]{1,0:T(8,128)(2,1)}, bf16[128,1792]{1,0:T(8,128)(2,1)}, u32[]{:S(2)}, u32[]{:S(2)}) %collective-permute-start) | collective-permute-done | bytes 458784 | tf_op jit(solution)/shard_map/ppermute | solution.py:92
  (90 shorter events, 61.9 us)
Async XLA Ops:
  7.2 1.7 copy-start
  7.2 1.5 copy-start.10
  7.2 76.2 %all-gather.3.cloned.1.call-start = ((), (), s32[]{:S(2)}) async-start(), calls=%async_computation.6 | async-start | bytes 8912896 | tf_op jit(solution)/shard_map/all_gather | solution.py:42
  7.9 98.2 %all-gather.5.cloned.1.call-start = ((), (), s32[]{:S(2)}) async-start(), calls=%async_computation.7 | async-start | bytes 11010048 | tf_op jit(solution)/shard_map/all_gather | solution.py:63
  8.7 306.4 %reduce-scatter.2.cloned.1.call-start = ((), (), s32[]{:S(2)}) async-start(), calls=%async_computation.8 | async-start | bytes 9175040 | tf_op jit(solution)/shard_map/reduce_scatter | solution.py:68
  127.4 1.2 copy-start.6
  135.8 22.6 %all-to-all-start.2 = ((bf16[32,2,8192]{2,1,0:T(2,128)(2,1)}), bf16[32,2,8192]{2,1,0:T(2,128)(2,1)S(1)}, u32[]{:S(2)}, u32[]{:S(2)}) async-start(bf16[32,2,8192]{2,1,0:T(2,128)(2,1)} %reshape.236), calls=%async_computation.3 | async-start | bytes 2097152 | tf_op jit(solution)/shard_map/all_to_all | solution.py:46
  148.0 17.8 %copy-start.4 = (bf16[128,2048]{1,0:T(8,128)(2,1)S(1)}, bf16[128,2048]{1,0:T(8,128)(2,1)}, u32[]{:S(2)}) copy-start(bf16[128,2048]{1,0:T(8,128)(2,1)} %param.7) | copy-start | bytes 1572868
  148.0 18.8 %copy-start.11 = (s32[32,4]{0,1:T(4,128)S(1)}, s32[32,4]{0,1:T(4,128)}, u32[]{:S(2)}) copy-start(s32[32,4]{0,1:T(4,128)} %param.13) | copy-start | bytes 1540
  158.4 1.0 copy-start.5
  159.4 56.0 %all-to-all-start.3 = ((bf16[4,32,64,224]{3,2,0,1:T(8,128)(2,1)}), bf16[4,32,64,224]{3,2,0,1:T(8,128)(2,1)}, u32[]{:S(2)}, u32[]{:S(2)}) async-start(bf16[4,32,64,224]{3,2,0,1:T(8,128)(2,1)} %copy.75), calls=%async_computation.4 | async-start | bytes 8388608 | tf_op jit(solution)/shard_map/all_to_all | solution.py:45
  215.3 42.4 %all-to-all-start.1 = ((bf16[128,32,64]{0,2,1:T(8,128)(2,1)}), bf16[128,32,64]{0,2,1:T(8,128)(2,1)S(1)}, u32[]{:S(2)}, u32[]{:S(2)}) async-start(bf16[128,32,64]{0,2,1:T(8,128)(2,1)} %bitcast.7), calls=%async_computation.2 | async-start | bytes 1048576 | tf_op jit(solution)/shard_map/all_to_all | solution.py:38
  231.9 8.9 %copy-start.3 = (bf16[128,7168]{1,0:T(8,128)(2,1)S(1)}, bf16[128,7168]{1,0:T(8,128)(2,1)}, u32[]{:S(2)}) copy-start(bf16[128,7168]{1,0:T(8,128)(2,1)} %param.8) | copy-start | bytes 5505028
  257.8 1.2 copy-start.8
  259.0 26.3 %all-to-all-start.4 = ((bf16[32,128,128]{1,2,0:T(8,128)(2,1)}), bf16[32,128,128]{1,2,0:T(8,128)(2,1)S(1)}, u32[]{:S(2)}, u32[]{:S(2)}) async-start(bf16[32,128,128]{1,2,0:T(8,128)(2,1)} %broadcast_in_dim.17), calls=%async_computation.5 | async-start | bytes 2097152 | tf_op jit(solution)/shard_map/all_to_all | solution.py:116
  285.3 29.7 %all-to-all-start = ((bf16[128,32,224]{0,2,1:T(8,128)(2,1)}), bf16[128,32,224]{0,2,1:T(8,128)(2,1)}, u32[]{:S(2)}, u32[]{:S(2)}) async-start(bf16[128,32,224]{0,2,1:T(8,128)(2,1)} %bitcast.3), calls=%async_computation.1 | async-start | bytes 3670016 | tf_op jit(solution)/shard_map/all_to_all | solution.py:35
  317.8 46.5 %collective-permute-start.3 = (bf16[128,1792]{1,0:T(8,128)(2,1)}, bf16[128,1792]{1,0:T(8,128)(2,1)}, u32[]{:S(2)}, u32[]{:S(2)}) collective-permute-start(bf16[128,1792]{1,0:T(8,128)(2,1)} %get-tuple-element.33), channel_id=1, source_target_pairs={{0,6},{1,7},{2,0},{3,1},{4,2},{5,3},{6,4},{7,5},{8,38},{9,39},{10,... | collective-permute-start | bytes 1376264 | tf_op jit(solution)/shard_map/ppermute | solution.py:92
  318.5 48.5 %collective-permute-start.2 = (bf16[128,1792]{1,0:T(8,128)(2,1)}, bf16[128,1792]{1,0:T(8,128)(2,1)}, u32[]{:S(2)}, u32[]{:S(2)}) collective-permute-start(bf16[128,1792]{1,0:T(8,128)(2,1)} %get-tuple-element.34), channel_id=1, source_target_pairs={{0,4},{1,5},{2,6},{3,7},{4,0},{5,1},{6,2},{7,3},{8,36},{9,37},{10,... | collective-permute-start | bytes 1376264 | tf_op jit(solution)/shard_map/ppermute | solution.py:92
  321.8 68.8 %collective-permute-start.1 = (bf16[128,1792]{1,0:T(8,128)(2,1)}, bf16[128,1792]{1,0:T(8,128)(2,1)}, u32[]{:S(2)}, u32[]{:S(2)}) collective-permute-start(bf16[128,1792]{1,0:T(8,128)(2,1)} %get-tuple-element.35), channel_id=1, source_target_pairs={{0,2},{1,3},{2,4},{3,5},{4,6},{5,7},{6,0},{7,1},{8,34},{9,35},{10,... | collective-permute-start | bytes 1376264 | tf_op jit(solution)/shard_map/ppermute | solution.py:92
  321.9 78.5 %collective-permute-start = (bf16[128,1792]{1,0:T(8,128)(2,1)}, bf16[128,1792]{1,0:T(8,128)(2,1)}, u32[]{:S(2)}, u32[]{:S(2)}) collective-permute-start(bf16[128,1792]{1,0:T(8,128)(2,1)} %get-tuple-element.32), channel_id=1, source_target_pairs={{0,0},{1,1},{2,2},{3,3},{4,4},{5,5},{6,6},{7,7},{8,32},{9,33},{10,... | collective-permute-start | bytes 1376264 | tf_op jit(solution)/shard_map/ppermute | solution.py:92
  345.6 4.5 %copy-start.7 = (f32[32,128,64]{1,2,0:T(8,128)S(1)}, f32[32,128,64]{1,2,0:T(8,128)}, u32[]{:S(2)}) copy-start(f32[32,128,64]{1,2,0:T(8,128)} %get-tuple-element.30) | copy-start | bytes 3145732
  345.6 4.5 %copy-start.9 = (bf16[128,32,64]{0,2,1:T(8,128)(2,1)S(1)}, bf16[128,32,64]{0,2,1:T(8,128)(2,1)}, u32[]{:S(2)}) copy-start(bf16[128,32,64]{0,2,1:T(8,128)(2,1)} %copy-done.8) | copy-start | bytes 1572868
  405.8 2.0 copy-start.2
  406.2 3.6 copy-start.1
Sparse Core Ops, SparseCore 0:
  10.2 73.1 all-gather.2
  85.0 21.1 all-gather.4
  127.6 73.3 reduce-scatter.1

commit v8 on v2

--- a/solution.py
+++ b/solution.py
@@ -92,9 +92,14 @@
                     dest_group = c // row_of_chip
                     pairs.append(((g * chip_count + c) * 2 + k, (dest_group * chip_count + dest_chip) * 2 + k))
         arrived.append(lax.ppermute(piece, ("grp", "chip", "core"), pairs))
-    arrived = jnp.stack(arrived)
-    order = (lane - jnp.arange(group_count)) % group_count
-    base_grad = jnp.take(arrived, order, axis=0).transpose(1, 0, 2).reshape(tok_rows, -1)
+    slots = []
+    for z in range(group_count):
+        source = (lane - z) % group_count
+        piece = arrived[group_count - 1]
+        for step in range(group_count - 2, -1, -1):
+            piece = jnp.where(source == step, arrived[step], piece)
+        slots.append(piece)
+    base_grad = jnp.concatenate(slots, axis=1)
     grad_rank = rank_sum[:, :ranks].astype(jnp.bfloat16)
     act_rank = rank_sum[:, ranks:].astype(jnp.bfloat16)
     grad_spread = (

time: 359 us -> 353 us (0.983)
  local copies, waits for them, and re-layouts: 76.9 us -> 73 us
where the time goes in v8:
time: 353 us; the launch traced here: 348 us
  waiting for transfers between devices  147 us (42%)
  local copies, waits for them, and re-layouts  73 us (21%)
  matrix products  42.1 us (12%)
  starting transfers between devices  37.4 us (11%)
  blocking collectives  31.5 us (9%)
  between operations  14.1 us (4%)
    all_to_all x1, waiting for transfers between devices, shards(): lax.all_to_all(adapter_down[chosen], SEQ, split_axis=1, concat_axis=3, ti...  50.1 us
    ppermute x4, waiting for transfers between devices, shards(): arrived.append(lax.ppermute(piece, ('grp', 'chip', 'core'), pairs))  41.6 us
    dot_general x1, matrix products, shards(): lax.dot_general(tokens_same_core, weight_pair, contract_last, preferred_e...  21.3 us
    all_to_all x1, waiting for transfers between devices, shards(): lax.all_to_all(hidden.reshape(tok_rows, shard_count, down_slab), SEQ, spl...  21 us
    all_to_all x1, blocking collectives, shards(): lax.all_to_all(grad_output.reshape(tok_rows, shard_count, up_slab), SEQ,...  16.4 us
    unnamed x26, local copies, waits for them, and re-layouts  15.8 us
    psum x1, blocking collectives, shards(): rank_sum = lax.psum(rank_part.astype(jnp.float32), 'grp')  15 us
    all_to_all x1, waiting for transfers between devices, shards(): lax.all_to_all(jnp.broadcast_to(rank_rows[None], (shard_count,) + rank_ro...  12.9 us
  transfers between devices with their start and end apart: 11, of which 9 were waited for; matrix products, arithmetic and copies ran while one was open for 23% of the time, Pallas kernels for 0%

profile of v8, /device:TPU:9, one launch (start us, length us, event | category | flops | bytes accessed | tf_op | source)
XLA Modules:
  0.0 348.1 jit_solution(11989922600307014734)
XLA Ops:
  14.1 4.6 %reshape.170 = bf16[32,2,8192]{2,1,0:T(2,128)(2,1)} reshape(bf16[32,4,64,64]{3,2,1,0:T(8,128)(2,1)} %bitcast.102) | data formatting | bytes 2097152
  18.7 8.9 %all-to-all-start = ((bf16[32,2,8192]{2,1,0:T(2,128)(2,1)}), bf16[32,2,8192]{2,1,0:T(2,128)(2,1)S(1)}, u32[]{:S(2)}, u32[]{:S(2)}) async-start(bf16[32,2,8192]{2,1,0:T(2,128)(2,1)} %reshape.170), calls=%async_computation | async-start | bytes 2097152 | tf_op jit(solution)/shard_map/all_to_all | solution.py:44
  30.4 4.8 %copy.69 = bf16[4,32,64,224]{3,2,0,1:T(8,128)(2,1)} copy(bf16[4,32,64,224]{3,2,1,0:T(8,128)(2,1)} %bitcast.99) | data formatting | bytes 7340032 | tf_op jit(solution)/shard_map/gather | solution.py:43
  35.2 7.6 %all-to-all-done = bf16[32,2,8192]{2,1,0:T(2,128)(2,1)S(1)} async-done(((bf16[32,2,8192]{2,1,0:T(2,128)(2,1)}), bf16[32,2,8192]{2,1,0:T(2,128)(2,1)S(1)}, u32[]{:S(2)}, u32[]{:S(2)}) %all-to-all-start) | async-done | bytes 1048608 | tf_op jit(solution)/shard_map/all_to_all | solution.py:44
  42.8 6.4 %all-to-all-start.1 = ((bf16[4,32,64,224]{3,2,0,1:T(8,128)(2,1)}), bf16[4,32,64,224]{3,2,0,1:T(8,128)(2,1)}, u32[]{:S(2)}, u32[]{:S(2)}) async-start(bf16[4,32,64,224]{3,2,0,1:T(8,128)(2,1)} %copy.69), calls=%async_computation.1 | async-start | bytes 8388608 | tf_op jit(solution)/shard_map/all_to_all | solution.py:43
  56.6 50.1 %all-to-all-done.1 = bf16[4,32,64,224]{3,2,0,1:T(8,128)(2,1)} async-done(((bf16[4,32,64,224]{3,2,0,1:T(8,128)(2,1)}), bf16[4,32,64,224]{3,2,0,1:T(8,128)(2,1)}, u32[]{:S(2)}, u32[]{:S(2)}) %all-to-all-start.1) | async-done | bytes 3670048 | tf_op jit(solution)/shard_map/all_to_all | solution.py:43
  106.7 6.6 %copy.70 = bf16[4,1,64,32,224]{4,3,2,0,1:T(8,128)(2,1)} copy(bf16[4,1,64,32,224]{4,2,0,3,1:T(8,128)(2,1)} %bitcast.12) | data formatting | bytes 7340032 | tf_op jit(solution)/shard_map/all_to_all | solution.py:43
  113.3 9.0 %reshape.134 = bf16[256,7168]{1,0:T(8,128)(2,1)} reshape(bf16[4,1,64,32,224]{4,3,2,0,1:T(8,128)(2,1)} %copy.70) | data formatting | bytes 7340032 | tf_op jit(solution)/shard_map/reshape | solution.py:46
  125.5 15.0 %psum.7 = bf16[128,128]{0,1:T(8,128)(2,1)S(1)} all-reduce(f32[128,128]{0,1:T(8,128)S(1)} %maximum_convert_fusion), channel_id=1, replica_groups=mesh['grp'=4,'chip'=16,'core'=2] {'grp'}, use_global_device_ids=true, to_apply=%region_3.4 | all-reduce | flops 16384 | bytes 98304 | tf_op jit(solution)/shard_map/psum | solution.py:63
  140.6 8.2 %all-gather.3.cloned.1.call-done = bf16[2048,2048]{1,0:T(8,128)(2,1)} async-done(((bf16[128,2048]{1,0:T(8,128)(2,1)}), bf16[2048,2048]{1,0:T(8,128)(2,1)}) %all-gather.3.cloned.1.call-update) | async-done | bytes 8388624 | tf_op jit(solution)/shard_map/all_gather | solution.py:62
  148.8 21.3 %convolution_convert_fusion = bf16[2048,1792]{1,0:T(8,128)(2,1)} fusion(bf16[2048,2048]{1,0:T(8,128)(2,1)} %all-gather.3.cloned.1.call-done, bf16[1792,2048]{1,0:T(8,128)(2,1)} %all-gather.5.cloned.1.call-done), kind=kOutput, calls=%fused_computation.4 | convolution fusion | flops 15036055552 | bytes 23068672 | tf_op jit(solution)/shard_map/dot_general | solution.py:67
  170.4 16.4 %all_to_all.65 = bf16[128,32,64]{0,2,1:T(8,128)(2,1)} all-to-all(bf16[128,32,64]{0,2,1:T(8,128)(2,1)S(1)} %bitcast.106), channel_id=1, replica_groups=mesh['grp'=4,'chip'=16,'core'=2] {'chip','core'}, dimensions={1} | all-to-all | bytes 1048576 | tf_op jit(solution)/shard_map/all_to_all | solution.py:38
  188.0 4.9 %all-to-all-start.4 = ((bf16[32,128,128]{1,2,0:T(8,128)(2,1)}), bf16[32,128,128]{1,2,0:T(8,128)(2,1)S(1)}, u32[]{:S(2)}, u32[]{:S(2)}) async-start(bf16[32,128,128]{1,2,0:T(8,128)(2,1)} %broadcast_in_dim.5), calls=%async_computation.5 | async-start | bytes 2097152 | tf_op jit(solution)/shard_map/all_to_all | solution.py:123
  195.2 12.9 %all-to-all-done.4 = bf16[32,128,128]{1,2,0:T(8,128)(2,1)S(1)} async-done(((bf16[32,128,128]{1,2,0:T(8,128)(2,1)}), bf16[32,128,128]{1,2,0:T(8,128)(2,1)S(1)}, u32[]{:S(2)}, u32[]{:S(2)}) %all-to-all-start.4) | async-done | bytes 1048608 | tf_op jit(solution)/shard_map/all_to_all | solution.py:123
  208.1 6.2 %all-to-all-start.2 = ((bf16[128,32,224]{0,2,1:T(8,128)(2,1)}), bf16[128,32,224]{0,2,1:T(8,128)(2,1)}, u32[]{:S(2)}, u32[]{:S(2)}) async-start(bf16[128,32,224]{0,2,1:T(8,128)(2,1)} %bitcast.16), calls=%async_computation.3 | async-start | bytes 3670016 | tf_op jit(solution)/shard_map/all_to_all | solution.py:35
  216.8 21.0 %all-to-all-done.2 = bf16[128,32,224]{0,2,1:T(8,128)(2,1)} async-done(((bf16[128,32,224]{0,2,1:T(8,128)(2,1)}), bf16[128,32,224]{0,2,1:T(8,128)(2,1)}, u32[]{:S(2)}, u32[]{:S(2)}) %all-to-all-start.2) | async-done | bytes 1835040 | tf_op jit(solution)/shard_map/all_to_all | solution.py:35
  237.8 4.5 %reduce-scatter.2.cloned.1.call-done = bf16[512,1792]{1,0:T(8,128)(2,1)} async-done(((bf16[2048,1792]{1,0:T(8,128)(2,1)}), bf16[512,1792]{1,0:T(8,128)(2,1)}) %reduce-scatter.2.cloned.1.call-update) | async-done | bytes 1835024 | tf_op jit(solution)/shard_map/reduce_scatter | solution.py:70
  264.0 4.8 %multiply_convert_fusion = bf16[32,4,64,224]{3,2,1,0:T(8,128)(2,1)} fusion(f32[32,4]{1,0:T(8,128)S(1)} %copy.76, f32[32,128,64]{1,2,0:T(8,128)S(1)} %get-tuple-element.33, f32[32,128,4]{1,2,0:T(4,128)S(1)} %fusion.7, bf16[32,128,224]{1,2,0:T(8,128)(2,1)} %bitcast.19), kind=kOutput, calls=%fused_computation.3 | convolution fusion | flops 475529216 | bytes 6619648 | tf_op jit(solution)/shard_map/stjr,stc->sjrc/dot_general | solution.py:136
  272.5 8.6 %reshape.143 = bf16[128,14336]{1,0:T(8,128)(2,1)} reshape(bf16[32,4,64,224]{3,2,1,0:T(8,128)(2,1)} %multiply_convert_fusion) | data formatting | bytes 7340032 | tf_op jit(solution)/shard_map/reshape | solution.py:143
  281.0 6.0 %copy.77 = bf16[14336,128]{1,0:T(8,128)(2,1)} copy(bf16[14336,128]{0,1:T(8,128)(2,1)} %bitcast.101) | data formatting | bytes 7340032 | tf_op jit(solution)/shard_map/dot_general | solution.py:141
  291.5 4.4 %copy.80 = f32[64,64,224]{2,1,0:T(8,128)} copy(f32[64,64,224]{2,0,1:T(8,128)S(1)} %fusion.11) | data formatting | bytes 7340032
  295.9 9.2 %collective-permute-done.1 = bf16[128,1792]{1,0:T(8,128)(2,1)} collective-permute-done((bf16[128,1792]{1,0:T(8,128)(2,1)}, bf16[128,1792]{1,0:T(8,128)(2,1)}, u32[]{:S(2)}, u32[]{:S(2)}) %collective-permute-start.1) | collective-permute-done | bytes 458784 | tf_op jit(solution)/shard_map/ppermute | solution.py:94
  305.1 24.2 %collective-permute-done.2 = bf16[128,1792]{1,0:T(8,128)(2,1)} collective-permute-done((bf16[128,1792]{1,0:T(8,128)(2,1)}, bf16[128,1792]{1,0:T(8,128)(2,1)}, u32[]{:S(2)}, u32[]{:S(2)}) %collective-permute-start.2) | collective-permute-done | bytes 458784 | tf_op jit(solution)/shard_map/ppermute | solution.py:94
  329.3 8.2 %collective-permute-done.3 = bf16[128,1792]{1,0:T(8,128)(2,1)} collective-permute-done((bf16[128,1792]{1,0:T(8,128)(2,1)}, bf16[128,1792]{1,0:T(8,128)(2,1)}, u32[]{:S(2)}, u32[]{:S(2)}) %collective-permute-start.3) | collective-permute-done | bytes 458784 | tf_op jit(solution)/shard_map/ppermute | solution.py:94
  (77 shorter events, 60.2 us)
Async XLA Ops:
  7.2 20.4 %copy-start = (bf16[64,64,224]{2,1,0:T(8,128)(2,1)S(1)}, bf16[64,64,224]{2,1,0:T(8,128)(2,1)}, u32[]{:S(2)}) copy-start(bf16[64,64,224]{2,1,0:T(8,128)(2,1)} %param.10) | copy-start | bytes 5505028
  7.2 1.5 copy-start.7
  7.2 1.6 copy-start.6
  7.2 133.4 %all-gather.5.cloned.1.call-start = ((), (), s32[]{:S(2)}) async-start(), calls=%async_computation.7 | async-start | bytes 11010048 | tf_op jit(solution)/shard_map/all_gather | solution.py:61
  7.9 140.9 %all-gather.3.cloned.1.call-start = ((), (), s32[]{:S(2)}) async-start(), calls=%async_computation.6 | async-start | bytes 8912896 | tf_op jit(solution)/shard_map/all_gather | solution.py:62
  18.7 24.1 %all-to-all-start = ((bf16[32,2,8192]{2,1,0:T(2,128)(2,1)}), bf16[32,2,8192]{2,1,0:T(2,128)(2,1)S(1)}, u32[]{:S(2)}, u32[]{:S(2)}) async-start(bf16[32,2,8192]{2,1,0:T(2,128)(2,1)} %reshape.170), calls=%async_computation | async-start | bytes 2097152 | tf_op jit(solution)/shard_map/all_to_all | solution.py:44
  35.2 14.0 %copy-start.8 = (s32[32,4]{0,1:T(4,128)S(1)}, s32[32,4]{0,1:T(4,128)}, u32[]{:S(2)}) copy-start(s32[32,4]{0,1:T(4,128)} %param.13) | copy-start | bytes 1540
  42.8 63.9 %all-to-all-start.1 = ((bf16[4,32,64,224]{3,2,0,1:T(8,128)(2,1)}), bf16[4,32,64,224]{3,2,0,1:T(8,128)(2,1)}, u32[]{:S(2)}, u32[]{:S(2)}) async-start(bf16[4,32,64,224]{3,2,0,1:T(8,128)(2,1)} %copy.69), calls=%async_computation.1 | async-start | bytes 8388608 | tf_op jit(solution)/shard_map/all_to_all | solution.py:43
  49.2 193.2 %reduce-scatter.2.cloned.1.call-start = ((), (), s32[]{:S(2)}) async-start(), calls=%async_computation.8 | async-start | bytes 9175040 | tf_op jit(solution)/shard_map/reduce_scatter | solution.py:70
  51.2 3.8 %copy-start.4 = (bf16[128,2048]{1,0:T(8,128)(2,1)S(1)}, bf16[128,2048]{1,0:T(8,128)(2,1)}, u32[]{:S(2)}) copy-start(bf16[128,2048]{1,0:T(8,128)(2,1)} %param.7) | copy-start | bytes 1572868
  113.3 9.0 %copy-start.3 = (bf16[128,7168]{1,0:T(8,128)(2,1)S(1)}, bf16[128,7168]{1,0:T(8,128)(2,1)}, u32[]{:S(2)}) copy-start(bf16[128,7168]{1,0:T(8,128)(2,1)} %param.8) | copy-start | bytes 5505028
  188.0 20.1 %all-to-all-start.4 = ((bf16[32,128,128]{1,2,0:T(8,128)(2,1)}), bf16[32,128,128]{1,2,0:T(8,128)(2,1)S(1)}, u32[]{:S(2)}, u32[]{:S(2)}) async-start(bf16[32,128,128]{1,2,0:T(8,128)(2,1)} %broadcast_in_dim.5), calls=%async_computation.5 | async-start | bytes 2097152 | tf_op jit(solution)/shard_map/all_to_all | solution.py:123
  208.1 29.7 %all-to-all-start.2 = ((bf16[128,32,224]{0,2,1:T(8,128)(2,1)}), bf16[128,32,224]{0,2,1:T(8,128)(2,1)}, u32[]{:S(2)}, u32[]{:S(2)}) async-start(bf16[128,32,224]{0,2,1:T(8,128)(2,1)} %bitcast.16), calls=%async_computation.3 | async-start | bytes 3670016 | tf_op jit(solution)/shard_map/all_to_all | solution.py:35
  253.1 15.7 %copy-start.5 = (bf16[4096,128]{1,0:T(8,128)(2,1)S(1)}, bf16[4096,128]{1,0:T(8,128)(2,1)}, u32[]{:S(2)}) copy-start(bf16[4096,128]{1,0:T(8,128)(2,1)} %copy.79) | copy-start | bytes 3145732
  253.1 42.9 %collective-permute-start = (bf16[128,1792]{1,0:T(8,128)(2,1)}, bf16[128,1792]{1,0:T(8,128)(2,1)}, u32[]{:S(2)}, u32[]{:S(2)}) collective-permute-start(bf16[128,1792]{1,0:T(8,128)(2,1)} %get-tuple-element.41), channel_id=1, source_target_pairs={{0,0},{1,1},{2,2},{3,3},{4,4},{5,5},{6,6},{7,7},{8,32},{9,33},{10,... | collective-permute-start | bytes 1376264 | tf_op jit(solution)/shard_map/ppermute | solution.py:94
  255.1 50.0 %collective-permute-start.1 = (bf16[128,1792]{1,0:T(8,128)(2,1)}, bf16[128,1792]{1,0:T(8,128)(2,1)}, u32[]{:S(2)}, u32[]{:S(2)}) collective-permute-start(bf16[128,1792]{1,0:T(8,128)(2,1)} %get-tuple-element.40), channel_id=1, source_target_pairs={{0,2},{1,3},{2,4},{3,5},{4,6},{5,7},{6,0},{7,1},{8,34},{9,35},{10,... | collective-permute-start | bytes 1376264 | tf_op jit(solution)/shard_map/ppermute | solution.py:94
  258.5 70.7 %collective-permute-start.2 = (bf16[128,1792]{1,0:T(8,128)(2,1)}, bf16[128,1792]{1,0:T(8,128)(2,1)}, u32[]{:S(2)}, u32[]{:S(2)}) collective-permute-start(bf16[128,1792]{1,0:T(8,128)(2,1)} %get-tuple-element.39), channel_id=1, source_target_pairs={{0,4},{1,5},{2,6},{3,7},{4,0},{5,1},{6,2},{7,3},{8,36},{9,37},{10,... | collective-permute-start | bytes 1376264 | tf_op jit(solution)/shard_map/ppermute | solution.py:94
  260.9 76.6 %collective-permute-start.3 = (bf16[128,1792]{1,0:T(8,128)(2,1)}, bf16[128,1792]{1,0:T(8,128)(2,1)}, u32[]{:S(2)}, u32[]{:S(2)}) collective-permute-start(bf16[128,1792]{1,0:T(8,128)(2,1)} %get-tuple-element.38), channel_id=1, source_target_pairs={{0,6},{1,7},{2,0},{3,1},{4,2},{5,3},{6,4},{7,5},{8,38},{9,39},{10,... | collective-permute-start | bytes 1376264 | tf_op jit(solution)/shard_map/ppermute | solution.py:94
  295.9 43.2 %copy-start.2 = (bf16[256,7168]{1,0:T(8,128)(2,1)S(1)}, bf16[256,7168]{1,0:T(8,128)(2,1)}, u32[]{:S(2)}) copy-start(bf16[256,7168]{1,0:T(8,128)(2,1)} %reshape.134) | copy-start | bytes 11010052
  339.1 2.4 copy-start.1
Sparse Core Ops, SparseCore 0:
  9.7 23.8 all-gather.4
  35.7 113.0 all-gather.2
  170.2 72.0 reduce-scatter.1

commit v9 on v2

--- a/solution.py
+++ b/solution.py
@@ -71,42 +71,8 @@
         partial_value.astype(jnp.bfloat16), "grp", scatter_dimension=0, tiled=True
     )
     quarter = quarter.reshape(group_count, tok_rows, quarter.shape[1])
-    quarter, hidden_cols, output_cols = lax.optimization_barrier(
-        (quarter, hidden_cols, output_cols)
-    )
-    chip_count = lax.axis_size("chip")
-    row_of_chip = chip_count // group_count
-    chip = lax.axis_index("chip")
-    group = lax.axis_index("grp")
-    core = lax.axis_index("core")
-    lane = chip % row_of_chip
-    arrived = []
-    for step in range(group_count):
-        piece = lax.dynamic_index_in_dim(quarter, (lane + step) % group_count, 0, keepdims=False)
-        pairs = []
-        for g in range(group_count):
-            for c in range(chip_count):
-                for k in range(2):
-                    z = c % row_of_chip
-                    dest_chip = g * row_of_chip + (z + step) % group_count
-                    dest_group = c // row_of_chip
-                    pairs.append(((g * chip_count + c) * 2 + k, (dest_group * chip_count + dest_chip) * 2 + k))
-        arrived.append(lax.ppermute(piece, ("grp", "chip", "core"), pairs))
-    arrived = jnp.stack(arrived)
-    order = (lane - jnp.arange(group_count)) % group_count
-    base_grad = jnp.take(arrived, order, axis=0).transpose(1, 0, 2).reshape(tok_rows, -1)
     grad_rank = rank_sum[:, :ranks].astype(jnp.bfloat16)
     act_rank = rank_sum[:, ranks:].astype(jnp.bfloat16)
-    grad_spread = (
-        (member[:, :, None] * lax.optimization_barrier(grad_rank).astype(jnp.float32)[:, None, :])
-        .reshape(tok_rows, job_slots * ranks)
-        .astype(jnp.bfloat16)
-    )
-    adapter_term = (
-        jnp.dot(grad_spread, down_stack, preferred_element_type=jnp.float32) * ADAPTER_SCALE
-    )
-    grad_hidden = (base_grad.astype(jnp.float32) + adapter_term).astype(jnp.bfloat16)
-
     all_positions = lax.broadcasted_iota(jnp.int32, (shard_count, tok_rows, job_slots), 1)
     all_ends = jnp.cumsum(job_count, axis=1)
     all_starts = all_ends - job_count
@@ -142,6 +108,46 @@
 
     grad_adapter_down = adapter_grad(rank_all[..., :ranks], hidden_cols)
     grad_adapter_up = adapter_grad(rank_all[..., ranks:], output_cols)
+    grad_adapter_up, quarter = lax.optimization_barrier((grad_adapter_up, quarter))
+    quarter, hidden_cols, output_cols = lax.optimization_barrier(
+        (quarter, hidden_cols, output_cols)
+    )
+    chip_count = lax.axis_size("chip")
+    row_of_chip = chip_count // group_count
+    chip = lax.axis_index("chip")
+    group = lax.axis_index("grp")
+    core = lax.axis_index("core")
+    lane = chip % row_of_chip
+    arrived = []
+    for step in range(group_count):
+        piece = lax.dynamic_index_in_dim(quarter, (lane + step) % group_count, 0, keepdims=False)
+        pairs = []
+        for g in range(group_count):
+            for c in range(chip_count):
+                for k in range(2):
+                    z = c % row_of_chip
+                    dest_chip = g * row_of_chip + (z + step) % group_count
+                    dest_group = c // row_of_chip
+                    pairs.append(((g * chip_count + c) * 2 + k, (dest_group * chip_count + dest_chip) * 2 + k))
+        arrived.append(lax.ppermute(piece, ("grp", "chip", "core"), pairs))
+    slots = []
+    for z in range(group_count):
+        source = (lane - z) % group_count
+        piece = arrived[group_count - 1]
+        for step in range(group_count - 2, -1, -1):
+            piece = jnp.where(source == step, arrived[step], piece)
+        slots.append(piece)
+    base_grad = jnp.concatenate(slots, axis=1)
+    grad_spread = (
+        (member[:, :, None] * lax.optimization_barrier(grad_rank).astype(jnp.float32)[:, None, :])
+        .reshape(tok_rows, job_slots * ranks)
+        .astype(jnp.bfloat16)
+    )
+    adapter_term = (
+        jnp.dot(grad_spread, down_stack, preferred_element_type=jnp.float32) * ADAPTER_SCALE
+    )
+    grad_hidden = (base_grad.astype(jnp.float32) + adapter_term).astype(jnp.bfloat16)
+
     return (grad_hidden, grad_adapter_down, grad_adapter_up)
 
 

time: 359 us -> 345 us (0.961)
  waiting for transfers between devices: 147 us -> 140 us
  local copies, waits for them, and re-layouts: 76.9 us -> 72.6 us
    all_to_all x1, waiting for transfers between devices: 21 us -> 0.01 us  [shards(): lax.all_to_all(hidden.reshape(tok_rows, shard_count, down_slab), SEQ, spl...]
    reduce_scatter x1, waiting for transfers between devices: 4.54 us -> 17.3 us  [shards(): lax.psum_scatter(partial_value.astype(jnp.bfloat16), 'grp', scatter_dimen...]
  transfers between devices with their start and end apart: 11 -> 11, of which waited for: 9 -> 8; matrix products, arithmetic and copies ran while one was open for 23% -> 27% of each run, Pallas kernels for 0% -> 0%
where the time goes in v9:
time: 345 us; the launch traced here: 340 us
  waiting for transfers between devices  140 us (41%)
  local copies, waits for them, and re-layouts  72.6 us (21%)
  matrix products  42 us (12%)
  starting transfers between devices  37.3 us (11%)
  blocking collectives  31.5 us (9%)
  between operations  14.2 us (4%)
    all_to_all x1, waiting for transfers between devices, shards(): lax.all_to_all(adapter_down[chosen], SEQ, split_axis=1, concat_axis=3, ti...  50.1 us
    ppermute x4, waiting for transfers between devices, shards(): arrived.append(lax.ppermute(piece, ('grp', 'chip', 'core'), pairs))  42.7 us
    dot_general x1, matrix products, shards(): lax.dot_general(tokens_same_core, weight_pair, contract_last, preferred_e...  21.3 us
    reduce_scatter x1, waiting for transfers between devices, shards(): lax.psum_scatter(partial_value.astype(jnp.bfloat16), 'grp', scatter_dimen...  17.3 us
    all_to_all x1, blocking collectives, shards(): lax.all_to_all(grad_output.reshape(tok_rows, shard_count, up_slab), SEQ,...  16.4 us
    unnamed x26, local copies, waits for them, and re-layouts  16.3 us
    psum x1, blocking collectives, shards(): rank_sum = lax.psum(rank_part.astype(jnp.float32), 'grp')  15 us
    all_to_all x1, waiting for transfers between devices, shards(): lax.all_to_all(jnp.broadcast_to(rank_rows[None], (shard_count,) + rank_ro...  12.4 us
  transfers between devices with their start and end apart: 11, of which 8 were waited for; matrix products, arithmetic and copies ran while one was open for 27% of the time, Pallas kernels for 0%

profile of v9, /device:TPU:9, one launch (start us, length us, event | category | flops | bytes accessed | tf_op | source)
XLA Modules:
  0.0 339.9 jit_solution(8063041235472422713)
XLA Ops:
  14.1 4.6 %reshape.170 = bf16[32,2,8192]{2,1,0:T(2,128)(2,1)} reshape(bf16[32,4,64,64]{3,2,1,0:T(8,128)(2,1)} %bitcast.104) | data formatting | bytes 2097152
  18.7 8.9 %all-to-all-start = ((bf16[32,2,8192]{2,1,0:T(2,128)(2,1)}), bf16[32,2,8192]{2,1,0:T(2,128)(2,1)S(1)}, u32[]{:S(2)}, u32[]{:S(2)}) async-start(bf16[32,2,8192]{2,1,0:T(2,128)(2,1)} %reshape.170), calls=%async_computation | async-start | bytes 2097152 | tf_op jit(solution)/shard_map/all_to_all | solution.py:44
  30.4 4.8 %copy.72 = bf16[4,32,64,224]{3,2,0,1:T(8,128)(2,1)} copy(bf16[4,32,64,224]{3,2,1,0:T(8,128)(2,1)} %bitcast.101) | data formatting | bytes 7340032 | tf_op jit(solution)/shard_map/gather | solution.py:43
  35.2 7.6 %all-to-all-done = bf16[32,2,8192]{2,1,0:T(2,128)(2,1)S(1)} async-done(((bf16[32,2,8192]{2,1,0:T(2,128)(2,1)}), bf16[32,2,8192]{2,1,0:T(2,128)(2,1)S(1)}, u32[]{:S(2)}, u32[]{:S(2)}) %all-to-all-start) | async-done | bytes 1048608 | tf_op jit(solution)/shard_map/all_to_all | solution.py:44
  42.8 6.4 %all-to-all-start.1 = ((bf16[4,32,64,224]{3,2,0,1:T(8,128)(2,1)}), bf16[4,32,64,224]{3,2,0,1:T(8,128)(2,1)}, u32[]{:S(2)}, u32[]{:S(2)}) async-start(bf16[4,32,64,224]{3,2,0,1:T(8,128)(2,1)} %copy.72), calls=%async_computation.1 | async-start | bytes 8388608 | tf_op jit(solution)/shard_map/all_to_all | solution.py:43
  56.6 50.1 %all-to-all-done.1 = bf16[4,32,64,224]{3,2,0,1:T(8,128)(2,1)} async-done(((bf16[4,32,64,224]{3,2,0,1:T(8,128)(2,1)}), bf16[4,32,64,224]{3,2,0,1:T(8,128)(2,1)}, u32[]{:S(2)}, u32[]{:S(2)}) %all-to-all-start.1) | async-done | bytes 3670048 | tf_op jit(solution)/shard_map/all_to_all | solution.py:43
  106.7 6.6 %copy.73 = bf16[4,1,64,32,224]{4,3,2,0,1:T(8,128)(2,1)} copy(bf16[4,1,64,32,224]{4,2,0,3,1:T(8,128)(2,1)} %bitcast.13) | data formatting | bytes 7340032 | tf_op jit(solution)/shard_map/all_to_all | solution.py:43
  113.3 9.0 %reshape.134 = bf16[256,7168]{1,0:T(8,128)(2,1)} reshape(bf16[4,1,64,32,224]{4,3,2,0,1:T(8,128)(2,1)} %copy.73) | data formatting | bytes 7340032 | tf_op jit(solution)/shard_map/reshape | solution.py:46
  125.5 15.0 %psum.7 = bf16[128,128]{0,1:T(8,128)(2,1)S(1)} all-reduce(f32[128,128]{0,1:T(8,128)S(1)} %maximum_convert_fusion), channel_id=1, replica_groups=mesh['grp'=4,'chip'=16,'core'=2] {'grp'}, use_global_device_ids=true, to_apply=%region_4.5 | all-reduce | flops 16384 | bytes 98304 | tf_op jit(solution)/shard_map/psum | solution.py:63
  140.6 8.2 %all-gather.3.cloned.1.call-done = bf16[2048,2048]{1,0:T(8,128)(2,1)} async-done(((bf16[128,2048]{1,0:T(8,128)(2,1)}), bf16[2048,2048]{1,0:T(8,128)(2,1)}) %all-gather.3.cloned.1.call-update) | async-done | bytes 8388624 | tf_op jit(solution)/shard_map/all_gather | solution.py:62
  148.8 21.3 %convolution_convert_fusion = bf16[2048,1792]{1,0:T(8,128)(2,1)} fusion(bf16[2048,2048]{1,0:T(8,128)(2,1)} %all-gather.3.cloned.1.call-done, bf16[1792,2048]{1,0:T(8,128)(2,1)} %all-gather.5.cloned.1.call-done), kind=kOutput, calls=%fused_computation.4 | convolution fusion | flops 15036055552 | bytes 23068672 | tf_op jit(solution)/shard_map/dot_general | solution.py:67
  170.4 16.4 %all_to_all.65 = bf16[128,32,64]{0,2,1:T(8,128)(2,1)} all-to-all(bf16[128,32,64]{0,2,1:T(8,128)(2,1)S(1)} %bitcast.108), channel_id=1, replica_groups=mesh['grp'=4,'chip'=16,'core'=2] {'chip','core'}, dimensions={1} | all-to-all | bytes 1048576 | tf_op jit(solution)/shard_map/all_to_all | solution.py:38
  188.0 4.9 %all-to-all-start.2 = ((bf16[32,128,128]{1,2,0:T(8,128)(2,1)}), bf16[32,128,128]{1,2,0:T(8,128)(2,1)S(1)}, u32[]{:S(2)}, u32[]{:S(2)}) async-start(bf16[32,128,128]{1,2,0:T(8,128)(2,1)} %broadcast_in_dim.5), calls=%async_computation.2 | async-start | bytes 2097152 | tf_op jit(solution)/shard_map/all_to_all | solution.py:84
  195.7 12.4 %all-to-all-done.2 = bf16[32,128,128]{1,2,0:T(8,128)(2,1)S(1)} async-done(((bf16[32,128,128]{1,2,0:T(8,128)(2,1)}), bf16[32,128,128]{1,2,0:T(8,128)(2,1)S(1)}, u32[]{:S(2)}, u32[]{:S(2)}) %all-to-all-start.2) | async-done | bytes 1048608 | tf_op jit(solution)/shard_map/all_to_all | solution.py:84
  208.1 6.2 %all-to-all-start.4 = ((bf16[128,32,224]{0,2,1:T(8,128)(2,1)}), bf16[128,32,224]{0,2,1:T(8,128)(2,1)}, u32[]{:S(2)}, u32[]{:S(2)}) async-start(bf16[128,32,224]{0,2,1:T(8,128)(2,1)} %bitcast.27), calls=%async_computation.5 | async-start | bytes 3670016 | tf_op jit(solution)/shard_map/all_to_all | solution.py:35
  225.0 17.3 %reduce-scatter.2.cloned.1.call-done = bf16[512,1792]{1,0:T(8,128)(2,1)} async-done(((bf16[2048,1792]{1,0:T(8,128)(2,1)}), bf16[512,1792]{1,0:T(8,128)(2,1)}) %reduce-scatter.2.cloned.1.call-update) | async-done | bytes 1835024 | tf_op jit(solution)/shard_map/reduce_scatter | solution.py:70
  255.9 4.8 %multiply_convert_fusion = bf16[32,4,64,224]{3,2,1,0:T(8,128)(2,1)} fusion(f32[32,4]{1,0:T(8,128)S(1)} %copy.75, f32[32,128,64]{1,2,0:T(8,128)S(1)} %get-tuple-element.32, f32[32,128,4]{1,2,0:T(4,128)S(1)} %fusion.7, bf16[128,32,224]{0,2,1:T(8,128)(2,1)} %all-to-all-done.4), kind=kOutput, calls=%fused_computation.3 | convolution fusion | flops 475529216 | bytes 6619648 | tf_op jit(solution)/shard_map/stjr,stc->sjrc/dot_general | solution.py:97
  260.7 8.6 %reshape.144 = bf16[128,14336]{1,0:T(8,128)(2,1)} reshape(bf16[32,4,64,224]{3,2,1,0:T(8,128)(2,1)} %multiply_convert_fusion) | data formatting | bytes 7340032 | tf_op jit(solution)/shard_map/reshape | solution.py:104
  269.3 6.0 %copy.79 = bf16[14336,128]{1,0:T(8,128)(2,1)} copy(bf16[14336,128]{0,1:T(8,128)(2,1)} %bitcast.103) | data formatting | bytes 7340032 | tf_op jit(solution)/shard_map/dot_general | solution.py:102
  275.3 4.4 %fusion.9 = f32[64,64,224]{2,0,1:T(8,128)S(1)} fusion(bf16[64,224,128]{2,1,0:T(8,128)(2,1)} %bitcast.102, s32[128]{0:T(128)S(1)} %eq.69), kind=kOutput, calls=%fused_computation.40 | convolution fusion | flops 234905600 | bytes 7340544 | tf_op jit(solution)/shard_map/dot_general | solution.py:102
  279.7 4.4 %copy.80 = f32[64,64,224]{2,1,0:T(8,128)} copy(f32[64,64,224]{2,0,1:T(8,128)S(1)} %fusion.9) | data formatting | bytes 7340032
  286.7 10.3 %collective-permute-done.1 = bf16[128,1792]{1,0:T(8,128)(2,1)} collective-permute-done((bf16[128,1792]{1,0:T(8,128)(2,1)}, bf16[128,1792]{1,0:T(8,128)(2,1)}, u32[]{:S(2)}, u32[]{:S(2)}) %collective-permute-start.1) | collective-permute-done | bytes 458784 | tf_op jit(solution)/shard_map/ppermute | solution.py:132
  297.0 24.1 %collective-permute-done.2 = bf16[128,1792]{1,0:T(8,128)(2,1)} collective-permute-done((bf16[128,1792]{1,0:T(8,128)(2,1)}, bf16[128,1792]{1,0:T(8,128)(2,1)}, u32[]{:S(2)}, u32[]{:S(2)}) %collective-permute-start.2) | collective-permute-done | bytes 458784 | tf_op jit(solution)/shard_map/ppermute | solution.py:132
  321.2 8.2 %collective-permute-done.3 = bf16[128,1792]{1,0:T(8,128)(2,1)} collective-permute-done((bf16[128,1792]{1,0:T(8,128)(2,1)}, bf16[128,1792]{1,0:T(8,128)(2,1)}, u32[]{:S(2)}, u32[]{:S(2)}) %collective-permute-start.3) | collective-permute-done | bytes 458784 | tf_op jit(solution)/shard_map/ppermute | solution.py:132
  (77 shorter events, 55.2 us)
Async XLA Ops:
  7.2 20.4 %copy-start = (bf16[64,64,224]{2,1,0:T(8,128)(2,1)S(1)}, bf16[64,64,224]{2,1,0:T(8,128)(2,1)}, u32[]{:S(2)}) copy-start(bf16[64,64,224]{2,1,0:T(8,128)(2,1)} %param.10) | copy-start | bytes 5505028
  7.2 1.5 copy-start.7
  7.2 1.6 copy-start.5
  7.2 133.4 %all-gather.5.cloned.1.call-start = ((), (), s32[]{:S(2)}) async-start(), calls=%async_computation.7 | async-start | bytes 11010048 | tf_op jit(solution)/shard_map/all_gather | solution.py:61
  7.9 140.9 %all-gather.3.cloned.1.call-start = ((), (), s32[]{:S(2)}) async-start(), calls=%async_computation.6 | async-start | bytes 8912896 | tf_op jit(solution)/shard_map/all_gather | solution.py:62
  18.7 24.1 %all-to-all-start = ((bf16[32,2,8192]{2,1,0:T(2,128)(2,1)}), bf16[32,2,8192]{2,1,0:T(2,128)(2,1)S(1)}, u32[]{:S(2)}, u32[]{:S(2)}) async-start(bf16[32,2,8192]{2,1,0:T(2,128)(2,1)} %reshape.170), calls=%async_computation | async-start | bytes 2097152 | tf_op jit(solution)/shard_map/all_to_all | solution.py:44
  35.2 14.0 %copy-start.8 = (s32[32,4]{0,1:T(4,128)S(1)}, s32[32,4]{0,1:T(4,128)}, u32[]{:S(2)}) copy-start(s32[32,4]{0,1:T(4,128)} %param.13) | copy-start | bytes 1540
  42.8 63.9 %all-to-all-start.1 = ((bf16[4,32,64,224]{3,2,0,1:T(8,128)(2,1)}), bf16[4,32,64,224]{3,2,0,1:T(8,128)(2,1)}, u32[]{:S(2)}, u32[]{:S(2)}) async-start(bf16[4,32,64,224]{3,2,0,1:T(8,128)(2,1)} %copy.72), calls=%async_computation.1 | async-start | bytes 8388608 | tf_op jit(solution)/shard_map/all_to_all | solution.py:43
  49.2 193.2 %reduce-scatter.2.cloned.1.call-start = ((), (), s32[]{:S(2)}) async-start(), calls=%async_computation.8 | async-start | bytes 9175040 | tf_op jit(solution)/shard_map/reduce_scatter | solution.py:70
  51.2 3.8 %copy-start.4 = (bf16[128,2048]{1,0:T(8,128)(2,1)S(1)}, bf16[128,2048]{1,0:T(8,128)(2,1)}, u32[]{:S(2)}) copy-start(bf16[128,2048]{1,0:T(8,128)(2,1)} %param.7) | copy-start | bytes 1572868
  113.3 9.0 %copy-start.3 = (bf16[128,7168]{1,0:T(8,128)(2,1)S(1)}, bf16[128,7168]{1,0:T(8,128)(2,1)}, u32[]{:S(2)}) copy-start(bf16[128,7168]{1,0:T(8,128)(2,1)} %param.8) | copy-start | bytes 5505028
  188.0 20.1 %all-to-all-start.2 = ((bf16[32,128,128]{1,2,0:T(8,128)(2,1)}), bf16[32,128,128]{1,2,0:T(8,128)(2,1)S(1)}, u32[]{:S(2)}, u32[]{:S(2)}) async-start(bf16[32,128,128]{1,2,0:T(8,128)(2,1)} %broadcast_in_dim.5), calls=%async_computation.2 | async-start | bytes 2097152 | tf_op jit(solution)/shard_map/all_to_all | solution.py:84
  208.1 47.8 %all-to-all-start.4 = ((bf16[128,32,224]{0,2,1:T(8,128)(2,1)}), bf16[128,32,224]{0,2,1:T(8,128)(2,1)}, u32[]{:S(2)}, u32[]{:S(2)}) async-start(bf16[128,32,224]{0,2,1:T(8,128)(2,1)} %bitcast.27), calls=%async_computation.5 | async-start | bytes 3670016 | tf_op jit(solution)/shard_map/all_to_all | solution.py:35
  215.0 1.0 copy-start.6
  245.1 41.6 %collective-permute-start = (bf16[128,1792]{1,0:T(8,128)(2,1)}, bf16[128,1792]{1,0:T(8,128)(2,1)}, u32[]{:S(2)}, u32[]{:S(2)}) collective-permute-start(bf16[128,1792]{1,0:T(8,128)(2,1)} %get-tuple-element.41), channel_id=1, source_target_pairs={{0,0},{1,1},{2,2},{3,3},{4,4},{5,5},{6,6},{7,7},{8,32},{9,33},{10,... | collective-permute-start | bytes 1376264 | tf_op jit(solution)/shard_map/ppermute | solution.py:132
  247.0 50.0 %collective-permute-start.1 = (bf16[128,1792]{1,0:T(8,128)(2,1)}, bf16[128,1792]{1,0:T(8,128)(2,1)}, u32[]{:S(2)}, u32[]{:S(2)}) collective-permute-start(bf16[128,1792]{1,0:T(8,128)(2,1)} %get-tuple-element.40), channel_id=1, source_target_pairs={{0,2},{1,3},{2,4},{3,5},{4,6},{5,7},{6,0},{7,1},{8,34},{9,35},{10,... | collective-permute-start | bytes 1376264 | tf_op jit(solution)/shard_map/ppermute | solution.py:132
  250.4 70.7 %collective-permute-start.2 = (bf16[128,1792]{1,0:T(8,128)(2,1)}, bf16[128,1792]{1,0:T(8,128)(2,1)}, u32[]{:S(2)}, u32[]{:S(2)}) collective-permute-start(bf16[128,1792]{1,0:T(8,128)(2,1)} %get-tuple-element.39), channel_id=1, source_target_pairs={{0,4},{1,5},{2,6},{3,7},{4,0},{5,1},{6,2},{7,3},{8,36},{9,37},{10,... | collective-permute-start | bytes 1376264 | tf_op jit(solution)/shard_map/ppermute | solution.py:132
  252.7 76.6 %collective-permute-start.3 = (bf16[128,1792]{1,0:T(8,128)(2,1)}, bf16[128,1792]{1,0:T(8,128)(2,1)}, u32[]{:S(2)}, u32[]{:S(2)}) collective-permute-start(bf16[128,1792]{1,0:T(8,128)(2,1)} %get-tuple-element.38), channel_id=1, source_target_pairs={{0,6},{1,7},{2,0},{3,1},{4,2},{5,3},{6,4},{7,5},{8,38},{9,39},{10,... | collective-permute-start | bytes 1376264 | tf_op jit(solution)/shard_map/ppermute | solution.py:132
  284.2 46.9 %copy-start.2 = (bf16[256,7168]{1,0:T(8,128)(2,1)S(1)}, bf16[256,7168]{1,0:T(8,128)(2,1)}, u32[]{:S(2)}) copy-start(bf16[256,7168]{1,0:T(8,128)(2,1)} %reshape.134) | copy-start | bytes 11010052
  331.0 2.4 copy-start.1
Sparse Core Ops, SparseCore 0:
  9.7 23.8 all-gather.4
  35.7 113.0 all-gather.2
  170.2 72.0 reduce-scatter.1

commit v10 on v9

--- a/solution.py
+++ b/solution.py
@@ -39,8 +39,10 @@
         grad_output.reshape(tok_rows, shard_count, up_slab), SEQ, split_axis=1, concat_axis=0, tiled=True
     ).reshape(shard_count, tok_rows, up_slab)
     chosen = job_tenant.T
+    tokens_same_core = lax.all_gather(grad_output, "chip", axis=0, tiled=True)
+    down_picked, tokens_same_core = lax.optimization_barrier((adapter_down[chosen], tokens_same_core))
     fetched_down, fetched_up = (
-        lax.all_to_all(adapter_down[chosen], SEQ, split_axis=1, concat_axis=3, tiled=True),
+        lax.all_to_all(down_picked, SEQ, split_axis=1, concat_axis=3, tiled=True),
         lax.all_to_all(adapter_up[chosen], SEQ, split_axis=1, concat_axis=3, tiled=True),
     )
     down_stack = fetched_down.reshape(job_slots * ranks, shard_count * down_slab)
@@ -59,11 +61,7 @@
         jnp.bfloat16
     )
     weight_pair = lax.all_gather(down_weight, "core", axis=0, tiled=True)
-    tokens_same_core = lax.all_gather(grad_output, "chip", axis=0, tiled=True)
     rank_sum = lax.psum(rank_part.astype(jnp.float32), "grp")
-    tokens_same_core, weight_pair, rank_sum = lax.optimization_barrier(
-        (tokens_same_core, weight_pair, rank_sum)
-    )
     partial_value = lax.dot_general(
         tokens_same_core, weight_pair, contract_last, preferred_element_type=jnp.float32
     )

time: 345 us -> 436 us (1.26)
  waiting for transfers between devices: 140 us -> 236 us
  blocking collectives: 31.5 us -> 13.7 us
  starting transfers between devices: 37.3 us -> 50.8 us
    all_to_all x1, waiting for transfers between devices: 0.01 us -> 78.2 us  [shards(): lax.all_to_all(hidden.reshape(tok_rows, shard_count, down_slab), SEQ, spl...]
    all_gather x1, waiting for transfers between devices: 8.24 us -> 71.7 us  [shards(): tokens_same_core = lax.all_gather(grad_output, 'chip', axis=0, tiled=True)]
    ppermute x4, waiting for transfers between devices: 42.7 us -> 0.01 us  [shards(): arrived.append(lax.ppermute(piece, ('grp', 'chip', 'core'), pairs))]
    all_gather x1, waiting for transfers between devices: 0.02 us -> 22.8 us  [shards(): weight_pair = lax.all_gather(down_weight, 'core', axis=0, tiled=True)]
    reduce_scatter x1, waiting for transfers between devices: 17.3 us -> 0.02 us  [shards(): lax.psum_scatter(partial_value.astype(jnp.bfloat16), 'grp', scatter_dimen...]
    all_to_all x1 -> x0, blocking collectives: 16.4 us -> none  [shards(): lax.all_to_all(grad_output.reshape(tok_rows, shard_count, up_slab), SEQ,...]
    all_to_all x1 -> x2, waiting for transfers between devices: 50.1 us -> 38.7 us  [the longest x1 38.7 us: shards(): lax.all_to_all(down_picked, SEQ, split_axis=1, concat_axis=3, tiled=True)]
    all_to_all x1 -> x2, starting transfers between devices: 6.36 us -> 16.3 us  [the longest x1 9.97 us: shards(): lax.all_to_all(grad_output.reshape(tok_rows, shard_count, up_slab), SEQ,...]
  transfers between devices with their start and end apart: 11 -> 12, of which waited for: 8 -> 6; matrix products, arithmetic and copies ran while one was open for 27% -> 21% of each run, Pallas kernels for 0% -> 0%
where the time goes in v10:
time: 436 us; the launch traced here: 434 us
  waiting for transfers between devices  236 us (54%)
  local copies, waits for them, and re-layouts  75.2 us (17%)
  starting transfers between devices  50.8 us (12%)
  matrix products  42 us (10%)
  between operations  14.2 us (3%)
  blocking collectives  13.7 us (3%)
    all_to_all x1, waiting for transfers between devices, shards(): lax.all_to_all(hidden.reshape(tok_rows, shard_count, down_slab), SEQ, spl...  78.2 us
    all_gather x1, waiting for transfers between devices, shards(): tokens_same_core = lax.all_gather(grad_output, 'chip', axis=0, tiled=True)  71.7 us
    all_to_all x1, waiting for transfers between devices, shards(): lax.all_to_all(down_picked, SEQ, split_axis=1, concat_axis=3, tiled=True)  38.7 us
    all_gather x1, waiting for transfers between devices, shards(): weight_pair = lax.all_gather(down_weight, 'core', axis=0, tiled=True)  22.8 us
    unnamed x30, local copies, waits for them, and re-layouts  21.7 us
    dot_general x1, matrix products, shards(): lax.dot_general(tokens_same_core, weight_pair, contract_last, preferred_e...  21.3 us
    psum x1, blocking collectives, shards(): rank_sum = lax.psum(rank_part.astype(jnp.float32), 'grp')  13.7 us
    all_to_all x1, waiting for transfers between devices, shards(): lax.all_to_all(jnp.broadcast_to(rank_rows[None], (shard_count,) + rank_ro...  12.4 us
  transfers between devices with their start and end apart: 12, of which 6 were waited for; matrix products, arithmetic and copies ran while one was open for 21% of the time, Pallas kernels for 0%

profile of v10, /device:TPU:9, one launch (start us, length us, event | category | flops | bytes accessed | tf_op | source)
XLA Modules:
  0.0 434.2 jit_solution(6582278886305879678)
XLA Ops:
  11.7 71.7 %all-gather.3.cloned.1.call-done = bf16[2048,2048]{1,0:T(8,128)(2,1)} async-done(((bf16[128,2048]{1,0:T(8,128)(2,1)}), bf16[2048,2048]{1,0:T(8,128)(2,1)}) %all-gather.3.cloned.1.call-update) | async-done | bytes 8388624 | tf_op jit(solution)/shard_map/all_gather | solution.py:42
  83.4 22.8 %all-gather.5.cloned.1.call-done = bf16[1792,2048]{1,0:T(8,128)(2,1)} async-done(((bf16[896,2048]{1,0:T(8,128)(2,1)}), bf16[1792,2048]{1,0:T(8,128)(2,1)}) %all-gather.5.cloned.1.call-update) | async-done | bytes 7340048 | tf_op jit(solution)/shard_map/all_gather | solution.py:63
  106.2 21.3 %convolution_convert_fusion = bf16[2048,1792]{1,0:T(8,128)(2,1)} fusion(bf16[2048,2048]{1,0:T(8,128)(2,1)} %all-gather.3.cloned.1.call-done, bf16[1792,2048]{1,0:T(8,128)(2,1)} %all-gather.5.cloned.1.call-done), kind=kOutput, calls=%fused_computation.4 | convolution fusion | flops 15036055552 | bytes 23068672 | tf_op jit(solution)/shard_map/dot_general | solution.py:65
  131.2 4.6 %reshape.170 = bf16[32,2,8192]{2,1,0:T(2,128)(2,1)} reshape(bf16[32,4,64,64]{3,2,1,0:T(8,128)(2,1)} %bitcast.105) | data formatting | bytes 2097152
  135.8 7.4 %all-to-all-start = ((bf16[32,2,8192]{2,1,0:T(2,128)(2,1)}), bf16[32,2,8192]{2,1,0:T(2,128)(2,1)S(1)}, u32[]{:S(2)}, u32[]{:S(2)}) async-start(bf16[32,2,8192]{2,1,0:T(2,128)(2,1)} %reshape.170), calls=%async_computation | async-start | bytes 2097152 | tf_op jit(solution)/shard_map/all_to_all | solution.py:46
  143.2 4.7 %copy.72 = bf16[4,32,64,224]{3,2,0,1:T(8,128)(2,1)} copy(bf16[4,32,64,224]{3,2,1,0:T(8,128)(2,1)} %bitcast.101) | data formatting | bytes 7340032 | tf_op jit(solution)/shard_map/optimization_barrier | solution.py:43
  148.0 10.4 %all-to-all-done = bf16[32,2,8192]{2,1,0:T(2,128)(2,1)S(1)} async-done(((bf16[32,2,8192]{2,1,0:T(2,128)(2,1)}), bf16[32,2,8192]{2,1,0:T(2,128)(2,1)S(1)}, u32[]{:S(2)}, u32[]{:S(2)}) %all-to-all-start) | async-done | bytes 1048608 | tf_op jit(solution)/shard_map/all_to_all | solution.py:46
  159.4 6.4 %all-to-all-start.1 = ((bf16[4,32,64,224]{3,2,0,1:T(8,128)(2,1)}), bf16[4,32,64,224]{3,2,0,1:T(8,128)(2,1)}, u32[]{:S(2)}, u32[]{:S(2)}) async-start(bf16[4,32,64,224]{3,2,0,1:T(8,128)(2,1)} %copy.72), calls=%async_computation.1 | async-start | bytes 8388608 | tf_op jit(solution)/shard_map/all_to_all | solution.py:45
  176.6 38.7 %all-to-all-done.1 = bf16[4,32,64,224]{3,2,0,1:T(8,128)(2,1)} async-done(((bf16[4,32,64,224]{3,2,0,1:T(8,128)(2,1)}), bf16[4,32,64,224]{3,2,0,1:T(8,128)(2,1)}, u32[]{:S(2)}, u32[]{:S(2)}) %all-to-all-start.1) | async-done | bytes 3670048 | tf_op jit(solution)/shard_map/all_to_all | solution.py:45
  215.3 10.0 %all-to-all-start.3 = ((bf16[128,32,64]{0,2,1:T(8,128)(2,1)}), bf16[128,32,64]{0,2,1:T(8,128)(2,1)S(1)}, u32[]{:S(2)}, u32[]{:S(2)}) async-start(bf16[128,32,64]{0,2,1:T(8,128)(2,1)} %bitcast.18), calls=%async_computation.3 | async-start | bytes 1048576 | tf_op jit(solution)/shard_map/all_to_all | solution.py:38
  225.3 6.6 %copy.73 = bf16[4,1,64,32,224]{4,3,2,0,1:T(8,128)(2,1)} copy(bf16[4,1,64,32,224]{4,2,0,3,1:T(8,128)(2,1)} %bitcast.13) | data formatting | bytes 7340032 | tf_op jit(solution)/shard_map/all_to_all | solution.py:45
  231.9 8.9 %reshape.134 = bf16[256,7168]{1,0:T(8,128)(2,1)} reshape(bf16[4,1,64,32,224]{4,3,2,0,1:T(8,128)(2,1)} %copy.73) | data formatting | bytes 7340032 | tf_op jit(solution)/shard_map/reshape | solution.py:48
  244.1 13.7 %psum.7 = bf16[128,128]{0,1:T(8,128)(2,1)S(1)} all-reduce(f32[128,128]{0,1:T(8,128)S(1)} %maximum_convert_fusion), channel_id=1, replica_groups=mesh['grp'=4,'chip'=16,'core'=2] {'grp'}, use_global_device_ids=true, to_apply=%region_4.5 | all-reduce | flops 16384 | bytes 98304 | tf_op jit(solution)/shard_map/psum | solution.py:64
  259.0 11.1 %all-to-all-start.2 = ((bf16[32,128,128]{1,2,0:T(8,128)(2,1)}), bf16[32,128,128]{1,2,0:T(8,128)(2,1)S(1)}, u32[]{:S(2)}, u32[]{:S(2)}) async-start(bf16[32,128,128]{1,2,0:T(8,128)(2,1)} %broadcast_in_dim.5), calls=%async_computation.2 | async-start | bytes 2097152 | tf_op jit(solution)/shard_map/all_to_all | solution.py:82
  272.9 12.4 %all-to-all-done.2 = bf16[32,128,128]{1,2,0:T(8,128)(2,1)S(1)} async-done(((bf16[32,128,128]{1,2,0:T(8,128)(2,1)}), bf16[32,128,128]{1,2,0:T(8,128)(2,1)S(1)}, u32[]{:S(2)}, u32[]{:S(2)}) %all-to-all-start.2) | async-done | bytes 1048608 | tf_op jit(solution)/shard_map/all_to_all | solution.py:82
  285.3 6.2 %all-to-all-start.4 = ((bf16[128,32,224]{0,2,1:T(8,128)(2,1)}), bf16[128,32,224]{0,2,1:T(8,128)(2,1)}, u32[]{:S(2)}, u32[]{:S(2)}) async-start(bf16[128,32,224]{0,2,1:T(8,128)(2,1)} %bitcast.27), calls=%async_computation.5 | async-start | bytes 3670016 | tf_op jit(solution)/shard_map/all_to_all | solution.py:35
  305.4 4.4 %collective-permute-start.2 = (bf16[128,1792]{1,0:T(8,128)(2,1)}, bf16[128,1792]{1,0:T(8,128)(2,1)}, u32[]{:S(2)}, u32[]{:S(2)}) collective-permute-start(bf16[128,1792]{1,0:T(8,128)(2,1)} %get-tuple-element.37), channel_id=1, source_target_pairs={{0,4},{1,5},{2,6},{3,7},{4,0},{5,1},{6,2},{7,3},{8,36},{9,37},{10,... | collective-permute-start | bytes 1376264 | tf_op jit(solution)/shard_map/ppermute | solution.py:130
  309.9 4.8 %collective-permute-start = (bf16[128,1792]{1,0:T(8,128)(2,1)}, bf16[128,1792]{1,0:T(8,128)(2,1)}, u32[]{:S(2)}, u32[]{:S(2)}) collective-permute-start(bf16[128,1792]{1,0:T(8,128)(2,1)} %get-tuple-element.39), channel_id=1, source_target_pairs={{0,0},{1,1},{2,2},{3,3},{4,4},{5,5},{6,6},{7,7},{8,32},{9,33},{10,... | collective-permute-start | bytes 1376264 | tf_op jit(solution)/shard_map/ppermute | solution.py:130
  314.6 78.2 %all-to-all-done.4 = bf16[128,32,224]{0,2,1:T(8,128)(2,1)} async-done(((bf16[128,32,224]{0,2,1:T(8,128)(2,1)}), bf16[128,32,224]{0,2,1:T(8,128)(2,1)}, u32[]{:S(2)}, u32[]{:S(2)}) %all-to-all-start.4) | async-done | bytes 1835040 | tf_op jit(solution)/shard_map/all_to_all | solution.py:35
  392.8 4.8 %multiply_convert_fusion = bf16[32,4,64,224]{3,2,1,0:T(8,128)(2,1)} fusion(f32[32,4]{1,0:T(8,128)S(1)} %copy.75, f32[32,128,64]{1,2,0:T(8,128)S(1)} %get-tuple-element.30, f32[32,128,4]{1,2,0:T(4,128)S(1)} %fusion.7, bf16[128,32,224]{0,2,1:T(8,128)(2,1)} %all-to-all-done.4), kind=kOutput, calls=%fused_computation.3 | convolution fusion | flops 475529216 | bytes 6619648 | tf_op jit(solution)/shard_map/stjr,stc->sjrc/dot_general | solution.py:95
  397.6 8.5 %reshape.144 = bf16[128,14336]{1,0:T(8,128)(2,1)} reshape(bf16[32,4,64,224]{3,2,1,0:T(8,128)(2,1)} %multiply_convert_fusion) | data formatting | bytes 7340032 | tf_op jit(solution)/shard_map/reshape | solution.py:102
  406.2 6.0 %copy.79 = bf16[14336,128]{1,0:T(8,128)(2,1)} copy(bf16[14336,128]{0,1:T(8,128)(2,1)} %bitcast.103) | data formatting | bytes 7340032 | tf_op jit(solution)/shard_map/dot_general | solution.py:100
  412.2 4.4 %fusion.9 = f32[64,64,224]{2,0,1:T(8,128)S(1)} fusion(bf16[64,224,128]{2,1,0:T(8,128)(2,1)} %bitcast.102, s32[128]{0:T(128)S(1)} %eq.69), kind=kOutput, calls=%fused_computation.40 | convolution fusion | flops 234905600 | bytes 7340544 | tf_op jit(solution)/shard_map/dot_general | solution.py:100
  416.6 4.5 %copy.80 = f32[64,64,224]{2,1,0:T(8,128)} copy(f32[64,64,224]{2,0,1:T(8,128)S(1)} %fusion.9) | data formatting | bytes 7340032
  (82 shorter events, 47.3 us)
Async XLA Ops:
  7.2 1.7 copy-start
  7.2 1.5 copy-start.9
  7.2 76.2 %all-gather.3.cloned.1.call-start = ((), (), s32[]{:S(2)}) async-start(), calls=%async_computation.6 | async-start | bytes 8912896 | tf_op jit(solution)/shard_map/all_gather | solution.py:42
  7.9 98.2 %all-gather.5.cloned.1.call-start = ((), (), s32[]{:S(2)}) async-start(), calls=%async_computation.7 | async-start | bytes 11010048 | tf_op jit(solution)/shard_map/all_gather | solution.py:63
  8.7 293.6 %reduce-scatter.2.cloned.1.call-start = ((), (), s32[]{:S(2)}) async-start(), calls=%async_computation.8 | async-start | bytes 9175040 | tf_op jit(solution)/shard_map/reduce_scatter | solution.py:68
  127.4 1.2 copy-start.6
  135.8 22.6 %all-to-all-start = ((bf16[32,2,8192]{2,1,0:T(2,128)(2,1)}), bf16[32,2,8192]{2,1,0:T(2,128)(2,1)S(1)}, u32[]{:S(2)}, u32[]{:S(2)}) async-start(bf16[32,2,8192]{2,1,0:T(2,128)(2,1)} %reshape.170), calls=%async_computation | async-start | bytes 2097152 | tf_op jit(solution)/shard_map/all_to_all | solution.py:46
  148.0 17.8 %copy-start.4 = (bf16[128,2048]{1,0:T(8,128)(2,1)S(1)}, bf16[128,2048]{1,0:T(8,128)(2,1)}, u32[]{:S(2)}) copy-start(bf16[128,2048]{1,0:T(8,128)(2,1)} %param.7) | copy-start | bytes 1572868
  148.0 18.8 %copy-start.10 = (s32[32,4]{0,1:T(4,128)S(1)}, s32[32,4]{0,1:T(4,128)}, u32[]{:S(2)}) copy-start(s32[32,4]{0,1:T(4,128)} %param.13) | copy-start | bytes 1540
  158.4 1.0 copy-start.5
  159.4 56.0 %all-to-all-start.1 = ((bf16[4,32,64,224]{3,2,0,1:T(8,128)(2,1)}), bf16[4,32,64,224]{3,2,0,1:T(8,128)(2,1)}, u32[]{:S(2)}, u32[]{:S(2)}) async-start(bf16[4,32,64,224]{3,2,0,1:T(8,128)(2,1)} %copy.72), calls=%async_computation.1 | async-start | bytes 8388608 | tf_op jit(solution)/shard_map/all_to_all | solution.py:45
  215.3 42.4 %all-to-all-start.3 = ((bf16[128,32,64]{0,2,1:T(8,128)(2,1)}), bf16[128,32,64]{0,2,1:T(8,128)(2,1)S(1)}, u32[]{:S(2)}, u32[]{:S(2)}) async-start(bf16[128,32,64]{0,2,1:T(8,128)(2,1)} %bitcast.18), calls=%async_computation.3 | async-start | bytes 1048576 | tf_op jit(solution)/shard_map/all_to_all | solution.py:38
  231.9 8.9 %copy-start.3 = (bf16[128,7168]{1,0:T(8,128)(2,1)S(1)}, bf16[128,7168]{1,0:T(8,128)(2,1)}, u32[]{:S(2)}) copy-start(bf16[128,7168]{1,0:T(8,128)(2,1)} %param.8) | copy-start | bytes 5505028
  257.8 1.2 copy-start.7
  259.0 26.3 %all-to-all-start.2 = ((bf16[32,128,128]{1,2,0:T(8,128)(2,1)}), bf16[32,128,128]{1,2,0:T(8,128)(2,1)S(1)}, u32[]{:S(2)}, u32[]{:S(2)}) async-start(bf16[32,128,128]{1,2,0:T(8,128)(2,1)} %broadcast_in_dim.5), calls=%async_computation.2 | async-start | bytes 2097152 | tf_op jit(solution)/shard_map/all_to_all | solution.py:82
  285.3 107.5 %all-to-all-start.4 = ((bf16[128,32,224]{0,2,1:T(8,128)(2,1)}), bf16[128,32,224]{0,2,1:T(8,128)(2,1)}, u32[]{:S(2)}, u32[]{:S(2)}) async-start(bf16[128,32,224]{0,2,1:T(8,128)(2,1)} %bitcast.27), calls=%async_computation.5 | async-start | bytes 3670016 | tf_op jit(solution)/shard_map/all_to_all | solution.py:35
  292.2 1.0 copy-start.8
  305.1 118.5 %collective-permute-start.3 = (bf16[128,1792]{1,0:T(8,128)(2,1)}, bf16[128,1792]{1,0:T(8,128)(2,1)}, u32[]{:S(2)}, u32[]{:S(2)}) collective-permute-start(bf16[128,1792]{1,0:T(8,128)(2,1)} %get-tuple-element.36), channel_id=1, source_target_pairs={{0,6},{1,7},{2,0},{3,1},{4,2},{5,3},{6,4},{7,5},{8,38},{9,39},{10,... | collective-permute-start | bytes 1376264 | tf_op jit(solution)/shard_map/ppermute | solution.py:130
  305.4 118.2 %collective-permute-start.2 = (bf16[128,1792]{1,0:T(8,128)(2,1)}, bf16[128,1792]{1,0:T(8,128)(2,1)}, u32[]{:S(2)}, u32[]{:S(2)}) collective-permute-start(bf16[128,1792]{1,0:T(8,128)(2,1)} %get-tuple-element.37), channel_id=1, source_target_pairs={{0,4},{1,5},{2,6},{3,7},{4,0},{5,1},{6,2},{7,3},{8,36},{9,37},{10,... | collective-permute-start | bytes 1376264 | tf_op jit(solution)/shard_map/ppermute | solution.py:130
  309.8 113.8 %collective-permute-start.1 = (bf16[128,1792]{1,0:T(8,128)(2,1)}, bf16[128,1792]{1,0:T(8,128)(2,1)}, u32[]{:S(2)}, u32[]{:S(2)}) collective-permute-start(bf16[128,1792]{1,0:T(8,128)(2,1)} %get-tuple-element.38), channel_id=1, source_target_pairs={{0,2},{1,3},{2,4},{3,5},{4,6},{5,7},{6,0},{7,1},{8,34},{9,35},{10,... | collective-permute-start | bytes 1376264 | tf_op jit(solution)/shard_map/ppermute | solution.py:130
  309.9 113.7 %collective-permute-start = (bf16[128,1792]{1,0:T(8,128)(2,1)}, bf16[128,1792]{1,0:T(8,128)(2,1)}, u32[]{:S(2)}, u32[]{:S(2)}) collective-permute-start(bf16[128,1792]{1,0:T(8,128)(2,1)} %get-tuple-element.39), channel_id=1, source_target_pairs={{0,0},{1,1},{2,2},{3,3},{4,4},{5,5},{6,6},{7,7},{8,32},{9,33},{10,... | collective-permute-start | bytes 1376264 | tf_op jit(solution)/shard_map/ppermute | solution.py:130
  421.0 4.2 copy-start.2
  425.3 2.4 copy-start.1
Sparse Core Ops, SparseCore 0:
  10.2 73.1 all-gather.2
  85.0 21.1 all-gather.4
  127.6 73.3 reduce-scatter.1
